TPU v7x, 512 devices: a whole 4x4x16 slice. The times are simulated.
512 devices in a mesh: blk: 64 (over x_hi, z, core), tgt: 8 (over y, x_lo).
Axes of the slice: x: 4 (x_hi: 2, x_lo: 2; x = x_hi * 2 + x_lo), y: 4, z: 16, core: 2. Of those that a mesh axis runs over, the one named last changes fastest.
Arguments:
- queries: bfloat16 [65536, 1024], P(('blk', 'tgt')), may hold values from -6 to 6
- keys: bfloat16 [4096, 1024], P('blk'), may hold values from -6 to 6
- values: bfloat16 [4096, 1024], P('blk'), may hold values from -6 to 6
- out_weight: bfloat16 [1024, 1024], P('tgt'), may hold values from -0.1875 to 0.1875
- out_grad: bfloat16 [65536, 1024], P(('blk', 'tgt')), may hold values from -24 to 24
Outputs:
- outputs: bfloat16 [65536, 1024], P(('blk', 'tgt'))
- query_grad: bfloat16 [65536, 1024], P(('blk', 'tgt'))
- key_grad: bfloat16 [4096, 1024], P('blk', 'tgt')
- value_grad: bfloat16 [4096, 1024], P('blk', 'tgt')
- weight_grad: bfloat16 [1024, 1024], P('tgt', 'blk')
All inputs are finite; a program needn't handle non-finite values.
Results may differ from a plain program's by a relative error of at most 0.017.
Values may be sent and summed in bfloat16 or wider, within the bound.
No kernel may reach another device: no remote copies, remote signals or barrier semaphores. Data moves between devices by JAX's collectives and lax.ppermute only.
A program may use at most 64 MiB of HBM per device.

v0:
```python
import jax
import jax.numpy as jnp
from jax import lax
from jax.sharding import PartitionSpec as P

D = 1024
HEADS = 16
HD = 64
WIN = 5
SRC_DEV = 64


def shifted(value, axis, steps):
    count = lax.axis_size(axis)
    pairs = [(source, (source + steps) % count) for source in range(count)]
    return lax.ppermute(value, axis, pairs)


def for_sending(value):
    return jax.tree.map(lambda a: a.astype(jnp.bfloat16) if a.dtype == jnp.float32 else a, value)


def head_block(query_cols, key_cols, value_cols, grad_cols, group_heads):
    scale = HD ** (-0.5)
    count = query_cols.shape[0]
    width = key_cols.shape[0]
    query_heads = query_cols.reshape(count, group_heads, HD)
    key_heads = key_cols.reshape(width, group_heads, HD)
    value_heads = value_cols.reshape(width, group_heads, HD)
    grad_heads = grad_cols.reshape(count, group_heads, HD)
    scores = (
        jnp.einsum("rhd,jhd->hrj", query_heads, key_heads, preferred_element_type=jnp.float32)
        * scale
    )
    top = jnp.max(scores, axis=-1, keepdims=True)
    expo = jnp.exp(scores - top)
    probs = expo / jnp.sum(expo, axis=-1, keepdims=True)
    probs_low = probs.astype(jnp.bfloat16)
    attended = jnp.einsum(
        "hrj,jhd->rhd", probs_low, value_heads, preferred_element_type=jnp.float32
    )
    attended = attended.reshape(count, group_heads * HD).astype(jnp.bfloat16)
    prob_grad = jnp.einsum(
        "rhd,jhd->hrj", grad_heads, value_heads, preferred_element_type=jnp.float32
    )
    center = jnp.sum(probs * prob_grad, axis=-1, keepdims=True)
    score_grad = (scale * probs * (prob_grad - center)).astype(jnp.bfloat16)
    query_grad = jnp.einsum(
        "hrj,jhd->rhd", score_grad, key_heads, preferred_element_type=jnp.float32
    )
    query_grad = query_grad.reshape(count, group_heads * HD).astype(jnp.bfloat16)
    key_part = jnp.einsum(
        "hrj,rhd->jhd", score_grad, query_heads, preferred_element_type=jnp.float32
    )
    value_part = jnp.einsum(
        "hrj,rhd->jhd", probs_low, grad_heads, preferred_element_type=jnp.float32
    )
    return (
        attended,
        query_grad,
        key_part.reshape(width, group_heads * HD),
        value_part.reshape(width, group_heads * HD),
    )


def local(queries, keys, values, out_weight, out_grad):
    full_weight = lax.all_gather(out_weight, "tgt", axis=0, tiled=True)
    current = (keys, values)
    key_list = [keys]
    value_list = [values]
    for step in range(1, WIN):
        current = shifted((current[0], current[1]), "blk", 1)
        key_list.append(current[0])
        value_list.append(current[1])
    seen_keys = jnp.concatenate(key_list, axis=0)
    seen_values = jnp.concatenate(value_list, axis=0)
    attended_grad = jnp.dot(out_grad, full_weight.T, preferred_element_type=jnp.float32).astype(
        jnp.bfloat16
    )
    group_heads = min(4, HEADS)
    span = group_heads * HD
    pieces = []
    for first in range(0, D, span):
        pieces.append(
            head_block(
                queries[:, first : first + span],
                seen_keys[:, first : first + span],
                seen_values[:, first : first + span],
                attended_grad[:, first : first + span],
                group_heads,
            )
        )
    attended = jnp.concatenate([p[0] for p in pieces], axis=1)
    query_grad = jnp.concatenate([p[1] for p in pieces], axis=1)
    key_part = jnp.concatenate([p[2] for p in pieces], axis=1)
    value_part = jnp.concatenate([p[3] for p in pieces], axis=1)
    outputs = jnp.dot(attended, full_weight, preferred_element_type=jnp.float32).astype(
        jnp.bfloat16
    )
    rows = SRC_DEV
    carried = (key_part[(WIN - 1) * rows : WIN * rows], value_part[(WIN - 1) * rows : WIN * rows])
    for step in range(WIN - 2, -1, -1):
        moved = shifted((for_sending(carried[0]), for_sending(carried[1])), "blk", -1)
        carried = (
            moved[0] + key_part[step * rows : (step + 1) * rows],
            moved[1] + value_part[step * rows : (step + 1) * rows],
        )
    key_total, value_total = carried
    key_grad, value_grad = (
        lax.psum_scatter(
            key_total.astype(jnp.bfloat16), "tgt", scatter_dimension=1, tiled=True
        ).astype(jnp.float32),
        lax.psum_scatter(
            value_total.astype(jnp.bfloat16), "tgt", scatter_dimension=1, tiled=True
        ).astype(jnp.float32),
    )
    tile_sum = lax.psum_scatter(
        jnp.einsum("rc,re->ce", attended, out_grad, preferred_element_type=jnp.float32).astype(
            jnp.bfloat16
        ),
        "tgt",
        scatter_dimension=0,
        tiled=True,
    ).astype(jnp.float32)
    weight_grad = lax.psum_scatter(tile_sum, "blk", scatter_dimension=1, tiled=True)
    return (
        outputs,
        query_grad,
        key_grad.astype(jnp.bfloat16),
        value_grad.astype(jnp.bfloat16),
        weight_grad.astype(jnp.bfloat16),
    )


def solution(mesh):
    return jax.shard_map(
        local,
        mesh=mesh,
        in_specs=(
            P(("blk", "tgt"), None),
            P("blk", None),
            P("blk", None),
            P("tgt", None),
            P(("blk", "tgt"), None),
        ),
        out_specs=(
            P(("blk", "tgt"), None),
            P(("blk", "tgt"), None),
            P("blk", "tgt"),
            P("blk", "tgt"),
            P("tgt", "blk"),
        ),
        check_vma=False,
    )
```

profile of v0, /device:TPU:8, one launch (start us, length us, event | category | flops | bytes accessed | tf_op | source)
XLA Modules:
  0.0 457.7 jit_solution(14117293037007560445)
XLA Ops:
  8.0 1.9 collective-permute-start.4
  9.9 3.9 collective-permute-start
  13.8 1.0 fusion.49
  14.8 0.9 constant_dynamic-update-slice_fusion.9
  15.7 0.9 constant_dynamic-update-slice_fusion.4
  17.1 7.0 %collective-permute-done.4 = bf16[64,1024]{1,0:T(8,128)(2,1)S(1)} collective-permute-done((bf16[64,1024]{1,0:T(8,128)(2,1)}, bf16[64,1024]{1,0:T(8,128)(2,1)S(1)}, u32[]{:S(2)}, u32[]{:S(2)}) %collective-permute-start.4) | collective-permute-done | bytes 131104 | tf_op jit(solution)/shard_map/ppermute | solution.py:16
  24.1 1.9 collective-permute-start.5
  26.1 1.9 collective-permute-start.1
  28.0 6.0 %collective-permute-done.5 = bf16[64,1024]{1,0:T(8,128)(2,1)S(1)} collective-permute-done((bf16[64,1024]{1,0:T(8,128)(2,1)S(1)}, bf16[64,1024]{1,0:T(8,128)(2,1)S(1)}, u32[]{:S(2)}, u32[]{:S(2)}) %collective-permute-start.5) | collective-permute-done | bytes 131104 | tf_op jit(solution)/shard_map/ppermute | solution.py:16
  34.0 1.9 collective-permute-start.6
  36.1 1.9 collective-permute-start.2
  38.0 6.0 %collective-permute-done.6 = bf16[64,1024]{1,0:T(8,128)(2,1)S(1)} collective-permute-done((bf16[64,1024]{1,0:T(8,128)(2,1)S(1)}, bf16[64,1024]{1,0:T(8,128)(2,1)S(1)}, u32[]{:S(2)}, u32[]{:S(2)}) %collective-permute-start.6) | collective-permute-done | bytes 131104 | tf_op jit(solution)/shard_map/ppermute | solution.py:16
  44.0 1.9 collective-permute-start.7
  46.0 1.9 collective-permute-start.3
  48.0 6.0 %collective-permute-done.7 = bf16[64,1024]{1,0:T(8,128)(2,1)S(1)} collective-permute-done((bf16[64,1024]{1,0:T(8,128)(2,1)S(1)}, bf16[64,1024]{1,0:T(8,128)(2,1)S(1)}, u32[]{:S(2)}, u32[]{:S(2)}) %collective-permute-start.7) | collective-permute-done | bytes 131104 | tf_op jit(solution)/shard_map/ppermute | solution.py:16
  54.8 1.3 collective-permute-done.3
  58.5 1.3 fusion.51
  61.4 1.3 fusion.53
  63.3 2.0 convolution_convert_fusion
  65.4 14.1 %all-gather.2.cloned.1.call-done = bf16[1024,1024]{1,0:T(8,128)(2,1)} async-done(((bf16[128,1024]{1,0:T(8,128)(2,1)}), bf16[1024,1024]{1,0:T(8,128)(2,1)}) %all-gather.2.cloned.1.call-update) | async-done | bytes 2097168 | tf_op jit(solution)/shard_map/all_gather | solution.py:67
  79.5 2.4 convolution_convert_fusion.1
  85.6 1.2 multiply_convert_fusion.2
  87.0 0.9 copy.93
  88.9 1.5 multiply_reduce_fusion.1
  91.4 0.9 copy.94
  92.9 0.9 copy.99
  97.9 2.1 collective-permute-start.12
  102.9 1.4 pad_maximum_fusion
  104.3 1.9 collective-permute-start.8
  106.2 0.9 fusion.19
  107.2 3.9 collective-permute-start.13
  111.2 5.1 %collective-permute-start.9 = (bf16[64,1024]{1,0:T(8,128)(2,1)S(1)}, bf16[64,1024]{1,0:T(8,128)(2,1)S(1)}, u32[]{:S(2)}, u32[]{:S(2)}) collective-permute-start(bf16[64,1024]{1,0:T(8,128)(2,1)S(1)} %fusion.23), channel_id=1, source_target_pairs={{0,504},{8,0},{16,8},{24,16},{32,24},{40,32},{48,40},{56,48},{64,5... | collective-permute-start | bytes 393224 | tf_op jit(solution)/shard_map/ppermute | solution.py:16
  116.3 4.8 %collective-permute-start.14 = (bf16[64,1024]{1,0:T(8,128)(2,1)S(1)}, bf16[64,1024]{1,0:T(8,128)(2,1)S(1)}, u32[]{:S(2)}, u32[]{:S(2)}) collective-permute-start(bf16[64,1024]{1,0:T(8,128)(2,1)S(1)} %fusion.18), channel_id=1, source_target_pairs={{0,504},{8,0},{16,8},{24,16},{32,24},{40,32},{48,40},{56,48},{64,5... | collective-permute-start | bytes 393224 | tf_op jit(solution)/shard_map/ppermute | solution.py:16
  121.2 5.1 %collective-permute-start.10 = (bf16[64,1024]{1,0:T(8,128)(2,1)S(1)}, bf16[64,1024]{1,0:T(8,128)(2,1)S(1)}, u32[]{:S(2)}, u32[]{:S(2)}) collective-permute-start(bf16[64,1024]{1,0:T(8,128)(2,1)S(1)} %fusion.22), channel_id=1, source_target_pairs={{0,504},{8,0},{16,8},{24,16},{32,24},{40,32},{48,40},{56,48},{64,5... | collective-permute-start | bytes 393224 | tf_op jit(solution)/shard_map/ppermute | solution.py:16
  126.3 4.8 %collective-permute-start.15 = (bf16[64,1024]{1,0:T(8,128)(2,1)S(1)}, bf16[64,1024]{1,0:T(8,128)(2,1)S(1)}, u32[]{:S(2)}, u32[]{:S(2)}) collective-permute-start(bf16[64,1024]{1,0:T(8,128)(2,1)S(1)} %fusion.17), channel_id=1, source_target_pairs={{0,504},{8,0},{16,8},{24,16},{32,24},{40,32},{48,40},{56,48},{64,5... | collective-permute-start | bytes 393224 | tf_op jit(solution)/shard_map/ppermute | solution.py:16
  131.9 5.1 %collective-permute-start.11 = (bf16[64,1024]{1,0:T(8,128)(2,1)}, bf16[64,1024]{1,0:T(8,128)(2,1)}, u32[]{:S(2)}, u32[]{:S(2)}) collective-permute-start(bf16[64,1024]{1,0:T(8,128)(2,1)} %fusion.21), channel_id=1, source_target_pairs={{0,504},{8,0},{16,8},{24,16},{32,24},{40,32},{48,40},{56,48},{64,5... | collective-permute-start | bytes 393224 | tf_op jit(solution)/shard_map/ppermute | solution.py:16
  137.7 1.8 copy.103
  139.8 0.9 fusion.20
  141.7 1.2 convolution_convert_fusion.5
  144.6 1.9 copy.105
  146.5 1.3 convolution_convert_fusion.3
  148.2 1.6 pad_maximum_fusion.3
  149.9 1.2 convolution_convert_fusion.2
  151.1 35.5 %reduce-scatter.15.cloned.1.call-done = bf16[128,64]{1,0:T(8,128)(2,1)} async-done(((bf16[1024,64]{1,0:T(8,128)(2,1)}), bf16[128,64]{1,0:T(8,128)(2,1)}) %reduce-scatter.15.cloned.1.call-update) | async-done | bytes 16400
  186.5 1.4 copy.104
  188.0 45.3 %reduce-scatter.13.cloned.1.call-done = bf16[128,64]{1,0:T(8,128)(2,1)} async-done(((bf16[1024,64]{1,0:T(8,128)(2,1)}), bf16[128,64]{1,0:T(8,128)(2,1)}) %reduce-scatter.13.cloned.1.call-update) | async-done | bytes 16400
  233.3 1.4 copy.102
  234.8 214.9 %reduce-scatter.17.cloned.1.call-done = f32[16,128]{1,0:T(8,128)} async-done(((f32[1024,128]{1,0:T(8,128)}), f32[16,128]{1,0:T(8,128)}) %reduce-scatter.17.cloned.1.call-update) | async-done | bytes 8208
  (174 shorter events, 26.5 us)
Async XLA Ops:
  7.2 56.1 %copy-start = (bf16[128,1024]{1,0:T(8,128)(2,1)S(1)}, bf16[128,1024]{1,0:T(8,128)(2,1)}, u32[]{:S(2)}) copy-start(bf16[128,1024]{1,0:T(8,128)(2,1)} %param.9) | copy-start | bytes 786436
  7.2 72.3 %all-gather.2.cloned.1.call-start = ((), (), s32[]{:S(2)}) async-start(), calls=%async_computation.4 | async-start | bytes 2359296 | tf_op jit(solution)/shard_map/all_gather | solution.py:67
  7.9 136.6 %reduce-scatter.11.cloned.1.call-start = ((), (), s32[]{:S(2)}) async-start(), calls=%async_computation.5 | async-start | bytes 2359296 | tf_op jit(solution)/shard_map/reduce_scatter | solution.py:117
  8.0 16.2 %collective-permute-start.4 = (bf16[64,1024]{1,0:T(8,128)(2,1)}, bf16[64,1024]{1,0:T(8,128)(2,1)S(1)}, u32[]{:S(2)}, u32[]{:S(2)}) collective-permute-start(bf16[64,1024]{1,0:T(8,128)(2,1)} %param.6), channel_id=1, source_target_pairs={{0,8},{8,16},{16,24},{24,32},{32,40},{40,48},{48,56},{56,64},{64,7... | collective-permute-start | bytes 393224 | tf_op jit(solution)/shard_map/ppermute | solution.py:16
  9.9 16.2 %collective-permute-start = (bf16[64,1024]{1,0:T(8,128)(2,1)}, bf16[64,1024]{1,0:T(8,128)(2,1)S(1)}, u32[]{:S(2)}, u32[]{:S(2)}) collective-permute-start(bf16[64,1024]{1,0:T(8,128)(2,1)} %param.7), channel_id=1, source_target_pairs={{0,8},{8,16},{16,24},{24,32},{32,40},{40,48},{48,56},{56,64},{64,7... | collective-permute-start | bytes 393224 | tf_op jit(solution)/shard_map/ppermute | solution.py:16
  16.7 79.4 %copy-start.24 = (bf16[128,256]{0,1:T(8,128)(2,1)}, bf16[128,256]{0,1:T(8,128)(2,1)S(1)}, u32[]{:S(2)}) copy-start(bf16[128,256]{0,1:T(8,128)(2,1)S(1)} %copy.74) | copy-start | bytes 196612
  17.1 42.6 %copy-start.26 = (bf16[128,256]{0,1:T(8,128)(2,1)}, bf16[128,256]{0,1:T(8,128)(2,1)S(1)}, u32[]{:S(2)}) copy-start(bf16[128,256]{0,1:T(8,128)(2,1)S(1)} %copy.80) | copy-start | bytes 196612
  24.1 9.9 %collective-permute-start.5 = (bf16[64,1024]{1,0:T(8,128)(2,1)S(1)}, bf16[64,1024]{1,0:T(8,128)(2,1)S(1)}, u32[]{:S(2)}, u32[]{:S(2)}) collective-permute-start(bf16[64,1024]{1,0:T(8,128)(2,1)S(1)} %collective-permute-done.4), channel_id=1, source_target_pairs={{0,8},{8,16},{16,24},{24,32},{32,40},{40,48},{48,56},{56,64},{64,7... | collective-permute-start | bytes 393224 | tf_op jit(solution)/shard_map/ppermute | solution.py:16
  26.1 10.0 %collective-permute-start.1 = (bf16[64,1024]{1,0:T(8,128)(2,1)S(1)}, bf16[64,1024]{1,0:T(8,128)(2,1)S(1)}, u32[]{:S(2)}, u32[]{:S(2)}) collective-permute-start(bf16[64,1024]{1,0:T(8,128)(2,1)S(1)} %collective-permute-done), channel_id=1, source_target_pairs={{0,8},{8,16},{16,24},{24,32},{32,40},{40,48},{48,56},{56,64},{64,7... | collective-permute-start | bytes 393224 | tf_op jit(solution)/shard_map/ppermute | solution.py:16
  34.0 10.0 %collective-permute-start.6 = (bf16[64,1024]{1,0:T(8,128)(2,1)S(1)}, bf16[64,1024]{1,0:T(8,128)(2,1)S(1)}, u32[]{:S(2)}, u32[]{:S(2)}) collective-permute-start(bf16[64,1024]{1,0:T(8,128)(2,1)S(1)} %collective-permute-done.5), channel_id=1, source_target_pairs={{0,8},{8,16},{16,24},{24,32},{32,40},{40,48},{48,56},{56,64},{64,7... | collective-permute-start | bytes 393224 | tf_op jit(solution)/shard_map/ppermute | solution.py:16
  36.1 10.0 %collective-permute-start.2 = (bf16[64,1024]{1,0:T(8,128)(2,1)S(1)}, bf16[64,1024]{1,0:T(8,128)(2,1)S(1)}, u32[]{:S(2)}, u32[]{:S(2)}) collective-permute-start(bf16[64,1024]{1,0:T(8,128)(2,1)S(1)} %collective-permute-done.1), channel_id=1, source_target_pairs={{0,8},{8,16},{16,24},{24,32},{32,40},{40,48},{48,56},{56,64},{64,7... | collective-permute-start | bytes 393224 | tf_op jit(solution)/shard_map/ppermute | solution.py:16
  44.0 10.0 %collective-permute-start.7 = (bf16[64,1024]{1,0:T(8,128)(2,1)S(1)}, bf16[64,1024]{1,0:T(8,128)(2,1)S(1)}, u32[]{:S(2)}, u32[]{:S(2)}) collective-permute-start(bf16[64,1024]{1,0:T(8,128)(2,1)S(1)} %collective-permute-done.6), channel_id=1, source_target_pairs={{0,8},{8,16},{16,24},{24,32},{32,40},{40,48},{48,56},{56,64},{64,7... | collective-permute-start | bytes 393224 | tf_op jit(solution)/shard_map/ppermute | solution.py:16
  46.0 10.0 %collective-permute-start.3 = (bf16[64,1024]{1,0:T(8,128)(2,1)S(1)}, bf16[64,1024]{1,0:T(8,128)(2,1)S(1)}, u32[]{:S(2)}, u32[]{:S(2)}) collective-permute-start(bf16[64,1024]{1,0:T(8,128)(2,1)S(1)} %collective-permute-done.2), channel_id=1, source_target_pairs={{0,8},{8,16},{16,24},{24,32},{32,40},{40,48},{48,56},{56,64},{64,7... | collective-permute-start | bytes 393224 | tf_op jit(solution)/shard_map/ppermute | solution.py:16
  54.2 41.9 %copy-start.7 = (bf16[320,256]{0,1:T(8,128)(2,1)}, bf16[320,256]{0,1:T(8,128)(2,1)S(1)}, u32[]{:S(2)}) copy-start(bf16[320,256]{0,1:T(8,128)(2,1)S(1)} %copy.73) | copy-start | bytes 491524
  54.4 37.9 %copy-start.9 = (bf16[320,256]{0,1:T(8,128)(2,1)}, bf16[320,256]{0,1:T(8,128)(2,1)S(1)}, u32[]{:S(2)}) copy-start(bf16[320,256]{0,1:T(8,128)(2,1)S(1)} %copy.82) | copy-start | bytes 491524
  54.6 33.4 %copy-start.10 = (bf16[320,256]{0,1:T(8,128)(2,1)}, bf16[320,256]{0,1:T(8,128)(2,1)S(1)}, u32[]{:S(2)}) copy-start(bf16[320,256]{0,1:T(8,128)(2,1)S(1)} %copy.79) | copy-start | bytes 491524
  54.8 29.5 %copy-start.12 = (bf16[320,256]{0,1:T(8,128)(2,1)}, bf16[320,256]{0,1:T(8,128)(2,1)S(1)}, u32[]{:S(2)}) copy-start(bf16[320,256]{0,1:T(8,128)(2,1)S(1)} %copy.76) | copy-start | bytes 491524
  56.3 6.4 %copy-start.29 = (bf16[320,256]{0,1:T(8,128)(2,1)}, bf16[320,256]{0,1:T(8,128)(2,1)S(1)}, u32[]{:S(2)}) copy-start(bf16[320,256]{0,1:T(8,128)(2,1)S(1)} %copy.72) | copy-start | bytes 491524
  57.3 2.5 copy-start.33
  57.9 27.2 %copy-start.15 = (f32[4,128,320]{1,2,0:T(8,128)}, f32[4,128,320]{1,2,0:T(8,128)S(1)}, u32[]{:S(2)}) copy-start(f32[4,128,320]{1,2,0:T(8,128)S(1)} %get-tuple-element.41) | copy-start | bytes 1966084
  58.5 4.8 %copy-start.16 = (bf16[4,64,128]{2,1,0:T(8,128)(2,1)}, bf16[4,64,128]{2,1,0:T(8,128)(2,1)S(1)}, u32[]{:S(2)}) copy-start(bf16[4,64,128]{2,1,0:T(8,128)(2,1)S(1)} %convolution_convert_fusion.9) | copy-start | bytes 196612
  60.3 2.9 copy-start.18
  63.2 2.1 copy-start.22
  65.3 121.2 %reduce-scatter.15.cloned.1.call-start = ((), (), s32[]{:S(2)}) async-start(), calls=%async_computation.7 | async-start | bytes 294912
  85.5 2.4 copy-start.27
  85.6 2.4 copy-start.40
  97.1 3.0 copy-start.13
  97.1 3.0 copy-start.30
  97.1 3.0 copy-start.38
  97.9 8.3 %collective-permute-start.12 = (bf16[64,1024]{1,0:T(8,128)(2,1)}, bf16[64,1024]{1,0:T(8,128)(2,1)}, u32[]{:S(2)}, u32[]{:S(2)}) collective-permute-start(bf16[64,1024]{1,0:T(8,128)(2,1)} %slice.154), channel_id=1, source_target_pairs={{0,504},{8,0},{16,8},{24,16},{32,24},{40,32},{48,40},{56,48},{64,5... | collective-permute-start | bytes 393224 | tf_op jit(solution)/shard_map/ppermute | solution.py:16
  104.3 6.8 %collective-permute-start.8 = (bf16[64,1024]{1,0:T(8,128)(2,1)S(1)}, bf16[64,1024]{1,0:T(8,128)(2,1)S(1)}, u32[]{:S(2)}, u32[]{:S(2)}) collective-permute-start(bf16[64,1024]{1,0:T(8,128)(2,1)S(1)} %slice.155), channel_id=1, source_target_pairs={{0,504},{8,0},{16,8},{24,16},{32,24},{40,32},{48,40},{56,48},{64,5... | collective-permute-start | bytes 393224 | tf_op jit(solution)/shard_map/ppermute | solution.py:16
  107.2 9.1 %collective-permute-start.13 = (bf16[64,1024]{1,0:T(8,128)(2,1)S(1)}, bf16[64,1024]{1,0:T(8,128)(2,1)S(1)}, u32[]{:S(2)}, u32[]{:S(2)}) collective-permute-start(bf16[64,1024]{1,0:T(8,128)(2,1)S(1)} %fusion.19), channel_id=1, source_target_pairs={{0,504},{8,0},{16,8},{24,16},{32,24},{40,32},{48,40},{56,48},{64,5... | collective-permute-start | bytes 393224 | tf_op jit(solution)/shard_map/ppermute | solution.py:16
  111.2 10.0 %collective-permute-start.9 = (bf16[64,1024]{1,0:T(8,128)(2,1)S(1)}, bf16[64,1024]{1,0:T(8,128)(2,1)S(1)}, u32[]{:S(2)}, u32[]{:S(2)}) collective-permute-start(bf16[64,1024]{1,0:T(8,128)(2,1)S(1)} %fusion.23), channel_id=1, source_target_pairs={{0,504},{8,0},{16,8},{24,16},{32,24},{40,32},{48,40},{56,48},{64,5... | collective-permute-start | bytes 393224 | tf_op jit(solution)/shard_map/ppermute | solution.py:16
  116.3 10.0 %collective-permute-start.14 = (bf16[64,1024]{1,0:T(8,128)(2,1)S(1)}, bf16[64,1024]{1,0:T(8,128)(2,1)S(1)}, u32[]{:S(2)}, u32[]{:S(2)}) collective-permute-start(bf16[64,1024]{1,0:T(8,128)(2,1)S(1)} %fusion.18), channel_id=1, source_target_pairs={{0,504},{8,0},{16,8},{24,16},{32,24},{40,32},{48,40},{56,48},{64,5... | collective-permute-start | bytes 393224 | tf_op jit(solution)/shard_map/ppermute | solution.py:16
  121.2 10.0 %collective-permute-start.10 = (bf16[64,1024]{1,0:T(8,128)(2,1)S(1)}, bf16[64,1024]{1,0:T(8,128)(2,1)S(1)}, u32[]{:S(2)}, u32[]{:S(2)}) collective-permute-start(bf16[64,1024]{1,0:T(8,128)(2,1)S(1)} %fusion.22), channel_id=1, source_target_pairs={{0,504},{8,0},{16,8},{24,16},{32,24},{40,32},{48,40},{56,48},{64,5... | collective-permute-start | bytes 393224 | tf_op jit(solution)/shard_map/ppermute | solution.py:16
  126.3 10.6 %collective-permute-start.15 = (bf16[64,1024]{1,0:T(8,128)(2,1)S(1)}, bf16[64,1024]{1,0:T(8,128)(2,1)S(1)}, u32[]{:S(2)}, u32[]{:S(2)}) collective-permute-start(bf16[64,1024]{1,0:T(8,128)(2,1)S(1)} %fusion.17), channel_id=1, source_target_pairs={{0,504},{8,0},{16,8},{24,16},{32,24},{40,32},{48,40},{56,48},{64,5... | collective-permute-start | bytes 393224 | tf_op jit(solution)/shard_map/ppermute | solution.py:16
  131.9 7.9 %collective-permute-start.11 = (bf16[64,1024]{1,0:T(8,128)(2,1)}, bf16[64,1024]{1,0:T(8,128)(2,1)}, u32[]{:S(2)}, u32[]{:S(2)}) collective-permute-start(bf16[64,1024]{1,0:T(8,128)(2,1)} %fusion.21), channel_id=1, source_target_pairs={{0,504},{8,0},{16,8},{24,16},{32,24},{40,32},{48,40},{56,48},{64,5... | collective-permute-start | bytes 393224 | tf_op jit(solution)/shard_map/ppermute | solution.py:16
  137.7 5.9 %copy-start.11 = (bf16[320,256]{0,1:T(8,128)(2,1)S(1)}, bf16[320,256]{0,1:T(8,128)(2,1)}, u32[]{:S(2)}) copy-start(bf16[320,256]{0,1:T(8,128)(2,1)} %copy-done.10) | copy-start | bytes 491524
  139.5 93.8 %reduce-scatter.13.cloned.1.call-start = ((), (), s32[]{:S(2)}) async-start(), calls=%async_computation.6 | async-start | bytes 294912
  141.6 4.9 %copy-start.3 = (bf16[4,128,320]{1,2,0:T(8,128)(2,1)S(1)}, bf16[4,128,320]{1,2,0:T(8,128)(2,1)}, u32[]{:S(2)}) copy-start(bf16[4,128,320]{1,2,0:T(8,128)(2,1)} %copy-done.2) | copy-start | bytes 983044
  141.6 308.0 %reduce-scatter.17.cloned.1.call-start = ((), (), s32[]{:S(2)}) async-start(), calls=%async_computation.8 | async-start | bytes 532480
  143.6 4.3 copy-start.5
  143.6 4.3 copy-start.8
  146.5 3.4 copy-start.1
  146.5 3.4 copy-start.17
  146.5 3.4 copy-start.19
  146.5 3.4 copy-start.21
  146.5 3.4 copy-start.23
  (14 other events, 16.8 us)
Sparse Core Ops, SparseCore 0:
  10.1 69.3 all-gather.1
  82.3 52.4 reduce-scatter.10
  139.7 46.8 reduce-scatter.14
  189.2 44.0 reduce-scatter.12
  237.7 211.8 reduce-scatter.16
where the time goes:
time: 459 us; the launch traced here: 458 us
  waiting for transfers between devices  337 us (73%)
  starting transfers between devices  50.4 us (11%)
  local copies, waits for them, and re-layouts  27.3 us (6%)
  matrix products  19.8 us (4%)
  between operations  14.7 us (3%)
  other arithmetic  8.21 us (2%)
    unnamed x8, waiting for transfers between devices  296 us
    ppermute x16, starting transfers between devices, shifted(): return lax.ppermute(value, axis, pairs)  50.2 us
    ppermute x16, waiting for transfers between devices, shifted(): return lax.ppermute(value, axis, pairs)  26.7 us
    unnamed x97, local copies, waits for them, and re-layouts  14.1 us
    all_gather x1, waiting for transfers between devices, local(): full_weight = lax.all_gather(out_weight, 'tgt', axis=0, tiled=True)  14.1 us
  transfers between devices with their start and end apart: 21, of which 12 were waited for; matrix products, arithmetic and copies ran while one was open for 11% of the time, Pallas kernels for 0%

commit v1 on v0

v1 whole, which is shorter than its diff:
```python
import jax
import jax.numpy as jnp
from jax import lax
from jax.experimental import pallas as pl
from jax.experimental.pallas import tpu as pltpu
from jax.sharding import PartitionSpec as P

HD = 64
PAIR = 2 * HD
WIN = 5
SRC_DEV = 64
TILE = 256
F32 = jnp.float32
BF16 = jnp.bfloat16
NT = (((1,), (1,)), ((), ()))


def dot(a, b):
    return jnp.dot(a, b, preferred_element_type=F32)


def dot_nt(a, b):
    return lax.dot_general(a, b, NT, preferred_element_type=F32)


def attend_kernel(
    x_ref, own_ref, kv1_ref, kv2_ref, kv3_ref, kv4_ref, w_ref,
    back_ref, tile_ref, kv_own_ref, kv_send_ref,
    key_ref, value_ref, key_t_ref, value_t_ref, key_acc, value_acc, tile_acc,
):
    depth = w_ref.shape[1]
    width = WIN * SRC_DEV
    n_src, rows_src, _ = x_ref.shape
    lane = lax.broadcasted_iota(jnp.int32, (SRC_DEV, PAIR), 1)
    zero = jnp.zeros((SRC_DEV, PAIR), BF16)
    for w, ref in enumerate((own_ref, kv1_ref, kv2_ref, kv3_ref, kv4_ref)):
        block_key = ref[:, :PAIR]
        block_value = ref[:, PAIR:]
        for head in range(2):
            mine = (lane < HD) if head == 0 else (lane >= HD)
            at = pl.ds(head * width + w * SRC_DEV, SRC_DEV)
            key_ref[at, :] = jnp.where(mine, block_key, zero)
            value_ref[at, :] = jnp.where(mine, block_value, zero)
    key_t_ref[...] = key_ref[...].T
    value_t_ref[...] = value_ref[...].T
    scale = HD ** -0.5
    per_tile = TILE // rows_src
    steps = n_src // per_tile
    for step in range(steps):
        src = pl.ds(step * per_tile, per_tile)
        out_grad = x_ref[src, :, :depth].reshape(TILE, depth)
        query = x_ref[src, :, depth:].reshape(TILE, PAIR)
        att_grad = dot_nt(out_grad, w_ref[...]).astype(BF16)
        scores = dot_nt(key_ref[...], query)
        prob_grad = dot_nt(value_ref[...], att_grad)
        probs_low = []
        score_grad = []
        for head in range(2):
            part = scores[head * width : (head + 1) * width]
            grad = prob_grad[head * width : (head + 1) * width]
            top = jnp.max(part, axis=0, keepdims=True)
            expo = jnp.exp((part - top) * scale)
            probs = expo * (1.0 / jnp.sum(expo, axis=0, keepdims=True))
            center = jnp.sum(probs * grad, axis=0, keepdims=True)
            probs_low.append(probs.astype(BF16))
            score_grad.append((scale * probs * (grad - center)).astype(BF16))
        probs_low = jnp.concatenate(probs_low, axis=0)
        score_grad = jnp.concatenate(score_grad, axis=0)
        attended_t = dot(value_t_ref[...], probs_low)
        query_grad_t = dot(key_t_ref[...], score_grad)
        back_ref[src, :, :PAIR] = attended_t.T.astype(BF16).reshape(per_tile, rows_src, PAIR)
        back_ref[src, :, PAIR:] = query_grad_t.T.astype(BF16).reshape(per_tile, rows_src, PAIR)
        key_part = dot(score_grad, query)
        value_part = dot(probs_low, att_grad)
        tile_part = dot(attended_t.astype(BF16), out_grad)
        if step == 0:
            key_acc[...] = key_part
            value_acc[...] = value_part
            tile_acc[...] = tile_part
        else:
            key_acc[...] += key_part
            value_acc[...] += value_part
            tile_acc[...] += tile_part
    for w in range(WIN):
        for at, acc in ((0, key_acc), (PAIR, value_acc)):
            first = acc[w * SRC_DEV : (w + 1) * SRC_DEV]
            second = acc[width + w * SRC_DEV : width + (w + 1) * SRC_DEV]
            grad = jnp.where(lane < HD, first, second)
            if w == 0:
                kv_own_ref[:, at : at + PAIR] = grad
            else:
                kv_send_ref[w - 1, :, at : at + PAIR] = grad.astype(BF16)
    tile_ref[...] = tile_acc[...].T.astype(BF16)


def attend(x, kvs, weight):
    n_src, rows_src, wide = x.shape
    depth = weight.shape[1]
    width = WIN * SRC_DEV
    vmem = pl.BlockSpec(memory_space=pltpu.VMEM)
    flops = 2 * n_src * rows_src * (6 * 2 * width * PAIR + 2 * depth * PAIR)
    return pl.pallas_call(
        attend_kernel,
        out_shape=(
            jax.ShapeDtypeStruct((n_src, rows_src, 2 * PAIR), BF16),
            jax.ShapeDtypeStruct((depth, PAIR), BF16),
            jax.ShapeDtypeStruct((SRC_DEV, 2 * PAIR), F32),
            jax.ShapeDtypeStruct((WIN - 1, SRC_DEV, 2 * PAIR), BF16),
        ),
        in_specs=[vmem] * 7,
        out_specs=(vmem,) * 4,
        scratch_shapes=[
            pltpu.VMEM((2 * width, PAIR), BF16),
            pltpu.VMEM((2 * width, PAIR), BF16),
            pltpu.VMEM((PAIR, 2 * width), BF16),
            pltpu.VMEM((PAIR, 2 * width), BF16),
            pltpu.VMEM((2 * width, PAIR), F32),
            pltpu.VMEM((2 * width, PAIR), F32),
            pltpu.VMEM((PAIR, depth), F32),
        ],
        cost_estimate=pl.CostEstimate(
            flops=flops, bytes_accessed=2 * n_src * rows_src * wide, transcendentals=2 * width * n_src * rows_src
        ),
        compiler_params=pltpu.CompilerParams(vmem_limit_bytes=40 * 1024 * 1024),
        name="attend",
    )(x, *kvs, weight)


def project_kernel(odd_ref, back_ref, mine_ref, theirs_ref, out_ref, query_grad_ref):
    n_src, rows_src, _ = back_ref.shape
    depth = mine_ref.shape[2]
    odd = odd_ref[0] == 1
    total = jnp.zeros((rows_src, depth), F32)
    for src in range(0, n_src, 2):
        attended, weight = [], []
        for at in (src, src + 1):
            query_grad_ref[:, at * PAIR : (at + 1) * PAIR] = back_ref[at, :, PAIR:]
            part = back_ref[at, :, :PAIR].astype(F32)
            attended.append(jnp.where(odd, pltpu.roll(part, HD, 1), part).astype(BF16))
            weight += [mine_ref[at], theirs_ref[at]]
        total = total + dot(jnp.concatenate(attended, axis=1), jnp.concatenate(weight, axis=0))
    out_ref[...] = total.astype(BF16)


def project(odd, back, mine, theirs):
    n_src, rows_src, _ = back.shape
    depth = mine.shape[2]
    vmem = pl.BlockSpec(memory_space=pltpu.VMEM)
    out = jax.ShapeDtypeStruct((rows_src, depth), BF16)
    return pl.pallas_call(
        project_kernel,
        out_shape=(out, out),
        in_specs=[pl.BlockSpec(memory_space=pltpu.SMEM)] + [vmem] * 3,
        out_specs=(vmem, vmem),
        cost_estimate=pl.CostEstimate(
            flops=2 * rows_src * depth * depth, bytes_accessed=2 * depth * depth, transcendentals=0
        ),
        name="project",
    )(odd, back, mine, theirs)


def shift(value, axis, steps):
    count = lax.axis_size(axis)
    return lax.ppermute(value, axis, [(i, (i + steps) % count) for i in range(count)])


def partner(value, axis):
    return lax.ppermute(value, axis, [(i, i ^ 1) for i in range(lax.axis_size(axis))])


def swap(value, axis):
    return lax.all_to_all(value, axis, split_axis=0, concat_axis=0, tiled=True)


def local(queries, keys, values, out_weight, out_grad):
    n_tgt = lax.axis_size("tgt")
    n_blk = lax.axis_size("blk")
    rows, depth = queries.shape
    tgt = lax.axis_index("tgt")
    odd = lax.axis_index("blk") % 2
    own = jnp.concatenate(
        [lax.dynamic_slice_in_dim(a, tgt * PAIR, PAIR, 1) for a in (keys, values)], axis=1
    )
    kvs = [own] + [shift(own, "blk", w) for w in range(1, WIN)]
    wide = jnp.broadcast_to(out_grad[None], (n_tgt, rows, depth))
    split = queries.reshape(rows, n_tgt, PAIR).transpose(1, 0, 2)
    x = swap(jnp.concatenate([wide, split], axis=2), "tgt")
    half_rows = out_weight.shape[0] // 2
    half = lax.dynamic_slice_in_dim(out_weight, odd * half_rows, half_rows, 0)
    mine = swap(jnp.broadcast_to(half[None], (n_tgt, half_rows, depth)), "tgt")
    theirs = partner(mine, "blk")
    back, tile, kv_own, kv_send = attend(x, kvs, out_weight)
    back = swap(back, "tgt")
    tiles = swap(tile.reshape(n_blk, depth // n_blk, PAIR), "blk")
    weight_grad = jnp.sum(tiles.astype(F32), axis=0).T.astype(BF16)
    kv_grad = kv_own
    for w in range(1, WIN):
        kv_grad = kv_grad + shift(kv_send[w - 1], "blk", -w).astype(F32)
    kv_grad = kv_grad.astype(BF16)
    outputs, query_grad = project(odd.reshape(1), back, mine, theirs)
    return outputs, query_grad, kv_grad[:, :PAIR], kv_grad[:, PAIR:], weight_grad


def solution(mesh):
    return jax.shard_map(
        local,
        mesh=mesh,
        in_specs=(
            P(("blk", "tgt"), None),
            P("blk", None),
            P("blk", None),
            P("tgt", None),
            P(("blk", "tgt"), None),
        ),
        out_specs=(
            P(("blk", "tgt"), None),
            P(("blk", "tgt"), None),
            P("blk", "tgt"),
            P("blk", "tgt"),
            P("tgt", "blk"),
        ),
        check_vma=False,
    )
```

time: 459 us -> 128 us (0.28)
  the two profiles are of different devices: /device:TPU:8 before, /device:TPU:1 now
where the time goes in v1:
time: 128 us; the launch traced here: 127 us
  starting transfers between devices  73.4 us (57%)
  waiting for transfers between devices  36.6 us (29%)
  Pallas kernels  7.85 us (6%)
  local copies, waits for them, and re-layouts  5.96 us (5%)
  other arithmetic  2.4 us (2%)
    ppermute x8, starting transfers between devices, shift(): lax.ppermute(value, axis, [(i, (i + steps) % count) for i in range(count)])  39.5 us
    all_to_all x4, waiting for transfers between devices, swap(): return lax.all_to_all(value, axis, split_axis=0, concat_axis=0, tiled=True)  30.4 us
    all_to_all x4, starting transfers between devices, swap(): return lax.all_to_all(value, axis, split_axis=0, concat_axis=0, tiled=True)  30.3 us
    ppermute x8, waiting for transfers between devices, shift(): lax.ppermute(value, axis, [(i, (i + steps) % count) for i in range(count)])  6.21 us
    pallas_call x1, Pallas kernels, attend(): pl.pallas_call(attend_kernel, out_shape=(jax.ShapeDtypeStruct((n_src, row...  4.95 us
    ppermute x1, starting transfers between devices, partner(): lax.ppermute(value, axis, [(i, i ^ 1) for i in range(lax.axis_size(axis))])  3.54 us
    pallas_call x1, Pallas kernels, project(): pl.pallas_call(project_kernel, out_shape=(out, out), in_specs=[pl.BlockSp...  2.9 us
  transfers between devices with their start and end apart: 13, of which 5 were waited for; matrix products, arithmetic and copies ran while one was open for 1% of the time, Pallas kernels for 6%

profile of v1, /device:TPU:1, one launch (start us, length us, event | category | flops | bytes accessed | tf_op | source)
XLA Modules:
  0.0 127.1 jit_solution(11570758216792238016)
XLA Ops:
  0.6 1.1 copy.10
  1.8 0.2 copy.11
  1.9 1.2 broadcast_in_dim.4
  3.2 1.7 %pad_maximum_fusion = bf16[8,128,1152]{2,1,0:T(8,128)(2,1)} fusion(bf16[8,128,128]{2,1,0:T(8,128)(2,1)S(1)} %bitcast.13, bf16[8,128,1024]{2,1,0:T(8,128)(2,1)S(1)} %broadcast_in_dim.4), kind=kLoop, calls=%fused_computation | loop fusion | flops 4718592 | bytes 4718592 | tf_op jit(solution)/shard_map/concatenate | solution.py:187
  4.9 0.0 copy-start
  4.9 6.1 %all-to-all-start = ((bf16[8,128,1152]{2,1,0:T(8,128)(2,1)}), bf16[8,128,1152]{2,1,0:T(8,128)(2,1)S(1)}, u32[]{:S(2)}, u32[]{:S(2)}) async-start(bf16[8,128,1152]{2,1,0:T(8,128)(2,1)} %pad_maximum_fusion), calls=%async_computation | async-start | bytes 4718592 | tf_op jit(solution)/shard_map/all_to_all | solution.py:172
  10.9 0.0 copy-done
  11.0 25.4 %all-to-all-done.x_ref = bf16[8,128,1152]{2,1,0:T(8,128)(2,1)S(1)} async-done(((bf16[8,128,1152]{2,1,0:T(8,128)(2,1)}), bf16[8,128,1152]{2,1,0:T(8,128)(2,1)S(1)}, u32[]{:S(2)}, u32[]{:S(2)}) %all-to-all-start) | async-done | bytes 2359328 | tf_op jit(solution)/shard_map/all_to_all | solution.py:172
  36.4 1.1 broadcast_in_dim.5
  37.5 5.6 %all-to-all-start.2 = ((bf16[8,64,1024]{2,1,0:T(8,128)(2,1)}), bf16[8,64,1024]{2,1,0:T(8,128)(2,1)}, u32[]{:S(2)}, u32[]{:S(2)}) async-start(bf16[8,64,1024]{2,1,0:T(8,128)(2,1)} %broadcast_in_dim.5), calls=%async_computation.2 | async-start | bytes 2097152 | tf_op jit(solution)/shard_map/all_to_all | solution.py:172
  43.1 0.7 constant_dynamic-slice_fusion.1
  43.8 7.4 %collective-permute-start = (bf16[64,256]{1,0:T(8,128)(2,1)S(1)}, bf16[64,256]{1,0:T(8,128)(2,1)S(1)}, u32[]{:S(2)}, u32[]{:S(2)}) collective-permute-start(bf16[64,256]{1,0:T(8,128)(2,1)S(1)} %pad_maximum_fusion.1.own_ref), channel_id=1, source_target_pairs={{0,8},{8,16},{16,24},{24,32},{32,40},{40,48},{48,56},{56,64},{64,7... | collective-permute-start | bytes 98312 | tf_op jit(solution)/shard_map/ppermute | solution.py:164
  51.2 3.5 %collective-permute-start.1 = (bf16[64,256]{1,0:T(8,128)(2,1)S(1)}, bf16[64,256]{1,0:T(8,128)(2,1)S(1)}, u32[]{:S(2)}, u32[]{:S(2)}) collective-permute-start(bf16[64,256]{1,0:T(8,128)(2,1)S(1)} %pad_maximum_fusion.1.own_ref), channel_id=1, source_target_pairs={{0,16},{8,24},{16,32},{24,40},{32,48},{40,56},{48,64},{56,72},{64,... | collective-permute-start | bytes 98312 | tf_op jit(solution)/shard_map/ppermute | solution.py:164
  54.8 3.6 %collective-permute-start.2 = (bf16[64,256]{1,0:T(8,128)(2,1)S(1)}, bf16[64,256]{1,0:T(8,128)(2,1)S(1)}, u32[]{:S(2)}, u32[]{:S(2)}) collective-permute-start(bf16[64,256]{1,0:T(8,128)(2,1)S(1)} %pad_maximum_fusion.1.own_ref), channel_id=1, source_target_pairs={{0,24},{8,32},{16,40},{24,48},{32,56},{40,64},{48,72},{56,80},{64,... | collective-permute-start | bytes 98312 | tf_op jit(solution)/shard_map/ppermute | solution.py:164
  58.3 6.1 %collective-permute-start.3 = (bf16[64,256]{1,0:T(8,128)(2,1)S(1)}, bf16[64,256]{1,0:T(8,128)(2,1)S(1)}, u32[]{:S(2)}, u32[]{:S(2)}) collective-permute-start(bf16[64,256]{1,0:T(8,128)(2,1)S(1)} %pad_maximum_fusion.1.own_ref), channel_id=1, source_target_pairs={{0,32},{8,40},{16,48},{24,56},{32,64},{40,72},{48,80},{56,88},{64,... | collective-permute-start | bytes 98312 | tf_op jit(solution)/shard_map/ppermute | solution.py:164
  64.5 0.0 collective-permute-done.kv1_ref
  64.5 0.0 collective-permute-done.1.kv2_ref
  64.5 1.9 %collective-permute-done.2.kv3_ref = bf16[64,256]{1,0:T(8,128)(2,1)S(1)} collective-permute-done((bf16[64,256]{1,0:T(8,128)(2,1)S(1)}, bf16[64,256]{1,0:T(8,128)(2,1)S(1)}, u32[]{:S(2)}, u32[]{:S(2)}) %collective-permute-start.2) | collective-permute-done | bytes 32800 | tf_op jit(solution)/shard_map/ppermute | solution.py:164
  66.4 2.9 %collective-permute-done.3.kv4_ref = bf16[64,256]{1,0:T(8,128)(2,1)S(1)} collective-permute-done((bf16[64,256]{1,0:T(8,128)(2,1)S(1)}, bf16[64,256]{1,0:T(8,128)(2,1)S(1)}, u32[]{:S(2)}, u32[]{:S(2)}) %collective-permute-start.3) | collective-permute-done | bytes 32800 | tf_op jit(solution)/shard_map/ppermute | solution.py:164
  69.3 4.9 %attend.1 = (bf16[8,128,256]{2,1,0:T(8,128)(2,1)}, bf16[1024,128]{1,0:T(8,128)(2,1)}, f32[64,256]{1,0:T(8,128)S(1)}, bf16[4,64,256]{2,1,0:T(8,128)(2,1)S(1)}) custom-call(bf16[8,128,1152]{2,1,0:T(8,128)(2,1)S(1)} %all-to-all-done.x_ref, bf16[64,256]{1,0:T(8,128)(2,1)S(1)} %pad_maximum_fusion.1.own_ref, bf16[64,256]{1,0:T(8,128)(2,1)S(1)} %collective-permute-done.kv1_ref, ...), custom_call_target="tpu_custom_call" | custom-call | flops 1543503872 | bytes 2359296 | tf_op jit(solution)/shard_map/attend/pallas_call | solution.py:102
  74.3 0.0 all-to-all-done.2.mine_ref
  74.3 4.6 %all-to-all-start.1 = ((bf16[8,128,256]{2,1,0:T(8,128)(2,1)}), bf16[8,128,256]{2,1,0:T(8,128)(2,1)S(1)}, u32[]{:S(2)}, u32[]{:S(2)}) async-start(bf16[8,128,256]{2,1,0:T(8,128)(2,1)} %get-tuple-element.11), calls=%async_computation.1 | async-start | bytes 1048576 | tf_op jit(solution)/shard_map/all_to_all | solution.py:172
  78.9 3.5 %collective-permute-start.4 = (bf16[8,64,1024]{2,1,0:T(8,128)(2,1)}, bf16[8,64,1024]{2,1,0:T(8,128)(2,1)S(1)}, u32[]{:S(2)}, u32[]{:S(2)}) collective-permute-start(bf16[8,64,1024]{2,1,0:T(8,128)(2,1)} %all-to-all-done.2.mine_ref), channel_id=1, source_target_pairs={{0,8},{8,0},{16,24},{24,16},{32,40},{40,32},{48,56},{56,48},{64,72... | collective-permute-start | bytes 3145736 | tf_op jit(solution)/shard_map/ppermute | solution.py:168
  82.4 5.0 %all-to-all-done.1.back_ref = bf16[8,128,256]{2,1,0:T(8,128)(2,1)S(1)} async-done(((bf16[8,128,256]{2,1,0:T(8,128)(2,1)}), bf16[8,128,256]{2,1,0:T(8,128)(2,1)S(1)}, u32[]{:S(2)}, u32[]{:S(2)}) %all-to-all-start.1) | async-done | bytes 524320 | tf_op jit(solution)/shard_map/all_to_all | solution.py:172
  87.4 0.0 copy-start.1
  87.4 14.1 %all-to-all-start.3 = ((bf16[64,16,128]{2,1,0:T(8,128)(2,1)}), bf16[64,16,128]{2,1,0:T(8,128)(2,1)S(1)}, u32[]{:S(2)}, u32[]{:S(2)}) async-start(bf16[64,16,128]{2,1,0:T(8,128)(2,1)} %bitcast.7), calls=%async_computation.3 | async-start | bytes 524288 | tf_op jit(solution)/shard_map/all_to_all | solution.py:172
  101.6 8.1 %collective-permute-start.8 = (bf16[64,256]{1,0:T(8,128)(2,1)S(1)}, bf16[64,256]{1,0:T(8,128)(2,1)S(1)}, u32[]{:S(2)}, u32[]{:S(2)}) collective-permute-start(bf16[64,256]{1,0:T(8,128)(2,1)S(1)} %get-tuple-element.18), channel_id=1, source_target_pairs={{0,480},{8,488},{16,496},{24,504},{32,0},{40,8},{48,16},{56,24},{6... | collective-permute-start | bytes 98312 | tf_op jit(solution)/shard_map/ppermute | solution.py:164
  109.6 3.6 %collective-permute-start.7 = (bf16[64,256]{1,0:T(8,128)(2,1)S(1)}, bf16[64,256]{1,0:T(8,128)(2,1)S(1)}, u32[]{:S(2)}, u32[]{:S(2)}) collective-permute-start(bf16[64,256]{1,0:T(8,128)(2,1)S(1)} %get-tuple-element.19), channel_id=1, source_target_pairs={{0,488},{8,496},{16,504},{24,0},{32,8},{40,16},{48,24},{56,32},{64... | collective-permute-start | bytes 98312 | tf_op jit(solution)/shard_map/ppermute | solution.py:164
  113.3 3.1 %collective-permute-start.6 = (bf16[64,256]{1,0:T(8,128)(2,1)S(1)}, bf16[64,256]{1,0:T(8,128)(2,1)S(1)}, u32[]{:S(2)}, u32[]{:S(2)}) collective-permute-start(bf16[64,256]{1,0:T(8,128)(2,1)S(1)} %get-tuple-element.20), channel_id=1, source_target_pairs={{0,496},{8,504},{16,0},{24,8},{32,16},{40,24},{48,32},{56,40},{64,... | collective-permute-start | bytes 98312 | tf_op jit(solution)/shard_map/ppermute | solution.py:164
  116.4 4.1 %collective-permute-start.5 = (bf16[64,256]{1,0:T(8,128)(2,1)S(1)}, bf16[64,256]{1,0:T(8,128)(2,1)S(1)}, u32[]{:S(2)}, u32[]{:S(2)}) collective-permute-start(bf16[64,256]{1,0:T(8,128)(2,1)S(1)} %get-tuple-element.17), channel_id=1, source_target_pairs={{0,504},{8,0},{16,8},{24,16},{32,24},{40,32},{48,40},{56,48},{64,5... | collective-permute-start | bytes 98312 | tf_op jit(solution)/shard_map/ppermute | solution.py:164
  120.5 0.0 collective-permute-done.8
  120.5 0.0 collective-permute-done.7
  120.5 0.0 collective-permute-done.6
  120.5 1.4 %collective-permute-done.5 = bf16[64,256]{1,0:T(8,128)(2,1)S(1)} collective-permute-done((bf16[64,256]{1,0:T(8,128)(2,1)S(1)}, bf16[64,256]{1,0:T(8,128)(2,1)S(1)}, u32[]{:S(2)}, u32[]{:S(2)}) %collective-permute-start.5) | collective-permute-done | bytes 32800 | tf_op jit(solution)/shard_map/ppermute | solution.py:164
  121.9 0.6 fusion
  122.5 0.0 collective-permute-done.4.theirs_ref
  122.5 0.0 copy-start.2
  122.5 0.0 copy-done.1
  122.5 1.0 copy-done.2
  123.5 2.9 %project.1 = (bf16[128,1024]{1,0:T(8,128)(2,1)}, bf16[128,1024]{1,0:T(8,128)(2,1)}) custom-call(s32[1]{0:T(128)} %bitcast.odd_ref, bf16[8,128,256]{2,1,0:T(8,128)(2,1)} %copy-done.1, bf16[8,64,1024]{2,1,0:T(8,128)(2,1)} %all-to-all-done.2.mine_ref, bf16[8,64,1024]{2,1,0:T(8,128)(2,1)} %copy-done.2), custom_call_target="tpu_custom_call" | custom-call | flops 268435456 | bytes 2097152 | tf_op jit(solution)/shard_map/project/pallas_call | solution.py:150
  126.4 0.0 all-to-all-done.3
  126.4 0.7 reduce_sum.12
  (4 shorter events, 0.1 us)
Async XLA Ops:
  4.9 6.1 %copy-start = (bf16[128,1024]{1,0:T(8,128)(2,1)S(1)}, bf16[128,1024]{1,0:T(8,128)(2,1)}, u32[]{:S(2)}) copy-start(bf16[128,1024]{1,0:T(8,128)(2,1)} %w_ref.1) | copy-start | bytes 786436
  4.9 31.5 %all-to-all-start = ((bf16[8,128,1152]{2,1,0:T(8,128)(2,1)}), bf16[8,128,1152]{2,1,0:T(8,128)(2,1)S(1)}, u32[]{:S(2)}, u32[]{:S(2)}) async-start(bf16[8,128,1152]{2,1,0:T(8,128)(2,1)} %pad_maximum_fusion), calls=%async_computation | async-start | bytes 4718592 | tf_op jit(solution)/shard_map/all_to_all | solution.py:172
  37.5 36.8 %all-to-all-start.2 = ((bf16[8,64,1024]{2,1,0:T(8,128)(2,1)}), bf16[8,64,1024]{2,1,0:T(8,128)(2,1)}, u32[]{:S(2)}, u32[]{:S(2)}) async-start(bf16[8,64,1024]{2,1,0:T(8,128)(2,1)} %broadcast_in_dim.5), calls=%async_computation.2 | async-start | bytes 2097152 | tf_op jit(solution)/shard_map/all_to_all | solution.py:172
  43.8 20.7 %collective-permute-start = (bf16[64,256]{1,0:T(8,128)(2,1)S(1)}, bf16[64,256]{1,0:T(8,128)(2,1)S(1)}, u32[]{:S(2)}, u32[]{:S(2)}) collective-permute-start(bf16[64,256]{1,0:T(8,128)(2,1)S(1)} %pad_maximum_fusion.1.own_ref), channel_id=1, source_target_pairs={{0,8},{8,16},{16,24},{24,32},{32,40},{40,48},{48,56},{56,64},{64,7... | collective-permute-start | bytes 98312 | tf_op jit(solution)/shard_map/ppermute | solution.py:164
  51.2 13.2 %collective-permute-start.1 = (bf16[64,256]{1,0:T(8,128)(2,1)S(1)}, bf16[64,256]{1,0:T(8,128)(2,1)S(1)}, u32[]{:S(2)}, u32[]{:S(2)}) collective-permute-start(bf16[64,256]{1,0:T(8,128)(2,1)S(1)} %pad_maximum_fusion.1.own_ref), channel_id=1, source_target_pairs={{0,16},{8,24},{16,32},{24,40},{32,48},{40,56},{48,64},{56,72},{64,... | collective-permute-start | bytes 98312 | tf_op jit(solution)/shard_map/ppermute | solution.py:164
  54.8 11.6 %collective-permute-start.2 = (bf16[64,256]{1,0:T(8,128)(2,1)S(1)}, bf16[64,256]{1,0:T(8,128)(2,1)S(1)}, u32[]{:S(2)}, u32[]{:S(2)}) collective-permute-start(bf16[64,256]{1,0:T(8,128)(2,1)S(1)} %pad_maximum_fusion.1.own_ref), channel_id=1, source_target_pairs={{0,24},{8,32},{16,40},{24,48},{32,56},{40,64},{48,72},{56,80},{64,... | collective-permute-start | bytes 98312 | tf_op jit(solution)/shard_map/ppermute | solution.py:164
  58.3 11.0 %collective-permute-start.3 = (bf16[64,256]{1,0:T(8,128)(2,1)S(1)}, bf16[64,256]{1,0:T(8,128)(2,1)S(1)}, u32[]{:S(2)}, u32[]{:S(2)}) collective-permute-start(bf16[64,256]{1,0:T(8,128)(2,1)S(1)} %pad_maximum_fusion.1.own_ref), channel_id=1, source_target_pairs={{0,32},{8,40},{16,48},{24,56},{32,64},{40,72},{48,80},{56,88},{64,... | collective-permute-start | bytes 98312 | tf_op jit(solution)/shard_map/ppermute | solution.py:164
  74.3 13.1 %all-to-all-start.1 = ((bf16[8,128,256]{2,1,0:T(8,128)(2,1)}), bf16[8,128,256]{2,1,0:T(8,128)(2,1)S(1)}, u32[]{:S(2)}, u32[]{:S(2)}) async-start(bf16[8,128,256]{2,1,0:T(8,128)(2,1)} %get-tuple-element.11), calls=%async_computation.1 | async-start | bytes 1048576 | tf_op jit(solution)/shard_map/all_to_all | solution.py:172
  78.9 43.7 %collective-permute-start.4 = (bf16[8,64,1024]{2,1,0:T(8,128)(2,1)}, bf16[8,64,1024]{2,1,0:T(8,128)(2,1)S(1)}, u32[]{:S(2)}, u32[]{:S(2)}) collective-permute-start(bf16[8,64,1024]{2,1,0:T(8,128)(2,1)} %all-to-all-done.2.mine_ref), channel_id=1, source_target_pairs={{0,8},{8,0},{16,24},{24,16},{32,40},{40,32},{48,56},{56,48},{64,72... | collective-permute-start | bytes 3145736 | tf_op jit(solution)/shard_map/ppermute | solution.py:168
  87.4 35.1 %copy-start.1 = (bf16[8,128,256]{2,1,0:T(8,128)(2,1)}, bf16[8,128,256]{2,1,0:T(8,128)(2,1)S(1)}, u32[]{:S(2)}) copy-start(bf16[8,128,256]{2,1,0:T(8,128)(2,1)S(1)} %all-to-all-done.1.back_ref) | copy-start | bytes 1572868
  87.4 39.0 %all-to-all-start.3 = ((bf16[64,16,128]{2,1,0:T(8,128)(2,1)}), bf16[64,16,128]{2,1,0:T(8,128)(2,1)S(1)}, u32[]{:S(2)}, u32[]{:S(2)}) async-start(bf16[64,16,128]{2,1,0:T(8,128)(2,1)} %bitcast.7), calls=%async_computation.3 | async-start | bytes 524288 | tf_op jit(solution)/shard_map/all_to_all | solution.py:172
  101.6 18.9 %collective-permute-start.8 = (bf16[64,256]{1,0:T(8,128)(2,1)S(1)}, bf16[64,256]{1,0:T(8,128)(2,1)S(1)}, u32[]{:S(2)}, u32[]{:S(2)}) collective-permute-start(bf16[64,256]{1,0:T(8,128)(2,1)S(1)} %get-tuple-element.18), channel_id=1, source_target_pairs={{0,480},{8,488},{16,496},{24,504},{32,0},{40,8},{48,16},{56,24},{6... | collective-permute-start | bytes 98312 | tf_op jit(solution)/shard_map/ppermute | solution.py:164
  109.6 10.9 %collective-permute-start.7 = (bf16[64,256]{1,0:T(8,128)(2,1)S(1)}, bf16[64,256]{1,0:T(8,128)(2,1)S(1)}, u32[]{:S(2)}, u32[]{:S(2)}) collective-permute-start(bf16[64,256]{1,0:T(8,128)(2,1)S(1)} %get-tuple-element.19), channel_id=1, source_target_pairs={{0,488},{8,496},{16,504},{24,0},{32,8},{40,16},{48,24},{56,32},{64... | collective-permute-start | bytes 98312 | tf_op jit(solution)/shard_map/ppermute | solution.py:164
  113.3 7.2 %collective-permute-start.6 = (bf16[64,256]{1,0:T(8,128)(2,1)S(1)}, bf16[64,256]{1,0:T(8,128)(2,1)S(1)}, u32[]{:S(2)}, u32[]{:S(2)}) collective-permute-start(bf16[64,256]{1,0:T(8,128)(2,1)S(1)} %get-tuple-element.20), channel_id=1, source_target_pairs={{0,496},{8,504},{16,0},{24,8},{32,16},{40,24},{48,32},{56,40},{64,... | collective-permute-start | bytes 98312 | tf_op jit(solution)/shard_map/ppermute | solution.py:164
  116.4 5.5 %collective-permute-start.5 = (bf16[64,256]{1,0:T(8,128)(2,1)S(1)}, bf16[64,256]{1,0:T(8,128)(2,1)S(1)}, u32[]{:S(2)}, u32[]{:S(2)}) collective-permute-start(bf16[64,256]{1,0:T(8,128)(2,1)S(1)} %get-tuple-element.17), channel_id=1, source_target_pairs={{0,504},{8,0},{16,8},{24,16},{32,24},{40,32},{48,40},{56,48},{64,5... | collective-permute-start | bytes 98312 | tf_op jit(solution)/shard_map/ppermute | solution.py:164
  122.5 1.0 copy-start.2

commit v2 on v1

v2 whole, which is shorter than its diff:
```python
import functools

import jax
import jax.numpy as jnp
from jax import lax
from jax.experimental import pallas as pl
from jax.experimental.pallas import tpu as pltpu
from jax.sharding import PartitionSpec as P


HD = 64
PAIR = 2 * HD
QUAD = 2 * PAIR
WIN = 5
SRC_DEV = 64
WIDTH = WIN * SRC_DEV
SCALE = HD ** -0.5
N_Y = 4
F32 = jnp.float32
BF16 = jnp.bfloat16
NT = (((1,), (1,)), ((), ()))
VMEM = pl.BlockSpec(memory_space=pltpu.VMEM)
SMEM = pl.BlockSpec(memory_space=pltpu.SMEM)


def dot(a, b):
    return jnp.dot(a, b, preferred_element_type=F32)


def dot_nt(a, b):
    return lax.dot_general(a, b, NT, preferred_element_type=F32)


def struct(shape, dtype=BF16):
    return jax.ShapeDtypeStruct(shape, dtype)


def pack_kernel(tgt_ref, query_ref, key_ref, value_ref, out_grad_ref, own_ref, send_ref):
    depth = out_grad_ref.shape[1]
    mine = pl.ds(pl.multiple_of((tgt_ref[0] >> 1) * QUAD, QUAD), QUAD)
    own_ref[:, :QUAD] = key_ref[:, mine]
    own_ref[:, QUAD:] = value_ref[:, mine]
    for i in range(N_Y):
        send_ref[i, :, :depth] = out_grad_ref[...]
        send_ref[i, :, depth:] = query_ref[:, i * QUAD : (i + 1) * QUAD]


def pack(tgt, queries, keys, values, out_grad):
    rows, depth = queries.shape
    return pl.pallas_call(
        pack_kernel,
        out_shape=(struct((SRC_DEV, 2 * QUAD)), struct((N_Y, rows, depth + QUAD))),
        in_specs=[SMEM] + [VMEM] * 4,
        out_specs=(VMEM,) * 2,
        compiler_params=pltpu.CompilerParams(vmem_limit_bytes=60 * 1024 * 1024),
        name="pack",
    )(tgt, queries, keys, values, out_grad)


def attend_kernel(
    chunk, tgt_ref, blk_ref, x_ref, own_ref, kv1_ref, kv2_ref, kv3_ref, kv4_ref, mine_ref, theirs_ref,
    back0, back1, back2, back3, four_ref,
    key_ref, value_ref, key_t_ref, value_t_ref, weight_ref, key_acc, value_acc, tile_acc,
):
    depth = mine_ref.shape[1]
    y = tgt_ref[0] >> 1
    low = tgt_ref[0] & 1
    lane = lax.broadcasted_iota(jnp.int32, (SRC_DEV, PAIR), 1)
    zero = jnp.zeros((SRC_DEV, PAIR), BF16)
    weight_ref[pl.ds(pl.multiple_of(low * PAIR, PAIR), PAIR), :] = mine_ref[...]
    weight_ref[pl.ds(pl.multiple_of((1 - low) * PAIR, PAIR), PAIR), :] = theirs_ref[...]
    for pair in range(2):
        for w, ref in enumerate((own_ref, kv1_ref, kv2_ref, kv3_ref, kv4_ref)):
            block_key = ref[:, pair * PAIR : (pair + 1) * PAIR]
            block_value = ref[:, QUAD + pair * PAIR : QUAD + (pair + 1) * PAIR]
            for head in range(2):
                own_lanes = (lane < HD) if head == 0 else (lane >= HD)
                at = pl.ds(head * WIDTH + w * SRC_DEV, SRC_DEV)
                key_ref[pair, at, :] = jnp.where(own_lanes, block_key, zero)
                value_ref[pair, at, :] = jnp.where(own_lanes, block_value, zero)
        key_t_ref[pair] = key_ref[pair].T
        value_t_ref[pair] = value_ref[pair].T
    backs = (back0, back1, back2, back3)
    rows = x_ref.shape[1]
    for step in range(N_Y // 2):
        here = (2 * step, 2 * step + 1)
        out_grad = jnp.concatenate([x_ref[y ^ s, :, :depth] for s in here], axis=0)
        att_grad_all = dot_nt(out_grad, weight_ref[...]).astype(BF16)
        attended, query_grad = [], []
        for pair in range(2):
            columns = slice(depth + pair * PAIR, depth + (pair + 1) * PAIR)
            query = jnp.concatenate([x_ref[y ^ s, :, columns] for s in here], axis=0)
            att_grad = att_grad_all[:, pair * PAIR : (pair + 1) * PAIR]
            scores = dot_nt(key_ref[pair], query)
            prob_grad = dot_nt(value_ref[pair], att_grad)
            probs_low, score_grad = [], []
            for head in range(2):
                part = scores[head * WIDTH : (head + 1) * WIDTH]
                grad = prob_grad[head * WIDTH : (head + 1) * WIDTH]
                top = jnp.max(part, axis=0, keepdims=True)
                expo = jnp.exp((part - top) * SCALE)
                probs = expo * (1.0 / jnp.sum(expo, axis=0, keepdims=True))
                center = jnp.sum(probs * grad, axis=0, keepdims=True)
                probs_low.append(probs.astype(BF16))
                score_grad.append((SCALE * probs * (grad - center)).astype(BF16))
            probs_low = jnp.concatenate(probs_low, axis=0)
            score_grad = jnp.concatenate(score_grad, axis=0)
            attended.append(dot(value_t_ref[pair], probs_low).astype(BF16))
            query_grad.append(dot(key_t_ref[pair], score_grad).astype(BF16))
            key_part = dot(score_grad, query)
            value_part = dot(probs_low, att_grad)
            if step == 0:
                key_acc[pair] = key_part
                value_acc[pair] = value_part
            else:
                key_acc[pair] += key_part
                value_acc[pair] += value_part
        attended = jnp.concatenate(attended, axis=0)
        query_grad = jnp.concatenate(query_grad, axis=0).T
        out_part = dot(attended.T, weight_ref[...]).astype(BF16)
        for k, i in enumerate(here):
            backs[i][:, :depth] = out_part[k * rows : (k + 1) * rows]
            backs[i][:, depth:] = query_grad[k * rows : (k + 1) * rows]
        tile_part = dot(attended, out_grad)
        if step == 0:
            tile_acc[...] = tile_part
        else:
            tile_acc[...] += tile_part
    core = blk_ref[0] & 1
    rows_tile = depth // 2
    for half in range(2):
        turned = tile_acc[half * PAIR : (half + 1) * PAIR, :].T.reshape(-1, 2, chunk, PAIR)
        for to in range(2):
            four_ref[2 * to + half, :rows_tile, :] = turned[:, to].reshape(rows_tile, PAIR).astype(BF16)
        for other in range(2):
            to = 2 * (core ^ other) + half
            for slot in range(WIN // 2 + 1):
                w = 2 * slot + other
                for part, acc in enumerate((key_acc, value_acc)):
                    at = pl.ds(rows_tile + (2 * slot + part) * SRC_DEV, SRC_DEV)
                    if w >= WIN:
                        four_ref[to, at, :] = zero
                        continue
                    first = acc[half, w * SRC_DEV : (w + 1) * SRC_DEV, :]
                    second = acc[half, WIDTH + w * SRC_DEV : WIDTH + (w + 1) * SRC_DEV, :]
                    four_ref[to, at, :] = jnp.where(lane < HD, first, second).astype(BF16)


def attend(tgt, blk, n_blk, x, kvs, mine, theirs):
    _, rows, wide = x.shape
    depth = mine.shape[1]
    flops = 2 * N_Y * rows * (6 * 2 * WIDTH * QUAD + 3 * depth * QUAD)
    return pl.pallas_call(
        functools.partial(attend_kernel, depth // n_blk),
        out_shape=(struct((rows, wide)),) * N_Y
        + (struct((4, depth // 2 + 2 * (WIN // 2 + 1) * SRC_DEV, PAIR)),),
        in_specs=[SMEM] * 2 + [VMEM] * 8,
        out_specs=(VMEM,) * (N_Y + 1),
        scratch_shapes=[
            pltpu.VMEM((2, 2 * WIDTH, PAIR), BF16),
            pltpu.VMEM((2, 2 * WIDTH, PAIR), BF16),
            pltpu.VMEM((2, PAIR, 2 * WIDTH), BF16),
            pltpu.VMEM((2, PAIR, 2 * WIDTH), BF16),
            pltpu.VMEM((QUAD, depth), BF16),
            pltpu.VMEM((2, 2 * WIDTH, PAIR), F32),
            pltpu.VMEM((2, 2 * WIDTH, PAIR), F32),
            pltpu.VMEM((QUAD, depth), F32),
        ],
        cost_estimate=pl.CostEstimate(
            flops=flops, bytes_accessed=4 * N_Y * rows * wide, transcendentals=4 * WIDTH * N_Y * rows
        ),
        compiler_params=pltpu.CompilerParams(vmem_limit_bytes=60 * 1024 * 1024),
        name="attend",
    )(tgt, blk, x, *kvs, mine, theirs)


def combine_kernel(blk_ref, four_ref, tile_ref, own_ref, near_ref, far_ref):
    chips, chunk, _ = tile_ref.shape
    rows_tile = chips * chunk
    block = 2 * SRC_DEV
    core = blk_ref[0] & 1
    total = four_ref[0, :rows_tile, :].astype(F32)
    for i in range(1, 4):
        total = total + four_ref[i, :rows_tile, :].astype(F32)
    tile_ref[...] = total.astype(BF16).reshape(chips, chunk, PAIR)

    def part(of_core, slot):
        at = pl.ds(rows_tile + slot * block, block)
        return four_ref[2 * of_core, at, :].astype(F32) + four_ref[2 * of_core + 1, at, :].astype(F32)

    one, three = part(1 - core, 0), part(1 - core, 1)
    zero = jnp.zeros_like(one)
    first = core == 0
    own_ref[...] = part(core, 0) + jnp.where(first, one, zero)
    near_ref[...] = (part(core, 1) + jnp.where(first, three, one)).astype(BF16)
    far_ref[...] = (part(core, 2) + jnp.where(first, zero, three)).astype(BF16)


def combine(blk, n_blk, four):
    rows_tile = four.shape[1] - 2 * (WIN // 2 + 1) * SRC_DEV
    chips = n_blk // 2
    block = (2 * SRC_DEV, PAIR)
    return pl.pallas_call(
        combine_kernel,
        out_shape=(struct((chips, rows_tile // chips, PAIR)), struct(block, F32), struct(block), struct(block)),
        in_specs=[SMEM, VMEM],
        out_specs=(VMEM,) * 4,
        compiler_params=pltpu.CompilerParams(vmem_limit_bytes=8 * 1024 * 1024),
        name="combine",
    )(blk, four)


def finish_kernel(tgt_ref, back0, back1, back2, back3, own_ref, near_ref, far_ref, out_ref, query_grad_ref, key_grad_ref, value_grad_ref):
    depth = out_ref.shape[1]
    total = None
    for s, ref in enumerate((back0, back1, back2, back3)):
        part = ref[:, :depth].astype(F32)
        total = part if total is None else total + part
        query_grad_ref[:, pl.ds(pl.multiple_of(((tgt_ref[0] >> 1) ^ s) * QUAD, QUAD), QUAD)] = ref[:, depth:]
    out_ref[...] = total.astype(BF16)
    grad = (own_ref[...] + near_ref[...].astype(F32) + far_ref[...].astype(F32)).astype(BF16)
    key_grad_ref[...] = grad[:SRC_DEV]
    value_grad_ref[...] = grad[SRC_DEV:]


def finish(tgt, backs, own, near, far):
    rows, wide = backs[0].shape
    out, grad = struct((rows, wide - QUAD)), struct((SRC_DEV, PAIR))
    return pl.pallas_call(
        finish_kernel,
        out_shape=(out, out, grad, grad),
        in_specs=[SMEM] + [VMEM] * (N_Y + 3),
        out_specs=(VMEM,) * 4,
        cost_estimate=pl.CostEstimate(
            flops=N_Y * rows * wide, bytes_accessed=2 * N_Y * rows * wide, transcendentals=0
        ),
        compiler_params=pltpu.CompilerParams(vmem_limit_bytes=8 * 1024 * 1024),
        name="finish",
    )(tgt, *backs, own, near, far)


def total_kernel(part_ref, total_ref):
    total = part_ref[0].astype(F32)
    for i in range(1, part_ref.shape[0]):
        total = total + part_ref[i].astype(F32)
    total_ref[...] = total.astype(BF16)


def total_of(parts):
    return pl.pallas_call(
        total_kernel,
        out_shape=struct(parts.shape[1:]),
        in_specs=[VMEM],
        out_specs=VMEM,
        compiler_params=pltpu.CompilerParams(vmem_limit_bytes=4 * 1024 * 1024),
        name="total",
    )(parts)


def shift(value, axis, steps):
    count = lax.axis_size(axis)
    return lax.ppermute(value, axis, [(i, (i + steps) % count) for i in range(count)])


def flip(value, bits):
    return lax.ppermute(value, "tgt", [(i, i ^ bits) for i in range(lax.axis_size("tgt"))])


def local(queries, keys, values, out_weight, out_grad):
    n_blk = lax.axis_size("blk")
    n_tgt = lax.axis_size("tgt")
    tgt = lax.axis_index("tgt").reshape(1)
    blk = lax.axis_index("blk").reshape(1)
    own, send = pack(tgt, queries, keys, values, out_grad)
    groups = [[2 * y + low for y in range(N_Y)] for low in range(2)]
    x = lax.all_to_all(
        send, "tgt", split_axis=0, concat_axis=0, tiled=True, axis_index_groups=groups
    )
    theirs = flip(out_weight, 1)
    kvs = [own] + [shift(own, "blk", w) for w in range(1, WIN)]
    *backs, four = attend(tgt, blk, n_blk, x, kvs, out_weight, theirs)
    fours = [
        [(2 * chip + core) * n_tgt + 2 * y + low for core in range(2) for low in range(2)]
        for chip in range(n_blk // 2)
        for y in range(N_Y)
    ]
    four = lax.all_to_all(four, ("blk", "tgt"), split_axis=0, concat_axis=0, tiled=True, axis_index_groups=fours)
    backs = [backs[0]] + [flip(backs[s], 2 * s) for s in range(1, N_Y)]
    tile, own_grad, near, far = combine(blk, n_blk, four)
    cores = [list(range(core, n_blk, 2)) for core in range(2)]
    tiles = lax.all_to_all(
        tile, "blk", split_axis=0, concat_axis=0, tiled=True, axis_index_groups=cores
    )
    near, far = shift(near, "blk", -2), shift(far, "blk", -4)
    outputs, query_grad, key_grad, value_grad = finish(tgt, backs, own_grad, near, far)
    weight_grad = total_of(tiles).T
    return outputs, query_grad, key_grad, value_grad, weight_grad


def solution(mesh):
    return jax.shard_map(
        local,
        mesh=mesh,
        in_specs=(
            P(("blk", "tgt"), None),
            P("blk", None),
            P("blk", None),
            P("tgt", None),
            P(("blk", "tgt"), None),
        ),
        out_specs=(
            P(("blk", "tgt"), None),
            P(("blk", "tgt"), None),
            P("blk", "tgt"),
            P("blk", "tgt"),
            P("tgt", "blk"),
        ),
        check_vma=False,
    )
```

time: 128 us -> 97.6 us (0.76)
  waiting for transfers between devices: 36.6 us -> 8.37 us
  blocking collectives: 0 us -> 18.2 us
  starting transfers between devices: 73.4 us -> 57 us
  local copies, waits for them, and re-layouts: 5.96 us -> 1.18 us
  Pallas kernels: 7.85 us -> 11.4 us
  other arithmetic: 2.4 us -> 0 us
    all_to_all x4 -> x2, waiting for transfers between devices: 30.4 us -> 0.01 us  [the longest x1 0.01 us: local(): lax.all_to_all(send, 'tgt', split_axis=0, concat_axis=0, tiled=True, axis...]
    all_to_all x0 -> x1, blocking collectives: none -> 18.2 us  [local(): lax.all_to_all(four, ('blk', 'tgt'), split_axis=0, concat_axis=0, tiled=T...]
    all_to_all x4 -> x2, starting transfers between devices: 30.3 us -> 15.3 us  [the longest x1 10.2 us: local(): lax.all_to_all(tile, 'blk', split_axis=0, concat_axis=0, tiled=True, axis...]
    ppermute x8 -> x6, starting transfers between devices: 39.5 us -> 28.7 us  [shift(): lax.ppermute(value, axis, [(i, (i + steps) % count) for i in range(count)])]
    ppermute x1 -> x4, starting transfers between devices: 3.54 us -> 13 us  [flip(): lax.ppermute(value, 'tgt', [(i, i ^ bits) for i in range(lax.axis_size('t...]
    ppermute x1 -> x4, waiting for transfers between devices: 0.01 us -> 5.24 us  [flip(): lax.ppermute(value, 'tgt', [(i, i ^ bits) for i in range(lax.axis_size('t...]
    pallas_call x2 -> x5, Pallas kernels: 7.85 us -> 11.4 us  [the longest x1 6.84 us: attend(): pl.pallas_call(functools.partial(attend_kernel, depth // n_blk), out_shap...]
    ppermute x8 -> x6, waiting for transfers between devices: 6.21 us -> 3.12 us  [shift(): lax.ppermute(value, axis, [(i, (i + steps) % count) for i in range(count)])]
  transfers between devices with their start and end apart: 13 -> 12, of which waited for: 5 -> 3; matrix products, arithmetic and copies ran while one was open for 1% -> 0% of each run, Pallas kernels for 6% -> 1%
where the time goes in v2:
time: 97.6 us; the launch traced here: 97 us
  starting transfers between devices  57 us (58%)
  blocking collectives  18.2 us (19%)
  Pallas kernels  11.4 us (12%)
  waiting for transfers between devices  8.37 us (9%)
  local copies, waits for them, and re-layouts  1.18 us (1%)
    ppermute x6, starting transfers between devices, shift(): lax.ppermute(value, axis, [(i, (i + steps) % count) for i in range(count)])  28.7 us
    all_to_all x1, blocking collectives, local(): lax.all_to_all(four, ('blk', 'tgt'), split_axis=0, concat_axis=0, tiled=T...  18.2 us
    ppermute x4, starting transfers between devices, flip(): lax.ppermute(value, 'tgt', [(i, i ^ bits) for i in range(lax.axis_size('t...  13 us
    all_to_all x1, starting transfers between devices, local(): lax.all_to_all(tile, 'blk', split_axis=0, concat_axis=0, tiled=True, axis...  10.2 us
    pallas_call x1, Pallas kernels, attend(): pl.pallas_call(functools.partial(attend_kernel, depth // n_blk), out_shap...  6.84 us
    ppermute x4, waiting for transfers between devices, flip(): lax.ppermute(value, 'tgt', [(i, i ^ bits) for i in range(lax.axis_size('t...  5.24 us
    all_to_all x1, starting transfers between devices, local(): lax.all_to_all(send, 'tgt', split_axis=0, concat_axis=0, tiled=True, axis...  5.14 us
    ppermute x6, waiting for transfers between devices, shift(): lax.ppermute(value, axis, [(i, (i + steps) % count) for i in range(count)])  3.12 us
  transfers between devices with their start and end apart: 12, of which 3 were waited for; matrix products, arithmetic and copies ran while one was open for 0% of the time, Pallas kernels for 1%

profile of v2, /device:TPU:1, one launch (start us, length us, event | category | flops | bytes accessed | tf_op | source)
XLA Modules:
  0.0 97.0 jit_solution(7591018462194488795)
XLA Ops:
  0.6 2.3 %pack.1 = (bf16[64,512]{1,0:T(8,128)(2,1)}, bf16[4,128,1280]{2,1,0:T(8,128)(2,1)}) custom-call(s32[1]{0:T(128)} %bitcast.tgt_ref, bf16[128,1024]{1,0:T(8,128)(2,1)} %query_ref.1, bf16[64,1024]{1,0:T(8,128)(2,1)} %key_ref.1, bf16[64,1024]{1,0:T(8,128)(2,1)} %value_ref.1, bf16[128,1024]{1,0:T(8,128)(2,1)} %out_grad_ref.1), custom_call_target="tpu_custom_call" | custom-call | tf_op jit(solution)/shard_map/pack/pallas_call | solution.py:50
  3.0 0.0 copy-start.5
  3.0 0.0 copy-start.7
  3.0 5.1 %all-to-all-start = ((bf16[4,128,1280]{2,1,0:T(8,128)(2,1)}), bf16[4,128,1280]{2,1,0:T(8,128)(2,1)S(1)}, u32[]{:S(2)}, u32[]{:S(2)}) async-start(bf16[4,128,1280]{2,1,0:T(8,128)(2,1)} %get-tuple-element.20), calls=%async_computation | async-start | bytes 2621440 | tf_op jit(solution)/shard_map/all_to_all | solution.py:276
  8.1 0.0 copy-done.5
  8.1 3.1 %collective-permute-start.4 = (bf16[128,1024]{1,0:T(8,128)(2,1)S(1)}, bf16[128,1024]{1,0:T(8,128)(2,1)S(1)}, u32[]{:S(2)}, u32[]{:S(2)}) collective-permute-start(bf16[128,1024]{1,0:T(8,128)(2,1)S(1)} %copy-done.5), channel_id=1, source_target_pairs={{0,1},{1,0},{2,3},{3,2},{4,5},{5,4},{6,7},{7,6},{8,9},{9,8},{10,11... | collective-permute-start | bytes 786440 | tf_op jit(solution)/shard_map/ppermute | solution.py:266
  11.2 0.0 copy-done.7
  11.2 4.9 %collective-permute-start.3 = (bf16[64,512]{1,0:T(8,128)(2,1)S(1)}, bf16[64,512]{1,0:T(8,128)(2,1)S(1)}, u32[]{:S(2)}, u32[]{:S(2)}) collective-permute-start(bf16[64,512]{1,0:T(8,128)(2,1)S(1)} %copy-done.7), channel_id=1, source_target_pairs={{0,32},{8,40},{16,48},{24,56},{32,64},{40,72},{48,80},{56,88},{64,... | collective-permute-start | bytes 196616 | tf_op jit(solution)/shard_map/ppermute | solution.py:262
  16.1 7.5 %collective-permute-start.2 = (bf16[64,512]{1,0:T(8,128)(2,1)S(1)}, bf16[64,512]{1,0:T(8,128)(2,1)S(1)}, u32[]{:S(2)}, u32[]{:S(2)}) collective-permute-start(bf16[64,512]{1,0:T(8,128)(2,1)S(1)} %copy-done.7), channel_id=1, source_target_pairs={{0,24},{8,32},{16,40},{24,48},{32,56},{40,64},{48,72},{56,80},{64,... | collective-permute-start | bytes 196616 | tf_op jit(solution)/shard_map/ppermute | solution.py:262
  23.7 3.5 %collective-permute-start.1 = (bf16[64,512]{1,0:T(8,128)(2,1)S(1)}, bf16[64,512]{1,0:T(8,128)(2,1)S(1)}, u32[]{:S(2)}, u32[]{:S(2)}) collective-permute-start(bf16[64,512]{1,0:T(8,128)(2,1)S(1)} %copy-done.7), channel_id=1, source_target_pairs={{0,16},{8,24},{16,32},{24,40},{32,48},{40,56},{48,64},{56,72},{64,... | collective-permute-start | bytes 196616 | tf_op jit(solution)/shard_map/ppermute | solution.py:262
  27.2 1.9 %collective-permute-start = (bf16[64,512]{1,0:T(8,128)(2,1)S(1)}, bf16[64,512]{1,0:T(8,128)(2,1)S(1)}, u32[]{:S(2)}, u32[]{:S(2)}) collective-permute-start(bf16[64,512]{1,0:T(8,128)(2,1)S(1)} %copy-done.7), channel_id=1, source_target_pairs={{0,8},{8,16},{16,24},{24,32},{32,40},{40,48},{48,56},{56,64},{64,7... | collective-permute-start | bytes 196616 | tf_op jit(solution)/shard_map/ppermute | solution.py:262
  29.2 0.0 collective-permute-done.3.kv4_ref
  29.2 0.0 copy-start.8
  29.2 1.5 %collective-permute-done.2.kv3_ref = bf16[64,512]{1,0:T(8,128)(2,1)S(1)} collective-permute-done((bf16[64,512]{1,0:T(8,128)(2,1)S(1)}, bf16[64,512]{1,0:T(8,128)(2,1)S(1)}, u32[]{:S(2)}, u32[]{:S(2)}) %collective-permute-start.2) | collective-permute-done | bytes 65568 | tf_op jit(solution)/shard_map/ppermute | solution.py:262
  30.6 1.7 %collective-permute-done.1.kv2_ref = bf16[64,512]{1,0:T(8,128)(2,1)S(1)} collective-permute-done((bf16[64,512]{1,0:T(8,128)(2,1)S(1)}, bf16[64,512]{1,0:T(8,128)(2,1)S(1)}, u32[]{:S(2)}, u32[]{:S(2)}) %collective-permute-start.1) | collective-permute-done | bytes 65568 | tf_op jit(solution)/shard_map/ppermute | solution.py:262
  32.3 0.0 collective-permute-done.kv1_ref
  32.3 0.0 collective-permute-done.4.theirs_ref
  32.3 0.0 copy-start.6
  32.3 0.0 all-to-all-done.x_ref
  32.3 0.0 copy-start.1
  32.3 0.0 copy-done.8
  32.3 0.0 copy-done.9
  32.4 0.6 copy-done.10
  32.9 0.0 copy-done.11
  32.9 0.1 copy-done.6
  33.0 0.5 copy-done.1
  33.5 6.8 %attend.1 = (bf16[128,1280]{1,0:T(8,128)(2,1)}, bf16[128,1280]{1,0:T(8,128)(2,1)}, bf16[128,1280]{1,0:T(8,128)(2,1)}, bf16[128,1280]{1,0:T(8,128)(2,1)}, bf16[4,896,128]{2,1,0:T(8,128)(2,1)}) custom-call(s32[1]{0:T(128)} %bitcast.tgt_ref, s32[1]{0:T(128)} %bitcast.1.blk_ref, bf16[4,128,1280]{2,1,0:T(8,128)(2,1)} %copy-done.1, ...), custom_call_target="tpu_custom_call" | custom-call | flops 1811939328 | bytes 2621440 | tf_op jit(solution)/shard_map/attend/pallas_call | solution.py:153
  40.3 0.0 copy-start
  40.4 18.2 %all_to_all.15.four_ref = bf16[4,896,128]{2,1,0:T(8,128)(2,1)S(1)} all-to-all(bf16[4,896,128]{2,1,0:T(8,128)(2,1)} %get-tuple-element.26), channel_id=1, replica_groups={{0,1,8,9},{2,3,10,11},{4,5,12,13},{6,7,14,15},{16,17,24,25},{18,19,26,2..., dimensions={0} | all-to-all | bytes 1835008 | tf_op jit(solution)/shard_map/all_to_all | solution.py:287
  58.6 0.7 combine.1
  59.3 10.2 %all-to-all-start.2 = ((bf16[32,16,128]{2,1,0:T(8,128)(2,1)}), bf16[32,16,128]{2,1,0:T(8,128)(2,1)S(1)}, u32[]{:S(2)}, u32[]{:S(2)}) async-start(bf16[32,16,128]{2,1,0:T(8,128)(2,1)} %get-tuple-element.34), calls=%async_computation.2 | async-start | bytes 262144 | tf_op jit(solution)/shard_map/all_to_all | solution.py:291
  69.4 0.0 copy-done.4
  69.5 3.6 %collective-permute-start.5 = (bf16[128,1280]{1,0:T(8,128)(2,1)S(1)}, bf16[128,1280]{1,0:T(8,128)(2,1)S(1)}, u32[]{:S(2)}, u32[]{:S(2)}) collective-permute-start(bf16[128,1280]{1,0:T(8,128)(2,1)S(1)} %copy-done.4), channel_id=1, source_target_pairs={{0,2},{1,3},{2,0},{3,1},{4,6},{5,7},{6,4},{7,5},{8,10},{9,11},{10,... | collective-permute-start | bytes 983048 | tf_op jit(solution)/shard_map/ppermute | solution.py:266
  73.1 0.0 copy-done.3
  73.1 4.3 %collective-permute-start.6 = (bf16[128,1280]{1,0:T(8,128)(2,1)S(1)}, bf16[128,1280]{1,0:T(8,128)(2,1)S(1)}, u32[]{:S(2)}, u32[]{:S(2)}) collective-permute-start(bf16[128,1280]{1,0:T(8,128)(2,1)S(1)} %copy-done.3), channel_id=1, source_target_pairs={{0,4},{1,5},{2,6},{3,7},{4,0},{5,1},{6,2},{7,3},{8,12},{9,13},{10,... | collective-permute-start | bytes 983048 | tf_op jit(solution)/shard_map/ppermute | solution.py:266
  77.4 0.0 copy-done.2
  77.4 1.9 %collective-permute-start.7 = (bf16[128,1280]{1,0:T(8,128)(2,1)S(1)}, bf16[128,1280]{1,0:T(8,128)(2,1)S(1)}, u32[]{:S(2)}, u32[]{:S(2)}) collective-permute-start(bf16[128,1280]{1,0:T(8,128)(2,1)S(1)} %copy-done.2), channel_id=1, source_target_pairs={{0,6},{1,7},{2,4},{3,5},{4,2},{5,3},{6,0},{7,1},{8,14},{9,15},{10,... | collective-permute-start | bytes 983048 | tf_op jit(solution)/shard_map/ppermute | solution.py:266
  79.4 6.8 %collective-permute-start.8 = (bf16[128,128]{1,0:T(8,128)(2,1)S(1)}, bf16[128,128]{1,0:T(8,128)(2,1)S(1)}, u32[]{:S(2)}, u32[]{:S(2)}) collective-permute-start(bf16[128,128]{1,0:T(8,128)(2,1)S(1)} %get-tuple-element.28), channel_id=1, source_target_pairs={{0,496},{8,504},{16,0},{24,8},{32,16},{40,24},{48,32},{56,40},{64,... | collective-permute-start | bytes 98312 | tf_op jit(solution)/shard_map/ppermute | solution.py:262
  86.2 4.0 %collective-permute-start.9 = (bf16[128,128]{1,0:T(8,128)(2,1)S(1)}, bf16[128,128]{1,0:T(8,128)(2,1)S(1)}, u32[]{:S(2)}, u32[]{:S(2)}) collective-permute-start(bf16[128,128]{1,0:T(8,128)(2,1)S(1)} %get-tuple-element.29), channel_id=1, source_target_pairs={{0,480},{8,488},{16,496},{24,504},{32,0},{40,8},{48,16},{56,24},{6... | collective-permute-start | bytes 98312 | tf_op jit(solution)/shard_map/ppermute | solution.py:262
  90.2 0.0 collective-permute-done.5.back1
  90.2 0.0 collective-permute-done.6.back2
  90.2 5.2 %collective-permute-done.7.back3 = bf16[128,1280]{1,0:T(8,128)(2,1)S(1)} collective-permute-done((bf16[128,1280]{1,0:T(8,128)(2,1)S(1)}, bf16[128,1280]{1,0:T(8,128)(2,1)S(1)}, u32[]{:S(2)}, u32[]{:S(2)}) %collective-permute-start.7) | collective-permute-done | bytes 327712 | tf_op jit(solution)/shard_map/ppermute | solution.py:266
  95.5 0.0 collective-permute-done.8.near_ref
  95.5 0.0 collective-permute-done.9.far_ref
  95.5 0.0 copy-done
  95.5 0.9 finish.1
  96.4 0.0 all-to-all-done.2.part_ref
  96.4 0.6 total.1
  (6 shorter events, 0.0 us)
Async XLA Ops:
  3.0 5.1 %copy-start.5 = (bf16[128,1024]{1,0:T(8,128)(2,1)S(1)}, bf16[128,1024]{1,0:T(8,128)(2,1)}, u32[]{:S(2)}) copy-start(bf16[128,1024]{1,0:T(8,128)(2,1)} %mine_ref.1) | copy-start | bytes 786436
  3.0 8.3 %copy-start.7 = (bf16[64,512]{1,0:T(8,128)(2,1)S(1)}, bf16[64,512]{1,0:T(8,128)(2,1)}, u32[]{:S(2)}) copy-start(bf16[64,512]{1,0:T(8,128)(2,1)} %get-tuple-element.21.own_ref) | copy-start | bytes 196612
  3.0 29.3 %all-to-all-start = ((bf16[4,128,1280]{2,1,0:T(8,128)(2,1)}), bf16[4,128,1280]{2,1,0:T(8,128)(2,1)S(1)}, u32[]{:S(2)}, u32[]{:S(2)}) async-start(bf16[4,128,1280]{2,1,0:T(8,128)(2,1)} %get-tuple-element.20), calls=%async_computation | async-start | bytes 2621440 | tf_op jit(solution)/shard_map/all_to_all | solution.py:276
  8.1 24.2 %collective-permute-start.4 = (bf16[128,1024]{1,0:T(8,128)(2,1)S(1)}, bf16[128,1024]{1,0:T(8,128)(2,1)S(1)}, u32[]{:S(2)}, u32[]{:S(2)}) collective-permute-start(bf16[128,1024]{1,0:T(8,128)(2,1)S(1)} %copy-done.5), channel_id=1, source_target_pairs={{0,1},{1,0},{2,3},{3,2},{4,5},{5,4},{6,7},{7,6},{8,9},{9,8},{10,11... | collective-permute-start | bytes 786440 | tf_op jit(solution)/shard_map/ppermute | solution.py:266
  11.2 17.9 %collective-permute-start.3 = (bf16[64,512]{1,0:T(8,128)(2,1)S(1)}, bf16[64,512]{1,0:T(8,128)(2,1)S(1)}, u32[]{:S(2)}, u32[]{:S(2)}) collective-permute-start(bf16[64,512]{1,0:T(8,128)(2,1)S(1)} %copy-done.7), channel_id=1, source_target_pairs={{0,32},{8,40},{16,48},{24,56},{32,64},{40,72},{48,80},{56,88},{64,... | collective-permute-start | bytes 196616 | tf_op jit(solution)/shard_map/ppermute | solution.py:262
  16.1 14.5 %collective-permute-start.2 = (bf16[64,512]{1,0:T(8,128)(2,1)S(1)}, bf16[64,512]{1,0:T(8,128)(2,1)S(1)}, u32[]{:S(2)}, u32[]{:S(2)}) collective-permute-start(bf16[64,512]{1,0:T(8,128)(2,1)S(1)} %copy-done.7), channel_id=1, source_target_pairs={{0,24},{8,32},{16,40},{24,48},{32,56},{40,64},{48,72},{56,80},{64,... | collective-permute-start | bytes 196616 | tf_op jit(solution)/shard_map/ppermute | solution.py:262
  23.7 8.6 %collective-permute-start.1 = (bf16[64,512]{1,0:T(8,128)(2,1)S(1)}, bf16[64,512]{1,0:T(8,128)(2,1)S(1)}, u32[]{:S(2)}, u32[]{:S(2)}) collective-permute-start(bf16[64,512]{1,0:T(8,128)(2,1)S(1)} %copy-done.7), channel_id=1, source_target_pairs={{0,16},{8,24},{16,32},{24,40},{32,48},{40,56},{48,64},{56,72},{64,... | collective-permute-start | bytes 196616 | tf_op jit(solution)/shard_map/ppermute | solution.py:262
  27.2 5.1 %collective-permute-start = (bf16[64,512]{1,0:T(8,128)(2,1)S(1)}, bf16[64,512]{1,0:T(8,128)(2,1)S(1)}, u32[]{:S(2)}, u32[]{:S(2)}) collective-permute-start(bf16[64,512]{1,0:T(8,128)(2,1)S(1)} %copy-done.7), channel_id=1, source_target_pairs={{0,8},{8,16},{16,24},{24,32},{32,40},{40,48},{48,56},{56,64},{64,7... | collective-permute-start | bytes 196616 | tf_op jit(solution)/shard_map/ppermute | solution.py:262
  29.2 3.2 %copy-start.8 = (bf16[64,512]{1,0:T(8,128)(2,1)}, bf16[64,512]{1,0:T(8,128)(2,1)S(1)}, u32[]{:S(2)}) copy-start(bf16[64,512]{1,0:T(8,128)(2,1)S(1)} %collective-permute-done.3.kv4_ref) | copy-start | bytes 196612
  30.6 1.7 %copy-start.9 = (bf16[64,512]{1,0:T(8,128)(2,1)}, bf16[64,512]{1,0:T(8,128)(2,1)S(1)}, u32[]{:S(2)}) copy-start(bf16[64,512]{1,0:T(8,128)(2,1)S(1)} %collective-permute-done.2.kv3_ref) | copy-start | bytes 196612
  32.3 0.6 copy-start.10
  32.3 0.7 copy-start.11
  32.3 0.7 copy-start.6
  32.3 1.2 %copy-start.1 = (bf16[4,128,1280]{2,1,0:T(8,128)(2,1)}, bf16[4,128,1280]{2,1,0:T(8,128)(2,1)S(1)}, u32[]{:S(2)}) copy-start(bf16[4,128,1280]{2,1,0:T(8,128)(2,1)S(1)} %all-to-all-done.x_ref) | copy-start | bytes 3932164
  40.3 29.1 %copy-start.4 = (bf16[128,1280]{1,0:T(8,128)(2,1)S(1)}, bf16[128,1280]{1,0:T(8,128)(2,1)}, u32[]{:S(2)}) copy-start(bf16[128,1280]{1,0:T(8,128)(2,1)} %get-tuple-element.23) | copy-start | bytes 983044
  40.3 32.8 %copy-start.3 = (bf16[128,1280]{1,0:T(8,128)(2,1)S(1)}, bf16[128,1280]{1,0:T(8,128)(2,1)}, u32[]{:S(2)}) copy-start(bf16[128,1280]{1,0:T(8,128)(2,1)} %get-tuple-element.24) | copy-start | bytes 983044
  40.3 37.1 %copy-start.2 = (bf16[128,1280]{1,0:T(8,128)(2,1)S(1)}, bf16[128,1280]{1,0:T(8,128)(2,1)}, u32[]{:S(2)}) copy-start(bf16[128,1280]{1,0:T(8,128)(2,1)} %get-tuple-element.25) | copy-start | bytes 983044
  40.3 55.1 %copy-start = (bf16[128,1280]{1,0:T(8,128)(2,1)S(1)}, bf16[128,1280]{1,0:T(8,128)(2,1)}, u32[]{:S(2)}) copy-start(bf16[128,1280]{1,0:T(8,128)(2,1)} %get-tuple-element.22.back0) | copy-start | bytes 983044
  59.3 37.1 %all-to-all-start.2 = ((bf16[32,16,128]{2,1,0:T(8,128)(2,1)}), bf16[32,16,128]{2,1,0:T(8,128)(2,1)S(1)}, u32[]{:S(2)}, u32[]{:S(2)}) async-start(bf16[32,16,128]{2,1,0:T(8,128)(2,1)} %get-tuple-element.34), calls=%async_computation.2 | async-start | bytes 262144 | tf_op jit(solution)/shard_map/all_to_all | solution.py:291
  69.5 20.8 %collective-permute-start.5 = (bf16[128,1280]{1,0:T(8,128)(2,1)S(1)}, bf16[128,1280]{1,0:T(8,128)(2,1)S(1)}, u32[]{:S(2)}, u32[]{:S(2)}) collective-permute-start(bf16[128,1280]{1,0:T(8,128)(2,1)S(1)} %copy-done.4), channel_id=1, source_target_pairs={{0,2},{1,3},{2,0},{3,1},{4,6},{5,7},{6,4},{7,5},{8,10},{9,11},{10,... | collective-permute-start | bytes 983048 | tf_op jit(solution)/shard_map/ppermute | solution.py:266
  73.1 17.1 %collective-permute-start.6 = (bf16[128,1280]{1,0:T(8,128)(2,1)S(1)}, bf16[128,1280]{1,0:T(8,128)(2,1)S(1)}, u32[]{:S(2)}, u32[]{:S(2)}) collective-permute-start(bf16[128,1280]{1,0:T(8,128)(2,1)S(1)} %copy-done.3), channel_id=1, source_target_pairs={{0,4},{1,5},{2,6},{3,7},{4,0},{5,1},{6,2},{7,3},{8,12},{9,13},{10,... | collective-permute-start | bytes 983048 | tf_op jit(solution)/shard_map/ppermute | solution.py:266
  77.4 18.0 %collective-permute-start.7 = (bf16[128,1280]{1,0:T(8,128)(2,1)S(1)}, bf16[128,1280]{1,0:T(8,128)(2,1)S(1)}, u32[]{:S(2)}, u32[]{:S(2)}) collective-permute-start(bf16[128,1280]{1,0:T(8,128)(2,1)S(1)} %copy-done.2), channel_id=1, source_target_pairs={{0,6},{1,7},{2,4},{3,5},{4,2},{5,3},{6,0},{7,1},{8,14},{9,15},{10,... | collective-permute-start | bytes 983048 | tf_op jit(solution)/shard_map/ppermute | solution.py:266
  79.4 16.1 %collective-permute-start.8 = (bf16[128,128]{1,0:T(8,128)(2,1)S(1)}, bf16[128,128]{1,0:T(8,128)(2,1)S(1)}, u32[]{:S(2)}, u32[]{:S(2)}) collective-permute-start(bf16[128,128]{1,0:T(8,128)(2,1)S(1)} %get-tuple-element.28), channel_id=1, source_target_pairs={{0,496},{8,504},{16,0},{24,8},{32,16},{40,24},{48,32},{56,40},{64,... | collective-permute-start | bytes 98312 | tf_op jit(solution)/shard_map/ppermute | solution.py:262
  86.2 9.2 %collective-permute-start.9 = (bf16[128,128]{1,0:T(8,128)(2,1)S(1)}, bf16[128,128]{1,0:T(8,128)(2,1)S(1)}, u32[]{:S(2)}, u32[]{:S(2)}) collective-permute-start(bf16[128,128]{1,0:T(8,128)(2,1)S(1)} %get-tuple-element.29), channel_id=1, source_target_pairs={{0,480},{8,488},{16,496},{24,504},{32,0},{40,8},{48,16},{56,24},{6... | collective-permute-start | bytes 98312 | tf_op jit(solution)/shard_map/ppermute | solution.py:262

commit v3 on v2

--- a/solution.py
+++ b/solution.py
@@ -58,8 +58,8 @@
 
 
 def attend_kernel(
-    chunk, tgt_ref, blk_ref, x_ref, own_ref, kv1_ref, kv2_ref, kv3_ref, kv4_ref, mine_ref, theirs_ref,
-    back0, back1, back2, back3, four_ref,
+    chunk, tgt_ref, x_ref, own_ref, kv1_ref, kv2_ref, kv3_ref, kv4_ref, mine_ref, theirs_ref,
+    back0, back1, back2, back3, eight_ref, keep_ref, low_ref, core_ref, both_ref,
     key_ref, value_ref, key_t_ref, value_t_ref, weight_ref, key_acc, value_acc, tile_acc,
 ):
     depth = mine_ref.shape[1]
@@ -126,36 +126,37 @@
             tile_acc[...] = tile_part
         else:
             tile_acc[...] += tile_part
-    core = blk_ref[0] & 1
-    rows_tile = depth // 2
     for half in range(2):
-        turned = tile_acc[half * PAIR : (half + 1) * PAIR, :].T.reshape(-1, 2, chunk, PAIR)
-        for to in range(2):
-            four_ref[2 * to + half, :rows_tile, :] = turned[:, to].reshape(rows_tile, PAIR).astype(BF16)
-        for other in range(2):
-            to = 2 * (core ^ other) + half
-            for slot in range(WIN // 2 + 1):
-                w = 2 * slot + other
-                for part, acc in enumerate((key_acc, value_acc)):
-                    at = pl.ds(rows_tile + (2 * slot + part) * SRC_DEV, SRC_DEV)
-                    if w >= WIN:
-                        four_ref[to, at, :] = zero
-                        continue
-                    first = acc[half, w * SRC_DEV : (w + 1) * SRC_DEV, :]
-                    second = acc[half, WIDTH + w * SRC_DEV : WIDTH + (w + 1) * SRC_DEV, :]
-                    four_ref[to, at, :] = jnp.where(lane < HD, first, second).astype(BF16)
-
-
-def attend(tgt, blk, n_blk, x, kvs, mine, theirs):
+        turned = tile_acc[half * PAIR : (half + 1) * PAIR, :].T.reshape(2, -1, 2, chunk, PAIR)
+        for high in range(2):
+            for core in range(2):
+                eight_ref[4 * high + 2 * core + half] = turned[high, :, core].astype(BF16)
+    for pair, even, odd in ((low, keep_ref, core_ref), (1 - low, low_ref, both_ref)):
+        for w in range(WIN):
+            ref = odd if w % 2 else even
+            for part, acc in enumerate((key_acc, value_acc)):
+                first = acc[pair, w * SRC_DEV : (w + 1) * SRC_DEV, :]
+                second = acc[pair, WIDTH + w * SRC_DEV : WIDTH + (w + 1) * SRC_DEV, :]
+                at = slice(part * SRC_DEV, (part + 1) * SRC_DEV)
+                ref[w // 2, at, :] = jnp.where(lane < HD, first, second).astype(ref.dtype)
+
+
+def attend(tgt, n_blk, x, kvs, mine, theirs):
     _, rows, wide = x.shape
     depth = mine.shape[1]
     flops = 2 * N_Y * rows * (6 * 2 * WIDTH * QUAD + 3 * depth * QUAD)
     return pl.pallas_call(
         functools.partial(attend_kernel, depth // n_blk),
         out_shape=(struct((rows, wide)),) * N_Y
-        + (struct((4, depth // 2 + 2 * (WIN // 2 + 1) * SRC_DEV, PAIR)),),
-        in_specs=[SMEM] * 2 + [VMEM] * 8,
-        out_specs=(VMEM,) * (N_Y + 1),
+        + (
+            struct((8, n_blk // 4, depth // n_blk, PAIR)),
+            struct((3, 2 * SRC_DEV, PAIR), F32),
+            struct((3, 2 * SRC_DEV, PAIR)),
+            struct((2, 2 * SRC_DEV, PAIR)),
+            struct((2, 2 * SRC_DEV, PAIR)),
+        ),
+        in_specs=[SMEM] + [VMEM] * 8,
+        out_specs=(VMEM,) * (N_Y + 5),
         scratch_shapes=[
             pltpu.VMEM((2, 2 * WIDTH, PAIR), BF16),
             pltpu.VMEM((2, 2 * WIDTH, PAIR), BF16),
@@ -171,43 +172,36 @@
         ),
         compiler_params=pltpu.CompilerParams(vmem_limit_bytes=60 * 1024 * 1024),
         name="attend",
-    )(tgt, blk, x, *kvs, mine, theirs)
-
-
-def combine_kernel(blk_ref, four_ref, tile_ref, own_ref, near_ref, far_ref):
-    chips, chunk, _ = tile_ref.shape
-    rows_tile = chips * chunk
-    block = 2 * SRC_DEV
-    core = blk_ref[0] & 1
-    total = four_ref[0, :rows_tile, :].astype(F32)
-    for i in range(1, 4):
-        total = total + four_ref[i, :rows_tile, :].astype(F32)
-    tile_ref[...] = total.astype(BF16).reshape(chips, chunk, PAIR)
-
-    def part(of_core, slot):
-        at = pl.ds(rows_tile + slot * block, block)
-        return four_ref[2 * of_core, at, :].astype(F32) + four_ref[2 * of_core + 1, at, :].astype(F32)
-
-    one, three = part(1 - core, 0), part(1 - core, 1)
+    )(tgt, x, *kvs, mine, theirs)
+
+
+def combine_kernel(blk_ref, eight_ref, keep_ref, low_ref, core_ref, both_ref, tile_ref, own_ref, near_ref, far_ref):
+    total = eight_ref[0].astype(F32)
+    for i in range(1, eight_ref.shape[0]):
+        total = total + eight_ref[i].astype(F32)
+    tile_ref[...] = total.astype(BF16)
+
+    def same(slot):
+        return keep_ref[slot] + low_ref[slot].astype(F32)
+
+    one, three = (core_ref[slot].astype(F32) + both_ref[slot].astype(F32) for slot in range(2))
     zero = jnp.zeros_like(one)
-    first = core == 0
-    own_ref[...] = part(core, 0) + jnp.where(first, one, zero)
-    near_ref[...] = (part(core, 1) + jnp.where(first, three, one)).astype(BF16)
-    far_ref[...] = (part(core, 2) + jnp.where(first, zero, three)).astype(BF16)
-
-
-def combine(blk, n_blk, four):
-    rows_tile = four.shape[1] - 2 * (WIN // 2 + 1) * SRC_DEV
-    chips = n_blk // 2
+    first = (blk_ref[0] & 1) == 0
+    own_ref[...] = same(0) + jnp.where(first, one, zero)
+    near_ref[...] = (same(1) + jnp.where(first, three, one)).astype(BF16)
+    far_ref[...] = (same(2) + jnp.where(first, zero, three)).astype(BF16)
+
+
+def combine(blk, eight, *parts):
     block = (2 * SRC_DEV, PAIR)
     return pl.pallas_call(
         combine_kernel,
-        out_shape=(struct((chips, rows_tile // chips, PAIR)), struct(block, F32), struct(block), struct(block)),
-        in_specs=[SMEM, VMEM],
+        out_shape=(struct(eight.shape[1:]), struct(block, F32), struct(block), struct(block)),
+        in_specs=[SMEM] + [VMEM] * 5,
         out_specs=(VMEM,) * 4,
         compiler_params=pltpu.CompilerParams(vmem_limit_bytes=8 * 1024 * 1024),
         name="combine",
-    )(blk, four)
+    )(blk, eight, *parts)
 
 
 def finish_kernel(tgt_ref, back0, back1, back2, back3, own_ref, near_ref, far_ref, out_ref, query_grad_ref, key_grad_ref, value_grad_ref):
@@ -262,8 +256,10 @@
     return lax.ppermute(value, axis, [(i, (i + steps) % count) for i in range(count)])
 
 
-def flip(value, bits):
-    return lax.ppermute(value, "tgt", [(i, i ^ bits) for i in range(lax.axis_size("tgt"))])
+def flip(value, bits, blk_bits=0):
+    n_tgt = lax.axis_size("tgt")
+    devices = range(lax.axis_size("blk") * n_tgt)
+    return lax.ppermute(value, ("blk", "tgt"), [(i, i ^ (blk_bits * n_tgt + bits)) for i in devices])
 
 
 def local(queries, keys, values, out_weight, out_grad):
@@ -278,18 +274,21 @@
     )
     theirs = flip(out_weight, 1)
     kvs = [own] + [shift(own, "blk", w) for w in range(1, WIN)]
-    *backs, four = attend(tgt, blk, n_blk, x, kvs, out_weight, theirs)
-    fours = [
-        [(2 * chip + core) * n_tgt + 2 * y + low for core in range(2) for low in range(2)]
-        for chip in range(n_blk // 2)
+    *backs, eight, keep, to_low, to_core, to_both = attend(tgt, n_blk, x, kvs, out_weight, theirs)
+    n_z = n_blk // 4
+    eights = [
+        [((high * n_z + z) * 2 + core) * n_tgt + 2 * y + low for high in range(2) for core in range(2) for low in range(2)]
+        for z in range(n_z)
         for y in range(N_Y)
     ]
-    four = lax.all_to_all(four, ("blk", "tgt"), split_axis=0, concat_axis=0, tiled=True, axis_index_groups=fours)
-    backs = [backs[0]] + [flip(backs[s], 2 * s) for s in range(1, N_Y)]
-    tile, own_grad, near, far = combine(blk, n_blk, four)
-    cores = [list(range(core, n_blk, 2)) for core in range(2)]
+    eight = lax.all_to_all(eight, ("blk", "tgt"), split_axis=0, concat_axis=0, tiled=True, axis_index_groups=eights)
+    parts = [keep, flip(to_low, 1), flip(to_core, 0, 1), flip(to_both, 1, 1)]
+    back2 = flip(backs[2], 4)
+    backs = [backs[0], flip(backs[1], 2), back2, flip(backs[3], 6)]
+    tile, own_grad, near, far = combine(blk, eight, *parts)
+    lines = [[(high * n_z + z) * 2 + core for z in range(n_z)] for high in range(2) for core in range(2)]
     tiles = lax.all_to_all(
-        tile, "blk", split_axis=0, concat_axis=0, tiled=True, axis_index_groups=cores
+        tile, "blk", split_axis=0, concat_axis=0, tiled=True, axis_index_groups=lines
     )
     near, far = shift(near, "blk", -2), shift(far, "blk", -4)
     outputs, query_grad, key_grad, value_grad = finish(tgt, backs, own_grad, near, far)

time: 97.6 us -> 95 us (0.973)
  the two profiles are of different devices: /device:TPU:1 before, /device:TPU:24 now
where the time goes in v3:
time: 95 us; the launch traced here: 94.2 us
  starting transfers between devices  67.2 us (71%)
  waiting for transfers between devices  11.8 us (12%)
  Pallas kernels  11.7 us (12%)
  local copies, waits for them, and re-layouts  2.71 us (3%)
    ppermute x6, starting transfers between devices, shift(): lax.ppermute(value, axis, [(i, (i + steps) % count) for i in range(count)])  25.6 us
    ppermute x7, starting transfers between devices, flip(): lax.ppermute(value, ('blk', 'tgt'), [(i, i ^ blk_bits * n_tgt + bits) for...  20.2 us
    all_to_all x1, starting transfers between devices, local(): lax.all_to_all(send, 'tgt', split_axis=0, concat_axis=0, tiled=True, axis...  9.21 us
    all_to_all x1, starting transfers between devices, local(): lax.all_to_all(tile, 'blk', split_axis=0, concat_axis=0, tiled=True, axis...  7.98 us
    ppermute x6, waiting for transfers between devices, shift(): lax.ppermute(value, axis, [(i, (i + steps) % count) for i in range(count)])  7.75 us
    pallas_call x1, Pallas kernels, attend(): pl.pallas_call(functools.partial(attend_kernel, depth // n_blk), out_shap...  7.13 us
    all_to_all x1, starting transfers between devices, local(): lax.all_to_all(eight, ('blk', 'tgt'), split_axis=0, concat_axis=0, tiled=...  4.15 us
    ppermute x7, waiting for transfers between devices, flip(): lax.ppermute(value, ('blk', 'tgt'), [(i, i ^ blk_bits * n_tgt + bits) for...  4.03 us
  transfers between devices with their start and end apart: 16, of which 5 were waited for; matrix products, arithmetic and copies ran while one was open for 0% of the time, Pallas kernels for 2%

profile of v3, /device:TPU:24, one launch (start us, length us, event | category | flops | bytes accessed | tf_op | source)
XLA Modules:
  0.0 94.2 jit_solution(11021310163298552415)
XLA Ops:
  0.6 2.3 %pack.1 = (bf16[64,512]{1,0:T(8,128)(2,1)}, bf16[4,128,1280]{2,1,0:T(8,128)(2,1)}) custom-call(s32[1]{0:T(128)} %bitcast.tgt_ref, bf16[128,1024]{1,0:T(8,128)(2,1)} %query_ref.1, bf16[64,1024]{1,0:T(8,128)(2,1)} %key_ref.1, bf16[64,1024]{1,0:T(8,128)(2,1)} %value_ref.1, bf16[128,1024]{1,0:T(8,128)(2,1)} %out_grad_ref.1), custom_call_target="tpu_custom_call" | custom-call | tf_op jit(solution)/shard_map/pack/pallas_call | solution.py:50
  3.0 0.0 copy-start.3
  3.0 9.2 %all-to-all-start = ((bf16[4,128,1280]{2,1,0:T(8,128)(2,1)}), bf16[4,128,1280]{2,1,0:T(8,128)(2,1)S(1)}, u32[]{:S(2)}, u32[]{:S(2)}) async-start(bf16[4,128,1280]{2,1,0:T(8,128)(2,1)} %get-tuple-element.24), calls=%async_computation | async-start | bytes 2621440 | tf_op jit(solution)/shard_map/all_to_all | solution.py:272
  12.2 0.0 copy-done.3
  12.2 1.9 %collective-permute-start.4 = (bf16[128,1024]{1,0:T(8,128)(2,1)S(1)}, bf16[128,1024]{1,0:T(8,128)(2,1)S(1)}, u32[]{:S(2)}, u32[]{:S(2)}) collective-permute-start(bf16[128,1024]{1,0:T(8,128)(2,1)S(1)} %copy-done.3), channel_id=1, source_target_pairs={{0,1},{1,0},{2,3},{3,2},{4,5},{5,4},{6,7},{7,6},{8,9},{9,8},{10,11... | collective-permute-start | bytes 786440 | tf_op jit(solution)/shard_map/ppermute | solution.py:262
  14.1 0.0 copy-done.5
  14.1 2.3 %collective-permute-start.3 = (bf16[64,512]{1,0:T(8,128)(2,1)S(1)}, bf16[64,512]{1,0:T(8,128)(2,1)S(1)}, u32[]{:S(2)}, u32[]{:S(2)}) collective-permute-start(bf16[64,512]{1,0:T(8,128)(2,1)S(1)} %copy-done.5), channel_id=1, source_target_pairs={{0,32},{8,40},{16,48},{24,56},{32,64},{40,72},{48,80},{56,88},{64,... | collective-permute-start | bytes 196616 | tf_op jit(solution)/shard_map/ppermute | solution.py:256
  16.4 2.1 %collective-permute-start.2 = (bf16[64,512]{1,0:T(8,128)(2,1)S(1)}, bf16[64,512]{1,0:T(8,128)(2,1)S(1)}, u32[]{:S(2)}, u32[]{:S(2)}) collective-permute-start(bf16[64,512]{1,0:T(8,128)(2,1)S(1)} %copy-done.5), channel_id=1, source_target_pairs={{0,24},{8,32},{16,40},{24,48},{32,56},{40,64},{48,72},{56,80},{64,... | collective-permute-start | bytes 196616 | tf_op jit(solution)/shard_map/ppermute | solution.py:256
  18.5 5.0 %collective-permute-start.1 = (bf16[64,512]{1,0:T(8,128)(2,1)S(1)}, bf16[64,512]{1,0:T(8,128)(2,1)S(1)}, u32[]{:S(2)}, u32[]{:S(2)}) collective-permute-start(bf16[64,512]{1,0:T(8,128)(2,1)S(1)} %copy-done.5), channel_id=1, source_target_pairs={{0,16},{8,24},{16,32},{24,40},{32,48},{40,56},{48,64},{56,72},{64,... | collective-permute-start | bytes 196616 | tf_op jit(solution)/shard_map/ppermute | solution.py:256
  23.6 4.8 %collective-permute-start = (bf16[64,512]{1,0:T(8,128)(2,1)S(1)}, bf16[64,512]{1,0:T(8,128)(2,1)S(1)}, u32[]{:S(2)}, u32[]{:S(2)}) collective-permute-start(bf16[64,512]{1,0:T(8,128)(2,1)S(1)} %copy-done.5), channel_id=1, source_target_pairs={{0,8},{8,16},{16,24},{24,32},{32,40},{40,48},{48,56},{56,64},{64,7... | collective-permute-start | bytes 196616 | tf_op jit(solution)/shard_map/ppermute | solution.py:256
  28.4 1.1 %collective-permute-done.3.kv4_ref = bf16[64,512]{1,0:T(8,128)(2,1)S(1)} collective-permute-done((bf16[64,512]{1,0:T(8,128)(2,1)S(1)}, bf16[64,512]{1,0:T(8,128)(2,1)S(1)}, u32[]{:S(2)}, u32[]{:S(2)}) %collective-permute-start.3) | collective-permute-done | bytes 65568 | tf_op jit(solution)/shard_map/ppermute | solution.py:256
  29.5 0.0 collective-permute-done.2.kv3_ref
  29.5 1.4 %collective-permute-done.1.kv2_ref = bf16[64,512]{1,0:T(8,128)(2,1)S(1)} collective-permute-done((bf16[64,512]{1,0:T(8,128)(2,1)S(1)}, bf16[64,512]{1,0:T(8,128)(2,1)S(1)}, u32[]{:S(2)}, u32[]{:S(2)}) %collective-permute-start.1) | collective-permute-done | bytes 65568 | tf_op jit(solution)/shard_map/ppermute | solution.py:256
  30.9 2.8 %collective-permute-done.kv1_ref = bf16[64,512]{1,0:T(8,128)(2,1)S(1)} collective-permute-done((bf16[64,512]{1,0:T(8,128)(2,1)S(1)}, bf16[64,512]{1,0:T(8,128)(2,1)S(1)}, u32[]{:S(2)}, u32[]{:S(2)}) %collective-permute-start) | collective-permute-done | bytes 65568 | tf_op jit(solution)/shard_map/ppermute | solution.py:256
  33.6 0.0 collective-permute-done.4.theirs_ref
  33.6 0.0 all-to-all-done.x_ref
  33.7 0.0 copy-done.6
  33.7 0.0 copy-done.7
  33.7 0.0 copy-done.8
  33.7 0.6 copy-done.9
  34.3 0.1 copy-done.4
  34.4 1.1 %copy-done.2 = bf16[4,128,1280]{2,1,0:T(8,128)(2,1)} copy-done((bf16[4,128,1280]{2,1,0:T(8,128)(2,1)}, bf16[4,128,1280]{2,1,0:T(8,128)(2,1)S(1)}, u32[]{:S(2)}) %copy-start.2) | copy-done | bytes 1310744
  35.4 7.1 %attend.1 = (bf16[128,1280]{1,0:T(8,128)(2,1)}, bf16[128,1280]{1,0:T(8,128)(2,1)}, bf16[128,1280]{1,0:T(8,128)(2,1)}, bf16[128,1280]{1,0:T(8,128)(2,1)}, bf16[8,...) custom-call(s32[1]{0:T(128)} %bitcast.tgt_ref, ...), custom_call_target="tpu_custom_call" | custom-call | flops 1811939328 | bytes 2621440 | tf_op jit(solution)/shard_map/attend/pallas_call | solution.py:148
  42.6 4.2 %all-to-all-start.1 = ((bf16[8,16,16,128]{3,2,1,0:T(8,128)(2,1)}), bf16[8,16,16,128]{3,2,1,0:T(8,128)(2,1)S(1)}, u32[]{:S(2)}, u32[]{:S(2)}) async-start(bf16[8,16,16,128]{3,2,1,0:T(8,128)(2,1)} %get-tuple-element.30), calls=%async_computation.1 | async-start | bytes 1048576 | tf_op jit(solution)/shard_map/all_to_all | solution.py:284
  46.7 2.4 %collective-permute-start.9 = (bf16[2,128,128]{2,1,0:T(8,128)(2,1)}, bf16[2,128,128]{2,1,0:T(8,128)(2,1)S(1)}, u32[]{:S(2)}, u32[]{:S(2)}) collective-permute-start(bf16[2,128,128]{2,1,0:T(8,128)(2,1)} %get-tuple-element.33), channel_id=1, source_target_pairs={{0,8},{1,9},{2,10},{3,11},{4,12},{5,13},{6,14},{7,15},{8,0},{9,1},... | collective-permute-start | bytes 196616 | tf_op jit(solution)/shard_map/ppermute | solution.py:262
  49.1 3.5 %collective-permute-start.8 = (bf16[3,128,128]{2,1,0:T(8,128)(2,1)}, bf16[3,128,128]{2,1,0:T(8,128)(2,1)S(1)}, u32[]{:S(2)}, u32[]{:S(2)}) collective-permute-start(bf16[3,128,128]{2,1,0:T(8,128)(2,1)} %get-tuple-element.32), channel_id=1, source_target_pairs={{0,1},{1,0},{2,3},{3,2},{4,5},{5,4},{6,7},{7,6},{8,9},{9,8},{10,11... | collective-permute-start | bytes 294920 | tf_op jit(solution)/shard_map/ppermute | solution.py:262
  52.7 2.8 %collective-permute-start.5 = (bf16[128,1280]{1,0:T(8,128)(2,1)}, bf16[128,1280]{1,0:T(8,128)(2,1)S(1)}, u32[]{:S(2)}, u32[]{:S(2)}) collective-permute-start(bf16[128,1280]{1,0:T(8,128)(2,1)} %get-tuple-element.27), channel_id=1, source_target_pairs={{0,2},{1,3},{2,0},{3,1},{4,6},{5,7},{6,4},{7,5},{8,10},{9,11},{10,... | collective-permute-start | bytes 983048 | tf_op jit(solution)/shard_map/ppermute | solution.py:262
  55.5 2.5 %collective-permute-start.6 = (bf16[128,1280]{1,0:T(8,128)(2,1)}, bf16[128,1280]{1,0:T(8,128)(2,1)S(1)}, u32[]{:S(2)}, u32[]{:S(2)}) collective-permute-start(bf16[128,1280]{1,0:T(8,128)(2,1)} %get-tuple-element.28), channel_id=1, source_target_pairs={{0,4},{1,5},{2,6},{3,7},{4,0},{5,1},{6,2},{7,3},{8,12},{9,13},{10,... | collective-permute-start | bytes 983048 | tf_op jit(solution)/shard_map/ppermute | solution.py:262
  58.0 5.1 %collective-permute-start.7 = (bf16[128,1280]{1,0:T(8,128)(2,1)}, bf16[128,1280]{1,0:T(8,128)(2,1)S(1)}, u32[]{:S(2)}, u32[]{:S(2)}) collective-permute-start(bf16[128,1280]{1,0:T(8,128)(2,1)} %get-tuple-element.29), channel_id=1, source_target_pairs={{0,6},{1,7},{2,4},{3,5},{4,2},{5,3},{6,0},{7,1},{8,14},{9,15},{10,... | collective-permute-start | bytes 983048 | tf_op jit(solution)/shard_map/ppermute | solution.py:262
  63.1 0.0 collective-permute-done.9.core_ref
  63.1 1.9 %collective-permute-start.10 = (bf16[2,128,128]{2,1,0:T(8,128)(2,1)}, bf16[2,128,128]{2,1,0:T(8,128)(2,1)S(1)}, u32[]{:S(2)}, u32[]{:S(2)}) collective-permute-start(bf16[2,128,128]{2,1,0:T(8,128)(2,1)} %get-tuple-element.34), channel_id=1, source_target_pairs={{0,9},{1,8},{2,11},{3,10},{4,13},{5,12},{6,15},{7,14},{8,1},{9,0},... | collective-permute-start | bytes 196616 | tf_op jit(solution)/shard_map/ppermute | solution.py:262
  65.1 4.0 %collective-permute-done.10.both_ref = bf16[2,128,128]{2,1,0:T(8,128)(2,1)S(1)} collective-permute-done((bf16[2,128,128]{2,1,0:T(8,128)(2,1)}, bf16[2,128,128]{2,1,0:T(8,128)(2,1)S(1)}, u32[]{:S(2)}, u32[]{:S(2)}) %collective-permute-start.10) | collective-permute-done | bytes 65568 | tf_op jit(solution)/shard_map/ppermute | solution.py:262
  69.1 0.0 collective-permute-done.8.low_ref
  69.1 0.0 all-to-all-done.1.eight_ref
  69.1 0.9 copy-done.1
  70.0 0.7 combine.1
  70.7 8.0 %all-to-all-start.2 = ((bf16[16,16,128]{2,1,0:T(8,128)(2,1)}), bf16[16,16,128]{2,1,0:T(8,128)(2,1)S(1)}, u32[]{:S(2)}, u32[]{:S(2)}) async-start(bf16[16,16,128]{2,1,0:T(8,128)(2,1)} %get-tuple-element.42), calls=%async_computation.2 | async-start | bytes 131072 | tf_op jit(solution)/shard_map/all_to_all | solution.py:290
  78.7 7.2 %collective-permute-start.11 = (bf16[128,128]{1,0:T(8,128)(2,1)S(1)}, bf16[128,128]{1,0:T(8,128)(2,1)S(1)}, u32[]{:S(2)}, u32[]{:S(2)}) collective-permute-start(bf16[128,128]{1,0:T(8,128)(2,1)S(1)} %get-tuple-element.36), channel_id=1, source_target_pairs={{0,496},{8,504},{16,0},{24,8},{32,16},{40,24},{48,32},{56,40},{64,... | collective-permute-start | bytes 98312 | tf_op jit(solution)/shard_map/ppermute | solution.py:256
  85.9 4.3 %collective-permute-start.12 = (bf16[128,128]{1,0:T(8,128)(2,1)S(1)}, bf16[128,128]{1,0:T(8,128)(2,1)S(1)}, u32[]{:S(2)}, u32[]{:S(2)}) collective-permute-start(bf16[128,128]{1,0:T(8,128)(2,1)S(1)} %get-tuple-element.37), channel_id=1, source_target_pairs={{0,480},{8,488},{16,496},{24,504},{32,0},{40,8},{48,16},{56,24},{6... | collective-permute-start | bytes 98312 | tf_op jit(solution)/shard_map/ppermute | solution.py:256
  90.2 0.0 collective-permute-done.5.back1
  90.2 0.0 collective-permute-done.6.back2
  90.2 0.0 collective-permute-done.7.back3
  90.2 0.0 collective-permute-done.11.near_ref
  90.2 2.5 %collective-permute-done.12.far_ref = bf16[128,128]{1,0:T(8,128)(2,1)S(1)} collective-permute-done((bf16[128,128]{1,0:T(8,128)(2,1)S(1)}, bf16[128,128]{1,0:T(8,128)(2,1)S(1)}, u32[]{:S(2)}, u32[]{:S(2)}) %collective-permute-start.12) | collective-permute-done | bytes 32800 | tf_op jit(solution)/shard_map/ppermute | solution.py:256
  92.7 0.0 copy-done
  92.7 0.9 finish.1
  93.6 0.0 all-to-all-done.2.part_ref
  93.6 0.6 total.1
  (9 shorter events, 0.0 us)
Async XLA Ops:
  3.0 9.2 %copy-start.3 = (bf16[128,1024]{1,0:T(8,128)(2,1)S(1)}, bf16[128,1024]{1,0:T(8,128)(2,1)}, u32[]{:S(2)}) copy-start(bf16[128,1024]{1,0:T(8,128)(2,1)} %mine_ref.1) | copy-start | bytes 786436
  3.0 11.1 %copy-start.5 = (bf16[64,512]{1,0:T(8,128)(2,1)S(1)}, bf16[64,512]{1,0:T(8,128)(2,1)}, u32[]{:S(2)}) copy-start(bf16[64,512]{1,0:T(8,128)(2,1)} %get-tuple-element.25.own_ref) | copy-start | bytes 196612
  3.0 30.7 %all-to-all-start = ((bf16[4,128,1280]{2,1,0:T(8,128)(2,1)}), bf16[4,128,1280]{2,1,0:T(8,128)(2,1)S(1)}, u32[]{:S(2)}, u32[]{:S(2)}) async-start(bf16[4,128,1280]{2,1,0:T(8,128)(2,1)} %get-tuple-element.24), calls=%async_computation | async-start | bytes 2621440 | tf_op jit(solution)/shard_map/all_to_all | solution.py:272
  12.2 21.5 %collective-permute-start.4 = (bf16[128,1024]{1,0:T(8,128)(2,1)S(1)}, bf16[128,1024]{1,0:T(8,128)(2,1)S(1)}, u32[]{:S(2)}, u32[]{:S(2)}) collective-permute-start(bf16[128,1024]{1,0:T(8,128)(2,1)S(1)} %copy-done.3), channel_id=1, source_target_pairs={{0,1},{1,0},{2,3},{3,2},{4,5},{5,4},{6,7},{7,6},{8,9},{9,8},{10,11... | collective-permute-start | bytes 786440 | tf_op jit(solution)/shard_map/ppermute | solution.py:262
  14.1 15.4 %collective-permute-start.3 = (bf16[64,512]{1,0:T(8,128)(2,1)S(1)}, bf16[64,512]{1,0:T(8,128)(2,1)S(1)}, u32[]{:S(2)}, u32[]{:S(2)}) collective-permute-start(bf16[64,512]{1,0:T(8,128)(2,1)S(1)} %copy-done.5), channel_id=1, source_target_pairs={{0,32},{8,40},{16,48},{24,56},{32,64},{40,72},{48,80},{56,88},{64,... | collective-permute-start | bytes 196616 | tf_op jit(solution)/shard_map/ppermute | solution.py:256
  16.4 13.1 %collective-permute-start.2 = (bf16[64,512]{1,0:T(8,128)(2,1)S(1)}, bf16[64,512]{1,0:T(8,128)(2,1)S(1)}, u32[]{:S(2)}, u32[]{:S(2)}) collective-permute-start(bf16[64,512]{1,0:T(8,128)(2,1)S(1)} %copy-done.5), channel_id=1, source_target_pairs={{0,24},{8,32},{16,40},{24,48},{32,56},{40,64},{48,72},{56,80},{64,... | collective-permute-start | bytes 196616 | tf_op jit(solution)/shard_map/ppermute | solution.py:256
  18.5 12.3 %collective-permute-start.1 = (bf16[64,512]{1,0:T(8,128)(2,1)S(1)}, bf16[64,512]{1,0:T(8,128)(2,1)S(1)}, u32[]{:S(2)}, u32[]{:S(2)}) collective-permute-start(bf16[64,512]{1,0:T(8,128)(2,1)S(1)} %copy-done.5), channel_id=1, source_target_pairs={{0,16},{8,24},{16,32},{24,40},{32,48},{40,56},{48,64},{56,72},{64,... | collective-permute-start | bytes 196616 | tf_op jit(solution)/shard_map/ppermute | solution.py:256
  23.6 10.0 %collective-permute-start = (bf16[64,512]{1,0:T(8,128)(2,1)S(1)}, bf16[64,512]{1,0:T(8,128)(2,1)S(1)}, u32[]{:S(2)}, u32[]{:S(2)}) collective-permute-start(bf16[64,512]{1,0:T(8,128)(2,1)S(1)} %copy-done.5), channel_id=1, source_target_pairs={{0,8},{8,16},{16,24},{24,32},{32,40},{40,48},{48,56},{56,64},{64,7... | collective-permute-start | bytes 196616 | tf_op jit(solution)/shard_map/ppermute | solution.py:256
  29.5 4.2 %copy-start.6 = (bf16[64,512]{1,0:T(8,128)(2,1)}, bf16[64,512]{1,0:T(8,128)(2,1)S(1)}, u32[]{:S(2)}) copy-start(bf16[64,512]{1,0:T(8,128)(2,1)S(1)} %collective-permute-done.3.kv4_ref) | copy-start | bytes 196612
  29.5 4.2 %copy-start.7 = (bf16[64,512]{1,0:T(8,128)(2,1)}, bf16[64,512]{1,0:T(8,128)(2,1)S(1)}, u32[]{:S(2)}) copy-start(bf16[64,512]{1,0:T(8,128)(2,1)S(1)} %collective-permute-done.2.kv3_ref) | copy-start | bytes 196612
  30.9 2.8 %copy-start.8 = (bf16[64,512]{1,0:T(8,128)(2,1)}, bf16[64,512]{1,0:T(8,128)(2,1)S(1)}, u32[]{:S(2)}) copy-start(bf16[64,512]{1,0:T(8,128)(2,1)S(1)} %collective-permute-done.1.kv2_ref) | copy-start | bytes 196612
  33.6 0.6 copy-start.9
  33.6 0.7 copy-start.4
  34.4 1.1 %copy-start.2 = (bf16[4,128,1280]{2,1,0:T(8,128)(2,1)}, bf16[4,128,1280]{2,1,0:T(8,128)(2,1)S(1)}, u32[]{:S(2)}) copy-start(bf16[4,128,1280]{2,1,0:T(8,128)(2,1)S(1)} %all-to-all-done.x_ref) | copy-start | bytes 3932164
  42.6 50.1 %copy-start = (bf16[128,1280]{1,0:T(8,128)(2,1)S(1)}, bf16[128,1280]{1,0:T(8,128)(2,1)}, u32[]{:S(2)}) copy-start(bf16[128,1280]{1,0:T(8,128)(2,1)} %get-tuple-element.26.back0) | copy-start | bytes 983044
  42.6 26.5 %all-to-all-start.1 = ((bf16[8,16,16,128]{3,2,1,0:T(8,128)(2,1)}), bf16[8,16,16,128]{3,2,1,0:T(8,128)(2,1)S(1)}, u32[]{:S(2)}, u32[]{:S(2)}) async-start(bf16[8,16,16,128]{3,2,1,0:T(8,128)(2,1)} %get-tuple-element.30), calls=%async_computation.1 | async-start | bytes 1048576 | tf_op jit(solution)/shard_map/all_to_all | solution.py:284
  46.7 16.4 %collective-permute-start.9 = (bf16[2,128,128]{2,1,0:T(8,128)(2,1)}, bf16[2,128,128]{2,1,0:T(8,128)(2,1)S(1)}, u32[]{:S(2)}, u32[]{:S(2)}) collective-permute-start(bf16[2,128,128]{2,1,0:T(8,128)(2,1)} %get-tuple-element.33), channel_id=1, source_target_pairs={{0,8},{1,9},{2,10},{3,11},{4,12},{5,13},{6,14},{7,15},{8,0},{9,1},... | collective-permute-start | bytes 196616 | tf_op jit(solution)/shard_map/ppermute | solution.py:262
  49.1 20.0 %collective-permute-start.8 = (bf16[3,128,128]{2,1,0:T(8,128)(2,1)}, bf16[3,128,128]{2,1,0:T(8,128)(2,1)S(1)}, u32[]{:S(2)}, u32[]{:S(2)}) collective-permute-start(bf16[3,128,128]{2,1,0:T(8,128)(2,1)} %get-tuple-element.32), channel_id=1, source_target_pairs={{0,1},{1,0},{2,3},{3,2},{4,5},{5,4},{6,7},{7,6},{8,9},{9,8},{10,11... | collective-permute-start | bytes 294920 | tf_op jit(solution)/shard_map/ppermute | solution.py:262
  52.7 37.5 %collective-permute-start.5 = (bf16[128,1280]{1,0:T(8,128)(2,1)}, bf16[128,1280]{1,0:T(8,128)(2,1)S(1)}, u32[]{:S(2)}, u32[]{:S(2)}) collective-permute-start(bf16[128,1280]{1,0:T(8,128)(2,1)} %get-tuple-element.27), channel_id=1, source_target_pairs={{0,2},{1,3},{2,0},{3,1},{4,6},{5,7},{6,4},{7,5},{8,10},{9,11},{10,... | collective-permute-start | bytes 983048 | tf_op jit(solution)/shard_map/ppermute | solution.py:262
  55.5 34.7 %collective-permute-start.6 = (bf16[128,1280]{1,0:T(8,128)(2,1)}, bf16[128,1280]{1,0:T(8,128)(2,1)S(1)}, u32[]{:S(2)}, u32[]{:S(2)}) collective-permute-start(bf16[128,1280]{1,0:T(8,128)(2,1)} %get-tuple-element.28), channel_id=1, source_target_pairs={{0,4},{1,5},{2,6},{3,7},{4,0},{5,1},{6,2},{7,3},{8,12},{9,13},{10,... | collective-permute-start | bytes 983048 | tf_op jit(solution)/shard_map/ppermute | solution.py:262
  58.0 32.2 %collective-permute-start.7 = (bf16[128,1280]{1,0:T(8,128)(2,1)}, bf16[128,1280]{1,0:T(8,128)(2,1)S(1)}, u32[]{:S(2)}, u32[]{:S(2)}) collective-permute-start(bf16[128,1280]{1,0:T(8,128)(2,1)} %get-tuple-element.29), channel_id=1, source_target_pairs={{0,6},{1,7},{2,4},{3,5},{4,2},{5,3},{6,0},{7,1},{8,14},{9,15},{10,... | collective-permute-start | bytes 983048 | tf_op jit(solution)/shard_map/ppermute | solution.py:262
  63.1 6.0 %collective-permute-start.10 = (bf16[2,128,128]{2,1,0:T(8,128)(2,1)}, bf16[2,128,128]{2,1,0:T(8,128)(2,1)S(1)}, u32[]{:S(2)}, u32[]{:S(2)}) collective-permute-start(bf16[2,128,128]{2,1,0:T(8,128)(2,1)} %get-tuple-element.34), channel_id=1, source_target_pairs={{0,9},{1,8},{2,11},{3,10},{4,13},{5,12},{6,15},{7,14},{8,1},{9,0},... | collective-permute-start | bytes 196616 | tf_op jit(solution)/shard_map/ppermute | solution.py:262
  69.1 0.9 copy-start.1
  70.7 22.9 %all-to-all-start.2 = ((bf16[16,16,128]{2,1,0:T(8,128)(2,1)}), bf16[16,16,128]{2,1,0:T(8,128)(2,1)S(1)}, u32[]{:S(2)}, u32[]{:S(2)}) async-start(bf16[16,16,128]{2,1,0:T(8,128)(2,1)} %get-tuple-element.42), calls=%async_computation.2 | async-start | bytes 131072 | tf_op jit(solution)/shard_map/all_to_all | solution.py:290
  78.7 11.5 %collective-permute-start.11 = (bf16[128,128]{1,0:T(8,128)(2,1)S(1)}, bf16[128,128]{1,0:T(8,128)(2,1)S(1)}, u32[]{:S(2)}, u32[]{:S(2)}) collective-permute-start(bf16[128,128]{1,0:T(8,128)(2,1)S(1)} %get-tuple-element.36), channel_id=1, source_target_pairs={{0,496},{8,504},{16,0},{24,8},{32,16},{40,24},{48,32},{56,40},{64,... | collective-permute-start | bytes 98312 | tf_op jit(solution)/shard_map/ppermute | solution.py:256
  85.9 6.8 %collective-permute-start.12 = (bf16[128,128]{1,0:T(8,128)(2,1)S(1)}, bf16[128,128]{1,0:T(8,128)(2,1)S(1)}, u32[]{:S(2)}, u32[]{:S(2)}) collective-permute-start(bf16[128,128]{1,0:T(8,128)(2,1)S(1)} %get-tuple-element.37), channel_id=1, source_target_pairs={{0,480},{8,488},{16,496},{24,504},{32,0},{40,8},{48,16},{56,24},{6... | collective-permute-start | bytes 98312 | tf_op jit(solution)/shard_map/ppermute | solution.py:256

commit v4 on v2

--- a/solution.py
+++ b/solution.py
@@ -58,7 +58,7 @@
 
 
 def attend_kernel(
-    chunk, tgt_ref, blk_ref, x_ref, own_ref, kv1_ref, kv2_ref, kv3_ref, kv4_ref, mine_ref, theirs_ref,
+    chunk, tgt_ref, blk_ref, x_ref, own_ref, mate_ref, kept_ref, low_ref, core_ref, both_ref, mine_ref, theirs_ref,
     back0, back1, back2, back3, four_ref,
     key_ref, value_ref, key_t_ref, value_t_ref, weight_ref, key_acc, value_acc, tile_acc,
 ):
@@ -69,10 +69,20 @@
     zero = jnp.zeros((SRC_DEV, PAIR), BF16)
     weight_ref[pl.ds(pl.multiple_of(low * PAIR, PAIR), PAIR), :] = mine_ref[...]
     weight_ref[pl.ds(pl.multiple_of((1 - low) * PAIR, PAIR), PAIR), :] = theirs_ref[...]
+    is_low, first = low == 0, (blk_ref[0] & 1) == 0
+    kept, other_low, other_core, both = kept_ref[...], low_ref[...], core_ref[...], both_ref[...]
+    near = jnp.where(is_low, other_core, both)
+    blocks = (
+        own_ref[...],
+        jnp.where(first, near, mate_ref[...]),
+        jnp.where(is_low, kept, other_low),
+        jnp.where(first, jnp.where(is_low, both, other_core), near),
+        jnp.where(is_low, other_low, kept),
+    )
     for pair in range(2):
-        for w, ref in enumerate((own_ref, kv1_ref, kv2_ref, kv3_ref, kv4_ref)):
-            block_key = ref[:, pair * PAIR : (pair + 1) * PAIR]
-            block_value = ref[:, QUAD + pair * PAIR : QUAD + (pair + 1) * PAIR]
+        for w, block in enumerate(blocks):
+            block_key = block[:, pair * PAIR : (pair + 1) * PAIR]
+            block_value = block[:, QUAD + pair * PAIR : QUAD + (pair + 1) * PAIR]
             for head in range(2):
                 own_lanes = (lane < HD) if head == 0 else (lane >= HD)
                 at = pl.ds(head * WIDTH + w * SRC_DEV, SRC_DEV)
@@ -154,7 +164,7 @@
         functools.partial(attend_kernel, depth // n_blk),
         out_shape=(struct((rows, wide)),) * N_Y
         + (struct((4, depth // 2 + 2 * (WIN // 2 + 1) * SRC_DEV, PAIR)),),
-        in_specs=[SMEM] * 2 + [VMEM] * 8,
+        in_specs=[SMEM] * 2 + [VMEM] * 9,
         out_specs=(VMEM,) * (N_Y + 1),
         scratch_shapes=[
             pltpu.VMEM((2, 2 * WIDTH, PAIR), BF16),
@@ -262,8 +272,18 @@
     return lax.ppermute(value, axis, [(i, (i + steps) % count) for i in range(count)])
 
 
-def flip(value, bits):
-    return lax.ppermute(value, "tgt", [(i, i ^ bits) for i in range(lax.axis_size("tgt"))])
+def flip(value, bits, blk_bits=0):
+    n_tgt = lax.axis_size("tgt")
+    devices = range(lax.axis_size("blk") * n_tgt)
+    return lax.ppermute(value, ("blk", "tgt"), [(i, i ^ (blk_bits * n_tgt + bits)) for i in devices])
+
+
+def fetch(value):
+    n_tgt, n_blk = lax.axis_size("tgt"), lax.axis_size("blk")
+    pairs = [
+        (b * n_tgt + t, (b + 2 + 2 * (t & 1)) % n_blk * n_tgt + t) for b in range(n_blk) for t in range(n_tgt)
+    ]
+    return lax.ppermute(value, ("blk", "tgt"), pairs)
 
 
 def local(queries, keys, values, out_weight, out_grad):
@@ -276,8 +296,10 @@
     x = lax.all_to_all(
         send, "tgt", split_axis=0, concat_axis=0, tiled=True, axis_index_groups=groups
     )
+    kept = fetch(own)
     theirs = flip(out_weight, 1)
-    kvs = [own] + [shift(own, "blk", w) for w in range(1, WIN)]
+    mate = flip(own, 0, 1)
+    kvs = [own, mate, kept, flip(kept, 1), flip(kept, 0, 1), flip(kept, 1, 1)]
     *backs, four = attend(tgt, blk, n_blk, x, kvs, out_weight, theirs)
     fours = [
         [(2 * chip + core) * n_tgt + 2 * y + low for core in range(2) for low in range(2)]

time: 97.6 us -> 102 us (1.045)
  waiting for transfers between devices: 8.37 us -> 14.6 us
  starting transfers between devices: 57 us -> 55.9 us
    ppermute x6 -> x2, starting transfers between devices: 28.7 us -> 10.8 us  [shift(): lax.ppermute(value, axis, [(i, (i + steps) % count) for i in range(count)])]
    ppermute x4 -> x9, starting transfers between devices: 13 us -> 30.1 us  [the longest x8 26.5 us: flip(): lax.ppermute(value, ('blk', 'tgt'), [(i, i ^ blk_bits * n_tgt + bits) for...]
    ppermute x4 -> x9, waiting for transfers between devices: 5.24 us -> 14.6 us  [the longest x8 7.74 us: flip(): lax.ppermute(value, ('blk', 'tgt'), [(i, i ^ blk_bits * n_tgt + bits) for...]
    ppermute x6 -> x2, waiting for transfers between devices: 3.12 us -> 0.01 us  [shift(): lax.ppermute(value, axis, [(i, (i + steps) % count) for i in range(count)])]
  transfers between devices with their start and end apart: 12 -> 13, of which waited for: 3 -> 3; matrix products, arithmetic and copies ran while one was open for 0% -> 0% of each run, Pallas kernels for 1% -> 1%
where the time goes in v4:
time: 102 us; the launch traced here: 101 us
  starting transfers between devices  55.9 us (55%)
  blocking collectives  17.2 us (17%)
  waiting for transfers between devices  14.6 us (14%)
  Pallas kernels  11.5 us (11%)
  local copies, waits for them, and re-layouts  1.17 us (1%)
    ppermute x8, starting transfers between devices, flip(): lax.ppermute(value, ('blk', 'tgt'), [(i, i ^ blk_bits * n_tgt + bits) for...  26.5 us
    all_to_all x1, blocking collectives, local(): lax.all_to_all(four, ('blk', 'tgt'), split_axis=0, concat_axis=0, tiled=T...  17.2 us
    ppermute x2, starting transfers between devices, shift(): lax.ppermute(value, axis, [(i, (i + steps) % count) for i in range(count)])  10.8 us
    all_to_all x1, starting transfers between devices, local(): lax.all_to_all(tile, 'blk', split_axis=0, concat_axis=0, tiled=True, axis...  9.85 us
    ppermute x8, waiting for transfers between devices, flip(): lax.ppermute(value, ('blk', 'tgt'), [(i, i ^ blk_bits * n_tgt + bits) for...  7.74 us
    ppermute x1, waiting for transfers between devices, fetch(): return lax.ppermute(value, ('blk', 'tgt'), pairs)  6.89 us
    pallas_call x1, Pallas kernels, attend(): pl.pallas_call(functools.partial(attend_kernel, depth // n_blk), out_shap...  6.88 us
    all_to_all x1, starting transfers between devices, local(): lax.all_to_all(send, 'tgt', split_axis=0, concat_axis=0, tiled=True, axis...  5.14 us
  transfers between devices with their start and end apart: 13, of which 3 were waited for; matrix products, arithmetic and copies ran while one was open for 0% of the time, Pallas kernels for 1%

profile of v4, /device:TPU:1, one launch (start us, length us, event | category | flops | bytes accessed | tf_op | source)
XLA Modules:
  0.0 101.3 jit_solution(1707946085680406127)
XLA Ops:
  0.6 2.3 %pack.1 = (bf16[64,512]{1,0:T(8,128)(2,1)}, bf16[4,128,1280]{2,1,0:T(8,128)(2,1)}) custom-call(s32[1]{0:T(128)} %bitcast.tgt_ref, bf16[128,1024]{1,0:T(8,128)(2,1)} %query_ref.1, bf16[64,1024]{1,0:T(8,128)(2,1)} %key_ref.1, bf16[64,1024]{1,0:T(8,128)(2,1)} %value_ref.1, bf16[128,1024]{1,0:T(8,128)(2,1)} %out_grad_ref.1), custom_call_target="tpu_custom_call" | custom-call | tf_op jit(solution)/shard_map/pack/pallas_call | solution.py:50
  3.0 5.1 %all-to-all-start = ((bf16[4,128,1280]{2,1,0:T(8,128)(2,1)}), bf16[4,128,1280]{2,1,0:T(8,128)(2,1)S(1)}, u32[]{:S(2)}, u32[]{:S(2)}) async-start(bf16[4,128,1280]{2,1,0:T(8,128)(2,1)} %get-tuple-element.20), calls=%async_computation | async-start | bytes 2621440 | tf_op jit(solution)/shard_map/all_to_all | solution.py:296
  8.1 0.0 copy-done.5
  8.1 3.1 %collective-permute-start.5 = (bf16[128,1024]{1,0:T(8,128)(2,1)S(1)}, bf16[128,1024]{1,0:T(8,128)(2,1)S(1)}, u32[]{:S(2)}, u32[]{:S(2)}) collective-permute-start(bf16[128,1024]{1,0:T(8,128)(2,1)S(1)} %copy-done.5), channel_id=1, source_target_pairs={{0,1},{1,0},{2,3},{3,2},{4,5},{5,4},{6,7},{7,6},{8,9},{9,8},{10,11... | collective-permute-start | bytes 786440 | tf_op jit(solution)/shard_map/ppermute | solution.py:278
  11.2 0.0 copy-done.7
  11.2 3.5 %collective-permute-start.1 = (bf16[64,512]{1,0:T(8,128)(2,1)S(1)}, bf16[64,512]{1,0:T(8,128)(2,1)S(1)}, u32[]{:S(2)}, u32[]{:S(2)}) collective-permute-start(bf16[64,512]{1,0:T(8,128)(2,1)S(1)} %copy-done.7), channel_id=1, source_target_pairs={{0,16},{1,33},{2,18},{3,35},{4,20},{5,37},{6,22},{7,39},{8,24},{9,... | collective-permute-start | bytes 196616 | tf_op jit(solution)/shard_map/ppermute | solution.py:286
  14.8 4.5 %collective-permute-start = (bf16[64,512]{1,0:T(8,128)(2,1)S(1)}, bf16[64,512]{1,0:T(8,128)(2,1)S(1)}, u32[]{:S(2)}, u32[]{:S(2)}) collective-permute-start(bf16[64,512]{1,0:T(8,128)(2,1)S(1)} %copy-done.7), channel_id=1, source_target_pairs={{0,8},{1,9},{2,10},{3,11},{4,12},{5,13},{6,14},{7,15},{8,0},{9,1},... | collective-permute-start | bytes 196616 | tf_op jit(solution)/shard_map/ppermute | solution.py:278
  19.3 6.9 %collective-permute-done.1.kept_ref = bf16[64,512]{1,0:T(8,128)(2,1)S(1)} collective-permute-done((bf16[64,512]{1,0:T(8,128)(2,1)S(1)}, bf16[64,512]{1,0:T(8,128)(2,1)S(1)}, u32[]{:S(2)}, u32[]{:S(2)}) %collective-permute-start.1) | collective-permute-done | bytes 65568 | tf_op jit(solution)/shard_map/ppermute | solution.py:286
  26.2 4.8 %collective-permute-start.4 = (bf16[64,512]{1,0:T(8,128)(2,1)S(1)}, bf16[64,512]{1,0:T(8,128)(2,1)S(1)}, u32[]{:S(2)}, u32[]{:S(2)}) collective-permute-start(bf16[64,512]{1,0:T(8,128)(2,1)S(1)} %collective-permute-done.1.kept_ref), channel_id=1, source_target_pairs={{0,9},{1,8},{2,11},{3,10},{4,13},{5,12},{6,15},{7,14},{8,1},{9,0},... | collective-permute-start | bytes 196616 | tf_op jit(solution)/shard_map/ppermute | solution.py:278
  31.0 1.9 %collective-permute-start.3 = (bf16[64,512]{1,0:T(8,128)(2,1)S(1)}, bf16[64,512]{1,0:T(8,128)(2,1)S(1)}, u32[]{:S(2)}, u32[]{:S(2)}) collective-permute-start(bf16[64,512]{1,0:T(8,128)(2,1)S(1)} %collective-permute-done.1.kept_ref), channel_id=1, source_target_pairs={{0,8},{1,9},{2,10},{3,11},{4,12},{5,13},{6,14},{7,15},{8,0},{9,1},... | collective-permute-start | bytes 196616 | tf_op jit(solution)/shard_map/ppermute | solution.py:278
  32.9 2.4 %collective-permute-start.2 = (bf16[64,512]{1,0:T(8,128)(2,1)S(1)}, bf16[64,512]{1,0:T(8,128)(2,1)S(1)}, u32[]{:S(2)}, u32[]{:S(2)}) collective-permute-start(bf16[64,512]{1,0:T(8,128)(2,1)S(1)} %collective-permute-done.1.kept_ref), channel_id=1, source_target_pairs={{0,1},{1,0},{2,3},{3,2},{4,5},{5,4},{6,7},{7,6},{8,9},{9,8},{10,11... | collective-permute-start | bytes 196616 | tf_op jit(solution)/shard_map/ppermute | solution.py:278
  35.4 0.0 collective-permute-done.mate_ref
  35.4 0.0 copy-start.9
  35.4 0.0 collective-permute-done.4.both_ref
  35.4 0.0 copy-start.10
  35.4 0.0 collective-permute-done.3.core_ref
  35.4 0.0 copy-start.11
  35.5 2.5 %collective-permute-done.2.low_ref = bf16[64,512]{1,0:T(8,128)(2,1)S(1)} collective-permute-done((bf16[64,512]{1,0:T(8,128)(2,1)S(1)}, bf16[64,512]{1,0:T(8,128)(2,1)S(1)}, u32[]{:S(2)}, u32[]{:S(2)}) %collective-permute-start.2) | collective-permute-done | bytes 65568 | tf_op jit(solution)/shard_map/ppermute | solution.py:278
  38.0 0.0 collective-permute-done.5.theirs_ref
  38.0 0.0 all-to-all-done.x_ref
  38.0 0.0 copy-start.1
  38.0 0.0 copy-done.8
  38.0 0.0 copy-done.9
  38.0 0.0 copy-done.10
  38.0 0.0 copy-done.11
  38.0 0.6 copy-done.12
  38.6 0.1 copy-done.6
  38.7 0.5 copy-done.1
  39.1 6.9 %attend.1 = (bf16[128,1280]{1,0:T(8,128)(2,1)}, bf16[128,1280]{1,0:T(8,128)(2,1)}, bf16[128,1280]{1,0:T(8,128)(2,1)}, bf16[128,1280]{1,0:T(8,128)(2,1)}, bf16[4,896,128]{2,1,0:T(8,128)(2,1)}) custom-call(s32[1]{0:T(128)} %bitcast.tgt_ref, s32[1]{0:T(128)} %bitcast.1.blk_ref, bf16[4,128,1280]{2,1,0:T(8,128)(2,1)} %copy-done.1, ...), custom_call_target="tpu_custom_call" | custom-call | flops 1811939328 | bytes 2621440 | tf_op jit(solution)/shard_map/attend/pallas_call | solution.py:163
  46.0 0.0 copy-start
  46.0 17.2 %all_to_all.15.four_ref = bf16[4,896,128]{2,1,0:T(8,128)(2,1)S(1)} all-to-all(bf16[4,896,128]{2,1,0:T(8,128)(2,1)} %get-tuple-element.26), channel_id=1, replica_groups={{0,1,8,9},{2,3,10,11},{4,5,12,13},{6,7,14,15},{16,17,24,25},{18,19,26,2..., dimensions={0} | all-to-all | bytes 1835008 | tf_op jit(solution)/shard_map/all_to_all | solution.py:309
  63.3 0.7 combine.1
  64.0 9.8 %all-to-all-start.2 = ((bf16[32,16,128]{2,1,0:T(8,128)(2,1)}), bf16[32,16,128]{2,1,0:T(8,128)(2,1)S(1)}, u32[]{:S(2)}, u32[]{:S(2)}) async-start(bf16[32,16,128]{2,1,0:T(8,128)(2,1)} %get-tuple-element.34), calls=%async_computation.2 | async-start | bytes 262144 | tf_op jit(solution)/shard_map/all_to_all | solution.py:313
  73.9 0.0 copy-done.4
  73.9 3.5 %collective-permute-start.6 = (bf16[128,1280]{1,0:T(8,128)(2,1)S(1)}, bf16[128,1280]{1,0:T(8,128)(2,1)S(1)}, u32[]{:S(2)}, u32[]{:S(2)}) collective-permute-start(bf16[128,1280]{1,0:T(8,128)(2,1)S(1)} %copy-done.4), channel_id=1, source_target_pairs={{0,2},{1,3},{2,0},{3,1},{4,6},{5,7},{6,4},{7,5},{8,10},{9,11},{10,... | collective-permute-start | bytes 983048 | tf_op jit(solution)/shard_map/ppermute | solution.py:278
  77.4 4.3 %collective-permute-start.7 = (bf16[128,1280]{1,0:T(8,128)(2,1)S(1)}, bf16[128,1280]{1,0:T(8,128)(2,1)S(1)}, u32[]{:S(2)}, u32[]{:S(2)}) collective-permute-start(bf16[128,1280]{1,0:T(8,128)(2,1)S(1)} %copy-done.3), channel_id=1, source_target_pairs={{0,4},{1,5},{2,6},{3,7},{4,0},{5,1},{6,2},{7,3},{8,12},{9,13},{10,... | collective-permute-start | bytes 983048 | tf_op jit(solution)/shard_map/ppermute | solution.py:278
  81.7 0.0 copy-done.2
  81.7 1.9 %collective-permute-start.8 = (bf16[128,1280]{1,0:T(8,128)(2,1)S(1)}, bf16[128,1280]{1,0:T(8,128)(2,1)S(1)}, u32[]{:S(2)}, u32[]{:S(2)}) collective-permute-start(bf16[128,1280]{1,0:T(8,128)(2,1)S(1)} %copy-done.2), channel_id=1, source_target_pairs={{0,6},{1,7},{2,4},{3,5},{4,2},{5,3},{6,0},{7,1},{8,14},{9,15},{10,... | collective-permute-start | bytes 983048 | tf_op jit(solution)/shard_map/ppermute | solution.py:278
  83.6 6.8 %collective-permute-start.9 = (bf16[128,128]{1,0:T(8,128)(2,1)S(1)}, bf16[128,128]{1,0:T(8,128)(2,1)S(1)}, u32[]{:S(2)}, u32[]{:S(2)}) collective-permute-start(bf16[128,128]{1,0:T(8,128)(2,1)S(1)} %get-tuple-element.28), channel_id=1, source_target_pairs={{0,496},{8,504},{16,0},{24,8},{32,16},{40,24},{48,32},{56,40},{64,... | collective-permute-start | bytes 98312 | tf_op jit(solution)/shard_map/ppermute | solution.py:272
  90.5 4.0 %collective-permute-start.10 = (bf16[128,128]{1,0:T(8,128)(2,1)S(1)}, bf16[128,128]{1,0:T(8,128)(2,1)S(1)}, u32[]{:S(2)}, u32[]{:S(2)}) collective-permute-start(bf16[128,128]{1,0:T(8,128)(2,1)S(1)} %get-tuple-element.29), channel_id=1, source_target_pairs={{0,480},{8,488},{16,496},{24,504},{32,0},{40,8},{48,16},{56,24},{6... | collective-permute-start | bytes 98312 | tf_op jit(solution)/shard_map/ppermute | solution.py:272
  94.5 0.0 collective-permute-done.6.back1
  94.5 0.0 collective-permute-done.7.back2
  94.5 5.2 %collective-permute-done.8.back3 = bf16[128,1280]{1,0:T(8,128)(2,1)S(1)} collective-permute-done((bf16[128,1280]{1,0:T(8,128)(2,1)S(1)}, bf16[128,1280]{1,0:T(8,128)(2,1)S(1)}, u32[]{:S(2)}, u32[]{:S(2)}) %collective-permute-start.8) | collective-permute-done | bytes 327712 | tf_op jit(solution)/shard_map/ppermute | solution.py:278
  99.7 0.0 collective-permute-done.9.near_ref
  99.7 0.0 collective-permute-done.10.far_ref
  99.8 0.9 finish.1
  100.6 0.0 all-to-all-done.2.part_ref
  100.6 0.6 total.1
  (10 shorter events, 0.0 us)
Async XLA Ops:
  3.0 5.1 %copy-start.5 = (bf16[128,1024]{1,0:T(8,128)(2,1)S(1)}, bf16[128,1024]{1,0:T(8,128)(2,1)}, u32[]{:S(2)}) copy-start(bf16[128,1024]{1,0:T(8,128)(2,1)} %mine_ref.1) | copy-start | bytes 786436
  3.0 8.3 %copy-start.7 = (bf16[64,512]{1,0:T(8,128)(2,1)S(1)}, bf16[64,512]{1,0:T(8,128)(2,1)}, u32[]{:S(2)}) copy-start(bf16[64,512]{1,0:T(8,128)(2,1)} %get-tuple-element.21.own_ref) | copy-start | bytes 196612
  3.0 35.0 %all-to-all-start = ((bf16[4,128,1280]{2,1,0:T(8,128)(2,1)}), bf16[4,128,1280]{2,1,0:T(8,128)(2,1)S(1)}, u32[]{:S(2)}, u32[]{:S(2)}) async-start(bf16[4,128,1280]{2,1,0:T(8,128)(2,1)} %get-tuple-element.20), calls=%async_computation | async-start | bytes 2621440 | tf_op jit(solution)/shard_map/all_to_all | solution.py:296
  8.1 29.8 %collective-permute-start.5 = (bf16[128,1024]{1,0:T(8,128)(2,1)S(1)}, bf16[128,1024]{1,0:T(8,128)(2,1)S(1)}, u32[]{:S(2)}, u32[]{:S(2)}) collective-permute-start(bf16[128,1024]{1,0:T(8,128)(2,1)S(1)} %copy-done.5), channel_id=1, source_target_pairs={{0,1},{1,0},{2,3},{3,2},{4,5},{5,4},{6,7},{7,6},{8,9},{9,8},{10,11... | collective-permute-start | bytes 786440 | tf_op jit(solution)/shard_map/ppermute | solution.py:278
  11.2 14.9 %collective-permute-start.1 = (bf16[64,512]{1,0:T(8,128)(2,1)S(1)}, bf16[64,512]{1,0:T(8,128)(2,1)S(1)}, u32[]{:S(2)}, u32[]{:S(2)}) collective-permute-start(bf16[64,512]{1,0:T(8,128)(2,1)S(1)} %copy-done.7), channel_id=1, source_target_pairs={{0,16},{1,33},{2,18},{3,35},{4,20},{5,37},{6,22},{7,39},{8,24},{9,... | collective-permute-start | bytes 196616 | tf_op jit(solution)/shard_map/ppermute | solution.py:286
  14.8 20.6 %collective-permute-start = (bf16[64,512]{1,0:T(8,128)(2,1)S(1)}, bf16[64,512]{1,0:T(8,128)(2,1)S(1)}, u32[]{:S(2)}, u32[]{:S(2)}) collective-permute-start(bf16[64,512]{1,0:T(8,128)(2,1)S(1)} %copy-done.7), channel_id=1, source_target_pairs={{0,8},{1,9},{2,10},{3,11},{4,12},{5,13},{6,14},{7,15},{8,0},{9,1},... | collective-permute-start | bytes 196616 | tf_op jit(solution)/shard_map/ppermute | solution.py:278
  26.2 11.8 %copy-start.8 = (bf16[64,512]{1,0:T(8,128)(2,1)}, bf16[64,512]{1,0:T(8,128)(2,1)S(1)}, u32[]{:S(2)}) copy-start(bf16[64,512]{1,0:T(8,128)(2,1)S(1)} %collective-permute-done.1.kept_ref) | copy-start | bytes 196612
  26.2 9.2 %collective-permute-start.4 = (bf16[64,512]{1,0:T(8,128)(2,1)S(1)}, bf16[64,512]{1,0:T(8,128)(2,1)S(1)}, u32[]{:S(2)}, u32[]{:S(2)}) collective-permute-start(bf16[64,512]{1,0:T(8,128)(2,1)S(1)} %collective-permute-done.1.kept_ref), channel_id=1, source_target_pairs={{0,9},{1,8},{2,11},{3,10},{4,13},{5,12},{6,15},{7,14},{8,1},{9,0},... | collective-permute-start | bytes 196616 | tf_op jit(solution)/shard_map/ppermute | solution.py:278
  31.0 4.4 %collective-permute-start.3 = (bf16[64,512]{1,0:T(8,128)(2,1)S(1)}, bf16[64,512]{1,0:T(8,128)(2,1)S(1)}, u32[]{:S(2)}, u32[]{:S(2)}) collective-permute-start(bf16[64,512]{1,0:T(8,128)(2,1)S(1)} %collective-permute-done.1.kept_ref), channel_id=1, source_target_pairs={{0,8},{1,9},{2,10},{3,11},{4,12},{5,13},{6,14},{7,15},{8,0},{9,1},... | collective-permute-start | bytes 196616 | tf_op jit(solution)/shard_map/ppermute | solution.py:278
  32.9 5.0 %collective-permute-start.2 = (bf16[64,512]{1,0:T(8,128)(2,1)S(1)}, bf16[64,512]{1,0:T(8,128)(2,1)S(1)}, u32[]{:S(2)}, u32[]{:S(2)}) collective-permute-start(bf16[64,512]{1,0:T(8,128)(2,1)S(1)} %collective-permute-done.1.kept_ref), channel_id=1, source_target_pairs={{0,1},{1,0},{2,3},{3,2},{4,5},{5,4},{6,7},{7,6},{8,9},{9,8},{10,11... | collective-permute-start | bytes 196616 | tf_op jit(solution)/shard_map/ppermute | solution.py:278
  35.4 2.6 %copy-start.9 = (bf16[64,512]{1,0:T(8,128)(2,1)}, bf16[64,512]{1,0:T(8,128)(2,1)S(1)}, u32[]{:S(2)}) copy-start(bf16[64,512]{1,0:T(8,128)(2,1)S(1)} %collective-permute-done.mate_ref) | copy-start | bytes 196612
  35.4 2.6 %copy-start.10 = (bf16[64,512]{1,0:T(8,128)(2,1)}, bf16[64,512]{1,0:T(8,128)(2,1)S(1)}, u32[]{:S(2)}) copy-start(bf16[64,512]{1,0:T(8,128)(2,1)S(1)} %collective-permute-done.4.both_ref) | copy-start | bytes 196612
  35.4 2.6 %copy-start.11 = (bf16[64,512]{1,0:T(8,128)(2,1)}, bf16[64,512]{1,0:T(8,128)(2,1)S(1)}, u32[]{:S(2)}) copy-start(bf16[64,512]{1,0:T(8,128)(2,1)S(1)} %collective-permute-done.3.core_ref) | copy-start | bytes 196612
  38.0 0.6 copy-start.12
  38.0 0.7 copy-start.6
  38.0 1.2 %copy-start.1 = (bf16[4,128,1280]{2,1,0:T(8,128)(2,1)}, bf16[4,128,1280]{2,1,0:T(8,128)(2,1)S(1)}, u32[]{:S(2)}) copy-start(bf16[4,128,1280]{2,1,0:T(8,128)(2,1)S(1)} %all-to-all-done.x_ref) | copy-start | bytes 3932164
  46.0 27.8 %copy-start.4 = (bf16[128,1280]{1,0:T(8,128)(2,1)S(1)}, bf16[128,1280]{1,0:T(8,128)(2,1)}, u32[]{:S(2)}) copy-start(bf16[128,1280]{1,0:T(8,128)(2,1)} %get-tuple-element.23) | copy-start | bytes 983044
  46.0 31.4 %copy-start.3 = (bf16[128,1280]{1,0:T(8,128)(2,1)S(1)}, bf16[128,1280]{1,0:T(8,128)(2,1)}, u32[]{:S(2)}) copy-start(bf16[128,1280]{1,0:T(8,128)(2,1)} %get-tuple-element.24) | copy-start | bytes 983044
  46.0 35.7 %copy-start.2 = (bf16[128,1280]{1,0:T(8,128)(2,1)S(1)}, bf16[128,1280]{1,0:T(8,128)(2,1)}, u32[]{:S(2)}) copy-start(bf16[128,1280]{1,0:T(8,128)(2,1)} %get-tuple-element.25) | copy-start | bytes 983044
  46.0 53.7 %copy-start = (bf16[128,1280]{1,0:T(8,128)(2,1)S(1)}, bf16[128,1280]{1,0:T(8,128)(2,1)}, u32[]{:S(2)}) copy-start(bf16[128,1280]{1,0:T(8,128)(2,1)} %get-tuple-element.22.back0) | copy-start | bytes 983044
  64.0 36.6 %all-to-all-start.2 = ((bf16[32,16,128]{2,1,0:T(8,128)(2,1)}), bf16[32,16,128]{2,1,0:T(8,128)(2,1)S(1)}, u32[]{:S(2)}, u32[]{:S(2)}) async-start(bf16[32,16,128]{2,1,0:T(8,128)(2,1)} %get-tuple-element.34), calls=%async_computation.2 | async-start | bytes 262144 | tf_op jit(solution)/shard_map/all_to_all | solution.py:313
  73.9 20.6 %collective-permute-start.6 = (bf16[128,1280]{1,0:T(8,128)(2,1)S(1)}, bf16[128,1280]{1,0:T(8,128)(2,1)S(1)}, u32[]{:S(2)}, u32[]{:S(2)}) collective-permute-start(bf16[128,1280]{1,0:T(8,128)(2,1)S(1)} %copy-done.4), channel_id=1, source_target_pairs={{0,2},{1,3},{2,0},{3,1},{4,6},{5,7},{6,4},{7,5},{8,10},{9,11},{10,... | collective-permute-start | bytes 983048 | tf_op jit(solution)/shard_map/ppermute | solution.py:278
  77.4 17.1 %collective-permute-start.7 = (bf16[128,1280]{1,0:T(8,128)(2,1)S(1)}, bf16[128,1280]{1,0:T(8,128)(2,1)S(1)}, u32[]{:S(2)}, u32[]{:S(2)}) collective-permute-start(bf16[128,1280]{1,0:T(8,128)(2,1)S(1)} %copy-done.3), channel_id=1, source_target_pairs={{0,4},{1,5},{2,6},{3,7},{4,0},{5,1},{6,2},{7,3},{8,12},{9,13},{10,... | collective-permute-start | bytes 983048 | tf_op jit(solution)/shard_map/ppermute | solution.py:278
  81.7 18.0 %collective-permute-start.8 = (bf16[128,1280]{1,0:T(8,128)(2,1)S(1)}, bf16[128,1280]{1,0:T(8,128)(2,1)S(1)}, u32[]{:S(2)}, u32[]{:S(2)}) collective-permute-start(bf16[128,1280]{1,0:T(8,128)(2,1)S(1)} %copy-done.2), channel_id=1, source_target_pairs={{0,6},{1,7},{2,4},{3,5},{4,2},{5,3},{6,0},{7,1},{8,14},{9,15},{10,... | collective-permute-start | bytes 983048 | tf_op jit(solution)/shard_map/ppermute | solution.py:278
  83.6 16.1 %collective-permute-start.9 = (bf16[128,128]{1,0:T(8,128)(2,1)S(1)}, bf16[128,128]{1,0:T(8,128)(2,1)S(1)}, u32[]{:S(2)}, u32[]{:S(2)}) collective-permute-start(bf16[128,128]{1,0:T(8,128)(2,1)S(1)} %get-tuple-element.28), channel_id=1, source_target_pairs={{0,496},{8,504},{16,0},{24,8},{32,16},{40,24},{48,32},{56,40},{64,... | collective-permute-start | bytes 98312 | tf_op jit(solution)/shard_map/ppermute | solution.py:272
  90.5 9.2 %collective-permute-start.10 = (bf16[128,128]{1,0:T(8,128)(2,1)S(1)}, bf16[128,128]{1,0:T(8,128)(2,1)S(1)}, u32[]{:S(2)}, u32[]{:S(2)}) collective-permute-start(bf16[128,128]{1,0:T(8,128)(2,1)S(1)} %get-tuple-element.29), channel_id=1, source_target_pairs={{0,480},{8,488},{16,496},{24,504},{32,0},{40,8},{48,16},{56,24},{6... | collective-permute-start | bytes 98312 | tf_op jit(solution)/shard_map/ppermute | solution.py:272

commit v5 on v2

--- a/solution.py
+++ b/solution.py
@@ -35,23 +35,50 @@
     return jax.ShapeDtypeStruct(shape, dtype)
 
 
-def pack_kernel(tgt_ref, query_ref, key_ref, value_ref, out_grad_ref, own_ref, send_ref):
-    depth = out_grad_ref.shape[1]
+def pack_kernel(tgt_ref, query_ref, key_ref, value_ref, out_grad_ref, own_ref, send_ref, grad_buf, query_buf, block_buf, sems):
+    depth = grad_buf.shape[1]
     mine = pl.ds(pl.multiple_of((tgt_ref[0] >> 1) * QUAD, QUAD), QUAD)
-    own_ref[:, :QUAD] = key_ref[:, mine]
-    own_ref[:, QUAD:] = value_ref[:, mine]
-    for i in range(N_Y):
-        send_ref[i, :, :depth] = out_grad_ref[...]
-        send_ref[i, :, depth:] = query_ref[:, i * QUAD : (i + 1) * QUAD]
+    ins = [
+        pltpu.make_async_copy(out_grad_ref, grad_buf, sems.at[0]),
+        pltpu.make_async_copy(query_ref, query_buf, sems.at[1]),
+        pltpu.make_async_copy(key_ref.at[:, mine], block_buf.at[:, :QUAD], sems.at[2]),
+        pltpu.make_async_copy(value_ref.at[:, mine], block_buf.at[:, QUAD:], sems.at[3]),
+    ]
+    for copy in ins:
+        copy.start()
+    ins[0].wait()
+    outs = [pltpu.make_async_copy(grad_buf, send_ref.at[i, :, :depth], sems.at[4 + i]) for i in range(N_Y)]
+    for copy in outs:
+        copy.start()
+    ins[1].wait()
+    more = [
+        pltpu.make_async_copy(query_buf.at[:, i * QUAD : (i + 1) * QUAD], send_ref.at[i, :, depth:], sems.at[8 + i])
+        for i in range(N_Y)
+    ]
+    for copy in more:
+        copy.start()
+    ins[2].wait()
+    ins[3].wait()
+    last = pltpu.make_async_copy(block_buf, own_ref, sems.at[12])
+    last.start()
+    for copy in outs + more + [last]:
+        copy.wait()
 
 
 def pack(tgt, queries, keys, values, out_grad):
     rows, depth = queries.shape
+    anywhere = pl.BlockSpec(memory_space=pl.ANY)
     return pl.pallas_call(
         pack_kernel,
         out_shape=(struct((SRC_DEV, 2 * QUAD)), struct((N_Y, rows, depth + QUAD))),
-        in_specs=[SMEM] + [VMEM] * 4,
-        out_specs=(VMEM,) * 2,
+        in_specs=[SMEM] + [anywhere] * 4,
+        out_specs=(anywhere,) * 2,
+        scratch_shapes=[
+            pltpu.VMEM((rows, depth), BF16),
+            pltpu.VMEM((rows, depth), BF16),
+            pltpu.VMEM((SRC_DEV, 2 * QUAD), BF16),
+            pltpu.SemaphoreType.DMA((13,)),
+        ],
         compiler_params=pltpu.CompilerParams(vmem_limit_bytes=60 * 1024 * 1024),
         name="pack",
     )(tgt, queries, keys, values, out_grad)
@@ -169,7 +196,7 @@
         cost_estimate=pl.CostEstimate(
             flops=flops, bytes_accessed=4 * N_Y * rows * wide, transcendentals=4 * WIDTH * N_Y * rows
         ),
-        compiler_params=pltpu.CompilerParams(vmem_limit_bytes=60 * 1024 * 1024),
+        compiler_params=pltpu.CompilerParams(vmem_limit_bytes=32 * 1024 * 1024),
         name="attend",
     )(tgt, blk, x, *kvs, mine, theirs)
 

time: 97.6 us -> 92.5 us (0.948)
  Pallas kernels: 11.4 us -> 8.68 us
  blocking collectives: 18.2 us -> 17 us
  local copies, waits for them, and re-layouts: 1.18 us -> 0.01 us
    pallas_call x1, Pallas kernels: 6.84 us -> 4.25 us  [attend(): pl.pallas_call(functools.partial(attend_kernel, depth // n_blk), out_shap...]
    all_to_all x1, blocking collectives: 18.2 us -> 17 us  [local(): lax.all_to_all(four, ('blk', 'tgt'), split_axis=0, concat_axis=0, tiled=T...]
    unnamed x24 -> x4, local copies, waits for them, and re-layouts: 1.18 us -> 0.01 us
where the time goes in v5:
time: 92.5 us; the launch traced here: 91.9 us
  starting transfers between devices  57 us (62%)
  blocking collectives  17 us (18%)
  Pallas kernels  8.68 us (9%)
  waiting for transfers between devices  8.4 us (9%)
    ppermute x6, starting transfers between devices, shift(): lax.ppermute(value, axis, [(i, (i + steps) % count) for i in range(count)])  28.7 us
    all_to_all x1, blocking collectives, local(): lax.all_to_all(four, ('blk', 'tgt'), split_axis=0, concat_axis=0, tiled=T...  17 us
    ppermute x4, starting transfers between devices, flip(): lax.ppermute(value, 'tgt', [(i, i ^ bits) for i in range(lax.axis_size('t...  13 us
    all_to_all x1, starting transfers between devices, local(): lax.all_to_all(tile, 'blk', split_axis=0, concat_axis=0, tiled=True, axis...  10.2 us
    ppermute x4, waiting for transfers between devices, flip(): lax.ppermute(value, 'tgt', [(i, i ^ bits) for i in range(lax.axis_size('t...  5.26 us
    all_to_all x1, starting transfers between devices, local(): lax.all_to_all(send, 'tgt', split_axis=0, concat_axis=0, tiled=True, axis...  5.14 us
    pallas_call x1, Pallas kernels, attend(): pl.pallas_call(functools.partial(attend_kernel, depth // n_blk), out_shap...  4.25 us
    ppermute x6, waiting for transfers between devices, shift(): lax.ppermute(value, axis, [(i, (i + steps) % count) for i in range(count)])  3.14 us
  transfers between devices with their start and end apart: 12, of which 3 were waited for; matrix products, arithmetic and copies ran while one was open for 0% of the time, Pallas kernels for 1%

profile of v5, /device:TPU:1, one launch (start us, length us, event | category | flops | bytes accessed | tf_op | source)
XLA Modules:
  0.0 91.9 jit_solution(685948067662705114)
XLA Ops:
  0.6 2.2 %pack.1 = (bf16[64,512]{1,0:T(8,128)(2,1)}, bf16[4,128,1280]{2,1,0:T(8,128)(2,1)}) custom-call(s32[1]{0:T(128)} %bitcast.tgt_ref, bf16[128,1024]{1,0:T(8,128)(2,1)} %query_ref.1, bf16[64,1024]{1,0:T(8,128)(2,1)} %key_ref.1, bf16[64,1024]{1,0:T(8,128)(2,1)} %value_ref.1, bf16[128,1024]{1,0:T(8,128)(2,1)} %out_grad_ref.1), custom_call_target="tpu_custom_call" | custom-call | tf_op jit(solution)/shard_map/pack/pallas_call | solution.py:71
  2.8 0.0 copy-start
  2.9 0.0 copy-start.1
  2.9 5.1 %all-to-all-start = ((bf16[4,128,1280]{2,1,0:T(8,128)(2,1)}), bf16[4,128,1280]{2,1,0:T(8,128)(2,1)S(1)}, u32[]{:S(2)}, u32[]{:S(2)}) async-start(bf16[4,128,1280]{2,1,0:T(8,128)(2,1)} %get-tuple-element.20), calls=%async_computation | async-start | bytes 2621440 | tf_op jit(solution)/shard_map/all_to_all | solution.py:303
  8.0 0.0 copy-done
  8.0 3.1 %collective-permute-start.4 = (bf16[128,1024]{1,0:T(8,128)(2,1)S(1)}, bf16[128,1024]{1,0:T(8,128)(2,1)S(1)}, u32[]{:S(2)}, u32[]{:S(2)}) collective-permute-start(bf16[128,1024]{1,0:T(8,128)(2,1)S(1)} %copy-done), channel_id=1, source_target_pairs={{0,1},{1,0},{2,3},{3,2},{4,5},{5,4},{6,7},{7,6},{8,9},{9,8},{10,11... | collective-permute-start | bytes 786440 | tf_op jit(solution)/shard_map/ppermute | solution.py:293
  11.1 0.0 copy-done.1
  11.1 4.9 %collective-permute-start.3 = (bf16[64,512]{1,0:T(8,128)(2,1)S(1)}, bf16[64,512]{1,0:T(8,128)(2,1)S(1)}, u32[]{:S(2)}, u32[]{:S(2)}) collective-permute-start(bf16[64,512]{1,0:T(8,128)(2,1)S(1)} %copy-done.1), channel_id=1, source_target_pairs={{0,32},{8,40},{16,48},{24,56},{32,64},{40,72},{48,80},{56,88},{64,... | collective-permute-start | bytes 196616 | tf_op jit(solution)/shard_map/ppermute | solution.py:289
  16.0 7.5 %collective-permute-start.2 = (bf16[64,512]{1,0:T(8,128)(2,1)S(1)}, bf16[64,512]{1,0:T(8,128)(2,1)S(1)}, u32[]{:S(2)}, u32[]{:S(2)}) collective-permute-start(bf16[64,512]{1,0:T(8,128)(2,1)S(1)} %copy-done.1), channel_id=1, source_target_pairs={{0,24},{8,32},{16,40},{24,48},{32,56},{40,64},{48,72},{56,80},{64,... | collective-permute-start | bytes 196616 | tf_op jit(solution)/shard_map/ppermute | solution.py:289
  23.6 3.5 %collective-permute-start.1 = (bf16[64,512]{1,0:T(8,128)(2,1)S(1)}, bf16[64,512]{1,0:T(8,128)(2,1)S(1)}, u32[]{:S(2)}, u32[]{:S(2)}) collective-permute-start(bf16[64,512]{1,0:T(8,128)(2,1)S(1)} %copy-done.1), channel_id=1, source_target_pairs={{0,16},{8,24},{16,32},{24,40},{32,48},{40,56},{48,64},{56,72},{64,... | collective-permute-start | bytes 196616 | tf_op jit(solution)/shard_map/ppermute | solution.py:289
  27.1 1.9 %collective-permute-start = (bf16[64,512]{1,0:T(8,128)(2,1)S(1)}, bf16[64,512]{1,0:T(8,128)(2,1)S(1)}, u32[]{:S(2)}, u32[]{:S(2)}) collective-permute-start(bf16[64,512]{1,0:T(8,128)(2,1)S(1)} %copy-done.1), channel_id=1, source_target_pairs={{0,8},{8,16},{16,24},{24,32},{32,40},{40,48},{48,56},{56,64},{64,7... | collective-permute-start | bytes 196616 | tf_op jit(solution)/shard_map/ppermute | solution.py:289
  29.0 0.0 collective-permute-done.3.kv4_ref
  29.1 1.5 %collective-permute-done.2.kv3_ref = bf16[64,512]{1,0:T(8,128)(2,1)S(1)} collective-permute-done((bf16[64,512]{1,0:T(8,128)(2,1)S(1)}, bf16[64,512]{1,0:T(8,128)(2,1)S(1)}, u32[]{:S(2)}, u32[]{:S(2)}) %collective-permute-start.2) | collective-permute-done | bytes 65568 | tf_op jit(solution)/shard_map/ppermute | solution.py:289
  30.5 1.7 %collective-permute-done.1.kv2_ref = bf16[64,512]{1,0:T(8,128)(2,1)S(1)} collective-permute-done((bf16[64,512]{1,0:T(8,128)(2,1)S(1)}, bf16[64,512]{1,0:T(8,128)(2,1)S(1)}, u32[]{:S(2)}, u32[]{:S(2)}) %collective-permute-start.1) | collective-permute-done | bytes 65568 | tf_op jit(solution)/shard_map/ppermute | solution.py:289
  32.2 0.0 collective-permute-done.kv1_ref
  32.2 0.0 collective-permute-done.4.theirs_ref
  32.2 0.0 all-to-all-done.x_ref
  32.2 4.2 %attend.1 = (bf16[128,1280]{1,0:T(8,128)(2,1)S(1)}, bf16[128,1280]{1,0:T(8,128)(2,1)S(1)}, bf16[128,1280]{1,0:T(8,128)(2,1)S(1)}, bf16[128,1280]{1,0:T(8,128)(2,1)S(1)}, bf16[4,896,128]{2,1,0:T(8,128)(2,1)S(1)}) custom-call(s32[1]{0:T(128)} %bitcast.tgt_ref, s32[1]{0:T(128)} %bitcast.1.blk_ref, bf16[4,128,1280]{2,1,0:T(8,128)(2,1)S(1)} %all-to-all-done.x_ref, ...), custom_call_target="tpu_custom_call" | custom-call | flops 1811939328 | bytes 2621440 | tf_op jit(solution)/shard_map/attend/pallas_call | solution.py:180
  36.5 17.0 %all_to_all.15.four_ref = bf16[4,896,128]{2,1,0:T(8,128)(2,1)S(1)} all-to-all(bf16[4,896,128]{2,1,0:T(8,128)(2,1)S(1)} %get-tuple-element.26), channel_id=1, replica_groups={{0,1,8,9},{2,3,10,11},{4,5,12,13},{6,7,14,15},{16,17,24,25},{18,19,26,2..., dimensions={0} | all-to-all | bytes 1835008 | tf_op jit(solution)/shard_map/all_to_all | solution.py:314
  53.5 0.7 combine.1
  54.2 10.2 %all-to-all-start.2 = ((bf16[32,16,128]{2,1,0:T(8,128)(2,1)}), bf16[32,16,128]{2,1,0:T(8,128)(2,1)S(1)}, u32[]{:S(2)}, u32[]{:S(2)}) async-start(bf16[32,16,128]{2,1,0:T(8,128)(2,1)} %get-tuple-element.34), calls=%async_computation.2 | async-start | bytes 262144 | tf_op jit(solution)/shard_map/all_to_all | solution.py:318
  64.3 3.7 %collective-permute-start.5 = (bf16[128,1280]{1,0:T(8,128)(2,1)S(1)}, bf16[128,1280]{1,0:T(8,128)(2,1)S(1)}, u32[]{:S(2)}, u32[]{:S(2)}) collective-permute-start(bf16[128,1280]{1,0:T(8,128)(2,1)S(1)} %get-tuple-element.23), channel_id=1, source_target_pairs={{0,2},{1,3},{2,0},{3,1},{4,6},{5,7},{6,4},{7,5},{8,10},{9,11},{10,... | collective-permute-start | bytes 983048 | tf_op jit(solution)/shard_map/ppermute | solution.py:293
  68.0 4.3 %collective-permute-start.6 = (bf16[128,1280]{1,0:T(8,128)(2,1)S(1)}, bf16[128,1280]{1,0:T(8,128)(2,1)S(1)}, u32[]{:S(2)}, u32[]{:S(2)}) collective-permute-start(bf16[128,1280]{1,0:T(8,128)(2,1)S(1)} %get-tuple-element.24), channel_id=1, source_target_pairs={{0,4},{1,5},{2,6},{3,7},{4,0},{5,1},{6,2},{7,3},{8,12},{9,13},{10,... | collective-permute-start | bytes 983048 | tf_op jit(solution)/shard_map/ppermute | solution.py:293
  72.3 1.9 %collective-permute-start.7 = (bf16[128,1280]{1,0:T(8,128)(2,1)S(1)}, bf16[128,1280]{1,0:T(8,128)(2,1)S(1)}, u32[]{:S(2)}, u32[]{:S(2)}) collective-permute-start(bf16[128,1280]{1,0:T(8,128)(2,1)S(1)} %get-tuple-element.25), channel_id=1, source_target_pairs={{0,6},{1,7},{2,4},{3,5},{4,2},{5,3},{6,0},{7,1},{8,14},{9,15},{10,... | collective-permute-start | bytes 983048 | tf_op jit(solution)/shard_map/ppermute | solution.py:293
  74.2 6.8 %collective-permute-start.8 = (bf16[128,128]{1,0:T(8,128)(2,1)S(1)}, bf16[128,128]{1,0:T(8,128)(2,1)S(1)}, u32[]{:S(2)}, u32[]{:S(2)}) collective-permute-start(bf16[128,128]{1,0:T(8,128)(2,1)S(1)} %get-tuple-element.28), channel_id=1, source_target_pairs={{0,496},{8,504},{16,0},{24,8},{32,16},{40,24},{48,32},{56,40},{64,... | collective-permute-start | bytes 98312 | tf_op jit(solution)/shard_map/ppermute | solution.py:289
  81.1 4.0 %collective-permute-start.9 = (bf16[128,128]{1,0:T(8,128)(2,1)S(1)}, bf16[128,128]{1,0:T(8,128)(2,1)S(1)}, u32[]{:S(2)}, u32[]{:S(2)}) collective-permute-start(bf16[128,128]{1,0:T(8,128)(2,1)S(1)} %get-tuple-element.29), channel_id=1, source_target_pairs={{0,480},{8,488},{16,496},{24,504},{32,0},{40,8},{48,16},{56,24},{6... | collective-permute-start | bytes 98312 | tf_op jit(solution)/shard_map/ppermute | solution.py:289
  85.1 0.0 collective-permute-done.5.back1
  85.1 0.0 collective-permute-done.6.back2
  85.1 5.2 %collective-permute-done.7.back3 = bf16[128,1280]{1,0:T(8,128)(2,1)S(1)} collective-permute-done((bf16[128,1280]{1,0:T(8,128)(2,1)S(1)}, bf16[128,1280]{1,0:T(8,128)(2,1)S(1)}, u32[]{:S(2)}, u32[]{:S(2)}) %collective-permute-start.7) | collective-permute-done | bytes 327712 | tf_op jit(solution)/shard_map/ppermute | solution.py:293
  90.4 0.0 collective-permute-done.8.near_ref
  90.4 0.0 collective-permute-done.9.far_ref
  90.4 0.9 finish.1
  91.2 0.0 all-to-all-done.2.part_ref
  91.2 0.6 total.1
Async XLA Ops:
  2.8 5.2 %copy-start = (bf16[128,1024]{1,0:T(8,128)(2,1)S(1)}, bf16[128,1024]{1,0:T(8,128)(2,1)}, u32[]{:S(2)}) copy-start(bf16[128,1024]{1,0:T(8,128)(2,1)} %mine_ref.1) | copy-start | bytes 786436
  2.9 8.3 %copy-start.1 = (bf16[64,512]{1,0:T(8,128)(2,1)S(1)}, bf16[64,512]{1,0:T(8,128)(2,1)}, u32[]{:S(2)}) copy-start(bf16[64,512]{1,0:T(8,128)(2,1)} %get-tuple-element.21.own_ref) | copy-start | bytes 196612
  2.9 29.3 %all-to-all-start = ((bf16[4,128,1280]{2,1,0:T(8,128)(2,1)}), bf16[4,128,1280]{2,1,0:T(8,128)(2,1)S(1)}, u32[]{:S(2)}, u32[]{:S(2)}) async-start(bf16[4,128,1280]{2,1,0:T(8,128)(2,1)} %get-tuple-element.20), calls=%async_computation | async-start | bytes 2621440 | tf_op jit(solution)/shard_map/all_to_all | solution.py:303
  8.0 24.2 %collective-permute-start.4 = (bf16[128,1024]{1,0:T(8,128)(2,1)S(1)}, bf16[128,1024]{1,0:T(8,128)(2,1)S(1)}, u32[]{:S(2)}, u32[]{:S(2)}) collective-permute-start(bf16[128,1024]{1,0:T(8,128)(2,1)S(1)} %copy-done), channel_id=1, source_target_pairs={{0,1},{1,0},{2,3},{3,2},{4,5},{5,4},{6,7},{7,6},{8,9},{9,8},{10,11... | collective-permute-start | bytes 786440 | tf_op jit(solution)/shard_map/ppermute | solution.py:293
  11.1 17.9 %collective-permute-start.3 = (bf16[64,512]{1,0:T(8,128)(2,1)S(1)}, bf16[64,512]{1,0:T(8,128)(2,1)S(1)}, u32[]{:S(2)}, u32[]{:S(2)}) collective-permute-start(bf16[64,512]{1,0:T(8,128)(2,1)S(1)} %copy-done.1), channel_id=1, source_target_pairs={{0,32},{8,40},{16,48},{24,56},{32,64},{40,72},{48,80},{56,88},{64,... | collective-permute-start | bytes 196616 | tf_op jit(solution)/shard_map/ppermute | solution.py:289
  16.0 14.5 %collective-permute-start.2 = (bf16[64,512]{1,0:T(8,128)(2,1)S(1)}, bf16[64,512]{1,0:T(8,128)(2,1)S(1)}, u32[]{:S(2)}, u32[]{:S(2)}) collective-permute-start(bf16[64,512]{1,0:T(8,128)(2,1)S(1)} %copy-done.1), channel_id=1, source_target_pairs={{0,24},{8,32},{16,40},{24,48},{32,56},{40,64},{48,72},{56,80},{64,... | collective-permute-start | bytes 196616 | tf_op jit(solution)/shard_map/ppermute | solution.py:289
  23.6 8.6 %collective-permute-start.1 = (bf16[64,512]{1,0:T(8,128)(2,1)S(1)}, bf16[64,512]{1,0:T(8,128)(2,1)S(1)}, u32[]{:S(2)}, u32[]{:S(2)}) collective-permute-start(bf16[64,512]{1,0:T(8,128)(2,1)S(1)} %copy-done.1), channel_id=1, source_target_pairs={{0,16},{8,24},{16,32},{24,40},{32,48},{40,56},{48,64},{56,72},{64,... | collective-permute-start | bytes 196616 | tf_op jit(solution)/shard_map/ppermute | solution.py:289
  27.1 5.1 %collective-permute-start = (bf16[64,512]{1,0:T(8,128)(2,1)S(1)}, bf16[64,512]{1,0:T(8,128)(2,1)S(1)}, u32[]{:S(2)}, u32[]{:S(2)}) collective-permute-start(bf16[64,512]{1,0:T(8,128)(2,1)S(1)} %copy-done.1), channel_id=1, source_target_pairs={{0,8},{8,16},{16,24},{24,32},{32,40},{40,48},{48,56},{56,64},{64,7... | collective-permute-start | bytes 196616 | tf_op jit(solution)/shard_map/ppermute | solution.py:289
  54.2 37.1 %all-to-all-start.2 = ((bf16[32,16,128]{2,1,0:T(8,128)(2,1)}), bf16[32,16,128]{2,1,0:T(8,128)(2,1)S(1)}, u32[]{:S(2)}, u32[]{:S(2)}) async-start(bf16[32,16,128]{2,1,0:T(8,128)(2,1)} %get-tuple-element.34), calls=%async_computation.2 | async-start | bytes 262144 | tf_op jit(solution)/shard_map/all_to_all | solution.py:318
  64.3 20.7 %collective-permute-start.5 = (bf16[128,1280]{1,0:T(8,128)(2,1)S(1)}, bf16[128,1280]{1,0:T(8,128)(2,1)S(1)}, u32[]{:S(2)}, u32[]{:S(2)}) collective-permute-start(bf16[128,1280]{1,0:T(8,128)(2,1)S(1)} %get-tuple-element.23), channel_id=1, source_target_pairs={{0,2},{1,3},{2,0},{3,1},{4,6},{5,7},{6,4},{7,5},{8,10},{9,11},{10,... | collective-permute-start | bytes 983048 | tf_op jit(solution)/shard_map/ppermute | solution.py:293
  68.0 17.1 %collective-permute-start.6 = (bf16[128,1280]{1,0:T(8,128)(2,1)S(1)}, bf16[128,1280]{1,0:T(8,128)(2,1)S(1)}, u32[]{:S(2)}, u32[]{:S(2)}) collective-permute-start(bf16[128,1280]{1,0:T(8,128)(2,1)S(1)} %get-tuple-element.24), channel_id=1, source_target_pairs={{0,4},{1,5},{2,6},{3,7},{4,0},{5,1},{6,2},{7,3},{8,12},{9,13},{10,... | collective-permute-start | bytes 983048 | tf_op jit(solution)/shard_map/ppermute | solution.py:293
  72.3 18.0 %collective-permute-start.7 = (bf16[128,1280]{1,0:T(8,128)(2,1)S(1)}, bf16[128,1280]{1,0:T(8,128)(2,1)S(1)}, u32[]{:S(2)}, u32[]{:S(2)}) collective-permute-start(bf16[128,1280]{1,0:T(8,128)(2,1)S(1)} %get-tuple-element.25), channel_id=1, source_target_pairs={{0,6},{1,7},{2,4},{3,5},{4,2},{5,3},{6,0},{7,1},{8,14},{9,15},{10,... | collective-permute-start | bytes 983048 | tf_op jit(solution)/shard_map/ppermute | solution.py:293
  74.2 16.1 %collective-permute-start.8 = (bf16[128,128]{1,0:T(8,128)(2,1)S(1)}, bf16[128,128]{1,0:T(8,128)(2,1)S(1)}, u32[]{:S(2)}, u32[]{:S(2)}) collective-permute-start(bf16[128,128]{1,0:T(8,128)(2,1)S(1)} %get-tuple-element.28), channel_id=1, source_target_pairs={{0,496},{8,504},{16,0},{24,8},{32,16},{40,24},{48,32},{56,40},{64,... | collective-permute-start | bytes 98312 | tf_op jit(solution)/shard_map/ppermute | solution.py:289
  81.1 9.3 %collective-permute-start.9 = (bf16[128,128]{1,0:T(8,128)(2,1)S(1)}, bf16[128,128]{1,0:T(8,128)(2,1)S(1)}, u32[]{:S(2)}, u32[]{:S(2)}) collective-permute-start(bf16[128,128]{1,0:T(8,128)(2,1)S(1)} %get-tuple-element.29), channel_id=1, source_target_pairs={{0,480},{8,488},{16,496},{24,504},{32,0},{40,8},{48,16},{56,24},{6... | collective-permute-start | bytes 98312 | tf_op jit(solution)/shard_map/ppermute | solution.py:289

commit v6 on v5

--- a/solution.py
+++ b/solution.py
@@ -85,7 +85,7 @@
 
 
 def attend_kernel(
-    chunk, tgt_ref, blk_ref, x_ref, own_ref, kv1_ref, kv2_ref, kv3_ref, kv4_ref, mine_ref, theirs_ref,
+    chunk, tgt_ref, blk_ref, x_ref, own_ref, near_ref, far_ref, mate_own_ref, mate_near_ref, mate_far_ref, mine_ref, theirs_ref,
     back0, back1, back2, back3, four_ref,
     key_ref, value_ref, key_t_ref, value_t_ref, weight_ref, key_acc, value_acc, tile_acc,
 ):
@@ -96,10 +96,19 @@
     zero = jnp.zeros((SRC_DEV, PAIR), BF16)
     weight_ref[pl.ds(pl.multiple_of(low * PAIR, PAIR), PAIR), :] = mine_ref[...]
     weight_ref[pl.ds(pl.multiple_of((1 - low) * PAIR, PAIR), PAIR), :] = theirs_ref[...]
+    first = (blk_ref[0] & 1) == 0
+    mate_near = mate_near_ref[...]
+    blocks = (
+        own_ref[...],
+        jnp.where(first, mate_near, mate_own_ref[...]),
+        near_ref[...],
+        jnp.where(first, mate_far_ref[...], mate_near),
+        far_ref[...],
+    )
     for pair in range(2):
-        for w, ref in enumerate((own_ref, kv1_ref, kv2_ref, kv3_ref, kv4_ref)):
-            block_key = ref[:, pair * PAIR : (pair + 1) * PAIR]
-            block_value = ref[:, QUAD + pair * PAIR : QUAD + (pair + 1) * PAIR]
+        for w, block in enumerate(blocks):
+            block_key = block[:, pair * PAIR : (pair + 1) * PAIR]
+            block_value = block[:, QUAD + pair * PAIR : QUAD + (pair + 1) * PAIR]
             for head in range(2):
                 own_lanes = (lane < HD) if head == 0 else (lane >= HD)
                 at = pl.ds(head * WIDTH + w * SRC_DEV, SRC_DEV)
@@ -181,7 +190,7 @@
         functools.partial(attend_kernel, depth // n_blk),
         out_shape=(struct((rows, wide)),) * N_Y
         + (struct((4, depth // 2 + 2 * (WIN // 2 + 1) * SRC_DEV, PAIR)),),
-        in_specs=[SMEM] * 2 + [VMEM] * 8,
+        in_specs=[SMEM] * 2 + [VMEM] * 9,
         out_specs=(VMEM,) * (N_Y + 1),
         scratch_shapes=[
             pltpu.VMEM((2, 2 * WIDTH, PAIR), BF16),
@@ -289,6 +298,10 @@
     return lax.ppermute(value, axis, [(i, (i + steps) % count) for i in range(count)])
 
 
+def mate(value):
+    return lax.ppermute(value, "blk", [(i, i ^ 1) for i in range(lax.axis_size("blk"))])
+
+
 def flip(value, bits):
     return lax.ppermute(value, "tgt", [(i, i ^ bits) for i in range(lax.axis_size("tgt"))])
 
@@ -304,7 +317,10 @@
         send, "tgt", split_axis=0, concat_axis=0, tiled=True, axis_index_groups=groups
     )
     theirs = flip(out_weight, 1)
-    kvs = [own] + [shift(own, "blk", w) for w in range(1, WIN)]
+    near = shift(own, "blk", 2)
+    far = shift(own, "blk", 4)
+    mate_own = mate(own)
+    kvs = [own, near, far, mate_own, mate(near), mate(far)]
     *backs, four = attend(tgt, blk, n_blk, x, kvs, out_weight, theirs)
     fours = [
         [(2 * chip + core) * n_tgt + 2 * y + low for core in range(2) for low in range(2)]

time: 92.5 us -> 91.2 us (0.986)
  blocking collectives: 17 us -> 14.6 us
    ppermute x0 -> x3, starting transfers between devices: none -> 10.1 us  [mate(): lax.ppermute(value, 'blk', [(i, i ^ 1) for i in range(lax.axis_size('blk'...]
    ppermute x6 -> x4, starting transfers between devices: 28.7 us -> 19.3 us  [shift(): lax.ppermute(value, axis, [(i, (i + steps) % count) for i in range(count)])]
    all_to_all x1, blocking collectives: 17 us -> 14.6 us  [local(): lax.all_to_all(four, ('blk', 'tgt'), split_axis=0, concat_axis=0, tiled=T...]
    ppermute x0 -> x3, waiting for transfers between devices: none -> 1.2 us  [mate(): lax.ppermute(value, 'blk', [(i, i ^ 1) for i in range(lax.axis_size('blk'...]
    ppermute x6 -> x4, waiting for transfers between devices: 3.14 us -> 3.32 us  [shift(): lax.ppermute(value, axis, [(i, (i + steps) % count) for i in range(count)])]
  transfers between devices with their start and end apart: 12 -> 13, of which waited for: 3 -> 3; matrix products, arithmetic and copies ran while one was open for 0% -> 0% of each run, Pallas kernels for 1% -> 1%
where the time goes in v6:
time: 91.2 us; the launch traced here: 90.6 us
  starting transfers between devices  57.3 us (63%)
  blocking collectives  14.6 us (16%)
  waiting for transfers between devices  9.3 us (10%)
  Pallas kernels  8.64 us (9%)
    ppermute x4, starting transfers between devices, shift(): lax.ppermute(value, axis, [(i, (i + steps) % count) for i in range(count)])  19.3 us
    all_to_all x1, blocking collectives, local(): lax.all_to_all(four, ('blk', 'tgt'), split_axis=0, concat_axis=0, tiled=T...  14.6 us
    ppermute x4, starting transfers between devices, flip(): lax.ppermute(value, 'tgt', [(i, i ^ bits) for i in range(lax.axis_size('t...  12.7 us
    all_to_all x1, starting transfers between devices, local(): lax.all_to_all(tile, 'blk', split_axis=0, concat_axis=0, tiled=True, axis...  10.1 us
    ppermute x3, starting transfers between devices, mate(): lax.ppermute(value, 'blk', [(i, i ^ 1) for i in range(lax.axis_size('blk'...  10.1 us
    all_to_all x1, starting transfers between devices, local(): lax.all_to_all(send, 'tgt', split_axis=0, concat_axis=0, tiled=True, axis...  5.14 us
    ppermute x4, waiting for transfers between devices, flip(): lax.ppermute(value, 'tgt', [(i, i ^ bits) for i in range(lax.axis_size('t...  4.78 us
    pallas_call x1, Pallas kernels, attend(): pl.pallas_call(functools.partial(attend_kernel, depth // n_blk), out_shap...  4.26 us
  transfers between devices with their start and end apart: 13, of which 3 were waited for; matrix products, arithmetic and copies ran while one was open for 0% of the time, Pallas kernels for 1%

profile of v6, /device:TPU:1, one launch (start us, length us, event | category | flops | bytes accessed | tf_op | source)
XLA Modules:
  0.0 90.6 jit_solution(12768439342897947185)
XLA Ops:
  0.6 2.1 %pack.1 = (bf16[64,512]{1,0:T(8,128)(2,1)}, bf16[4,128,1280]{2,1,0:T(8,128)(2,1)}) custom-call(s32[1]{0:T(128)} %bitcast.tgt_ref, bf16[128,1024]{1,0:T(8,128)(2,1)} %query_ref.1, bf16[64,1024]{1,0:T(8,128)(2,1)} %key_ref.1, bf16[64,1024]{1,0:T(8,128)(2,1)} %value_ref.1, bf16[128,1024]{1,0:T(8,128)(2,1)} %out_grad_ref.1), custom_call_target="tpu_custom_call" | custom-call | tf_op jit(solution)/shard_map/pack/pallas_call | solution.py:71
  2.8 0.0 copy-start
  2.8 0.0 copy-start.1
  2.8 5.1 %all-to-all-start = ((bf16[4,128,1280]{2,1,0:T(8,128)(2,1)}), bf16[4,128,1280]{2,1,0:T(8,128)(2,1)S(1)}, u32[]{:S(2)}, u32[]{:S(2)}) async-start(bf16[4,128,1280]{2,1,0:T(8,128)(2,1)} %get-tuple-element.20), calls=%async_computation | async-start | bytes 2621440 | tf_op jit(solution)/shard_map/all_to_all | solution.py:316
  8.0 0.0 copy-done
  8.0 3.1 %collective-permute-start.5 = (bf16[128,1024]{1,0:T(8,128)(2,1)S(1)}, bf16[128,1024]{1,0:T(8,128)(2,1)S(1)}, u32[]{:S(2)}, u32[]{:S(2)}) collective-permute-start(bf16[128,1024]{1,0:T(8,128)(2,1)S(1)} %copy-done), channel_id=1, source_target_pairs={{0,1},{1,0},{2,3},{3,2},{4,5},{5,4},{6,7},{7,6},{8,9},{9,8},{10,11... | collective-permute-start | bytes 786440 | tf_op jit(solution)/shard_map/ppermute | solution.py:306
  11.1 0.0 copy-done.1
  11.1 4.9 %collective-permute-start.1 = (bf16[64,512]{1,0:T(8,128)(2,1)S(1)}, bf16[64,512]{1,0:T(8,128)(2,1)S(1)}, u32[]{:S(2)}, u32[]{:S(2)}) collective-permute-start(bf16[64,512]{1,0:T(8,128)(2,1)S(1)} %copy-done.1), channel_id=1, source_target_pairs={{0,32},{8,40},{16,48},{24,56},{32,64},{40,72},{48,80},{56,88},{64,... | collective-permute-start | bytes 196616 | tf_op jit(solution)/shard_map/ppermute | solution.py:298
  16.0 3.5 %collective-permute-start = (bf16[64,512]{1,0:T(8,128)(2,1)S(1)}, bf16[64,512]{1,0:T(8,128)(2,1)S(1)}, u32[]{:S(2)}, u32[]{:S(2)}) collective-permute-start(bf16[64,512]{1,0:T(8,128)(2,1)S(1)} %copy-done.1), channel_id=1, source_target_pairs={{0,16},{8,24},{16,32},{24,40},{32,48},{40,56},{48,64},{56,72},{64,... | collective-permute-start | bytes 196616 | tf_op jit(solution)/shard_map/ppermute | solution.py:298
  19.5 3.7 %collective-permute-start.2 = (bf16[64,512]{1,0:T(8,128)(2,1)S(1)}, bf16[64,512]{1,0:T(8,128)(2,1)S(1)}, u32[]{:S(2)}, u32[]{:S(2)}) collective-permute-start(bf16[64,512]{1,0:T(8,128)(2,1)S(1)} %copy-done.1), channel_id=1, source_target_pairs={{0,8},{8,0},{16,24},{24,16},{32,40},{40,32},{48,56},{56,48},{64,72... | collective-permute-start | bytes 196616 | tf_op jit(solution)/shard_map/ppermute | solution.py:302
  23.3 3.3 %collective-permute-done.1.far_ref = bf16[64,512]{1,0:T(8,128)(2,1)S(1)} collective-permute-done((bf16[64,512]{1,0:T(8,128)(2,1)S(1)}, bf16[64,512]{1,0:T(8,128)(2,1)S(1)}, u32[]{:S(2)}, u32[]{:S(2)}) %collective-permute-start.1) | collective-permute-done | bytes 65568 | tf_op jit(solution)/shard_map/ppermute | solution.py:298
  26.6 4.5 %collective-permute-start.4 = (bf16[64,512]{1,0:T(8,128)(2,1)S(1)}, bf16[64,512]{1,0:T(8,128)(2,1)S(1)}, u32[]{:S(2)}, u32[]{:S(2)}) collective-permute-start(bf16[64,512]{1,0:T(8,128)(2,1)S(1)} %collective-permute-done.1.far_ref), channel_id=1, source_target_pairs={{0,8},{8,0},{16,24},{24,16},{32,40},{40,32},{48,56},{56,48},{64,72... | collective-permute-start | bytes 196616 | tf_op jit(solution)/shard_map/ppermute | solution.py:302
  31.0 0.0 collective-permute-done.near_ref
  31.0 1.9 %collective-permute-start.3 = (bf16[64,512]{1,0:T(8,128)(2,1)S(1)}, bf16[64,512]{1,0:T(8,128)(2,1)S(1)}, u32[]{:S(2)}, u32[]{:S(2)}) collective-permute-start(bf16[64,512]{1,0:T(8,128)(2,1)S(1)} %collective-permute-done.near_ref), channel_id=1, source_target_pairs={{0,8},{8,0},{16,24},{24,16},{32,40},{40,32},{48,56},{56,48},{64,72... | collective-permute-start | bytes 196616 | tf_op jit(solution)/shard_map/ppermute | solution.py:302
  33.0 0.0 collective-permute-done.2.mate_own_ref
  33.0 0.0 collective-permute-done.4.mate_far_ref
  33.0 1.2 %collective-permute-done.3.mate_near_ref = bf16[64,512]{1,0:T(8,128)(2,1)S(1)} collective-permute-done((bf16[64,512]{1,0:T(8,128)(2,1)S(1)}, bf16[64,512]{1,0:T(8,128)(2,1)S(1)}, u32[]{:S(2)}, u32[]{:S(2)}) %collective-permute-start.3) | collective-permute-done | bytes 65568 | tf_op jit(solution)/shard_map/ppermute | solution.py:302
  34.2 0.0 collective-permute-done.5.theirs_ref
  34.2 0.0 all-to-all-done.x_ref
  34.2 4.3 %attend.1 = (bf16[128,1280]{1,0:T(8,128)(2,1)S(1)}, bf16[128,1280]{1,0:T(8,128)(2,1)S(1)}, bf16[128,1280]{1,0:T(8,128)(2,1)S(1)}, bf16[128,1280]{1,0:T(8,128)(2,1)S(1)}, bf16[4,896,128]{2,1,0:T(8,128)(2,1)S(1)}) custom-call(s32[1]{0:T(128)} %bitcast.tgt_ref, s32[1]{0:T(128)} %bitcast.1.blk_ref, bf16[4,128,1280]{2,1,0:T(8,128)(2,1)S(1)} %all-to-all-done.x_ref, ...), custom_call_target="tpu_custom_call" | custom-call | flops 1811939328 | bytes 2621440 | tf_op jit(solution)/shard_map/attend/pallas_call | solution.py:189
  38.5 14.6 %all_to_all.15.four_ref = bf16[4,896,128]{2,1,0:T(8,128)(2,1)S(1)} all-to-all(bf16[4,896,128]{2,1,0:T(8,128)(2,1)S(1)} %get-tuple-element.26), channel_id=1, replica_groups={{0,1,8,9},{2,3,10,11},{4,5,12,13},{6,7,14,15},{16,17,24,25},{18,19,26,2..., dimensions={0} | all-to-all | bytes 1835008 | tf_op jit(solution)/shard_map/all_to_all | solution.py:330
  53.0 0.7 combine.1
  53.7 10.1 %all-to-all-start.2 = ((bf16[32,16,128]{2,1,0:T(8,128)(2,1)}), bf16[32,16,128]{2,1,0:T(8,128)(2,1)S(1)}, u32[]{:S(2)}, u32[]{:S(2)}) async-start(bf16[32,16,128]{2,1,0:T(8,128)(2,1)} %get-tuple-element.34), calls=%async_computation.2 | async-start | bytes 262144 | tf_op jit(solution)/shard_map/all_to_all | solution.py:334
  63.9 2.9 %collective-permute-start.6 = (bf16[128,1280]{1,0:T(8,128)(2,1)S(1)}, bf16[128,1280]{1,0:T(8,128)(2,1)S(1)}, u32[]{:S(2)}, u32[]{:S(2)}) collective-permute-start(bf16[128,1280]{1,0:T(8,128)(2,1)S(1)} %get-tuple-element.23), channel_id=1, source_target_pairs={{0,2},{1,3},{2,0},{3,1},{4,6},{5,7},{6,4},{7,5},{8,10},{9,11},{10,... | collective-permute-start | bytes 983048 | tf_op jit(solution)/shard_map/ppermute | solution.py:306
  66.8 4.3 %collective-permute-start.7 = (bf16[128,1280]{1,0:T(8,128)(2,1)S(1)}, bf16[128,1280]{1,0:T(8,128)(2,1)S(1)}, u32[]{:S(2)}, u32[]{:S(2)}) collective-permute-start(bf16[128,1280]{1,0:T(8,128)(2,1)S(1)} %get-tuple-element.24), channel_id=1, source_target_pairs={{0,4},{1,5},{2,6},{3,7},{4,0},{5,1},{6,2},{7,3},{8,12},{9,13},{10,... | collective-permute-start | bytes 983048 | tf_op jit(solution)/shard_map/ppermute | solution.py:306
  71.1 2.4 %collective-permute-start.8 = (bf16[128,1280]{1,0:T(8,128)(2,1)S(1)}, bf16[128,1280]{1,0:T(8,128)(2,1)S(1)}, u32[]{:S(2)}, u32[]{:S(2)}) collective-permute-start(bf16[128,1280]{1,0:T(8,128)(2,1)S(1)} %get-tuple-element.25), channel_id=1, source_target_pairs={{0,6},{1,7},{2,4},{3,5},{4,2},{5,3},{6,0},{7,1},{8,14},{9,15},{10,... | collective-permute-start | bytes 983048 | tf_op jit(solution)/shard_map/ppermute | solution.py:306
  73.5 6.8 %collective-permute-start.9 = (bf16[128,128]{1,0:T(8,128)(2,1)S(1)}, bf16[128,128]{1,0:T(8,128)(2,1)S(1)}, u32[]{:S(2)}, u32[]{:S(2)}) collective-permute-start(bf16[128,128]{1,0:T(8,128)(2,1)S(1)} %get-tuple-element.28), channel_id=1, source_target_pairs={{0,496},{8,504},{16,0},{24,8},{32,16},{40,24},{48,32},{56,40},{64,... | collective-permute-start | bytes 98312 | tf_op jit(solution)/shard_map/ppermute | solution.py:298
  80.3 4.0 %collective-permute-start.10 = (bf16[128,128]{1,0:T(8,128)(2,1)S(1)}, bf16[128,128]{1,0:T(8,128)(2,1)S(1)}, u32[]{:S(2)}, u32[]{:S(2)}) collective-permute-start(bf16[128,128]{1,0:T(8,128)(2,1)S(1)} %get-tuple-element.29), channel_id=1, source_target_pairs={{0,480},{8,488},{16,496},{24,504},{32,0},{40,8},{48,16},{56,24},{6... | collective-permute-start | bytes 98312 | tf_op jit(solution)/shard_map/ppermute | solution.py:298
  84.3 0.0 collective-permute-done.6.back1
  84.3 0.0 collective-permute-done.7.back2
  84.3 4.8 %collective-permute-done.8.back3 = bf16[128,1280]{1,0:T(8,128)(2,1)S(1)} collective-permute-done((bf16[128,1280]{1,0:T(8,128)(2,1)S(1)}, bf16[128,1280]{1,0:T(8,128)(2,1)S(1)}, u32[]{:S(2)}, u32[]{:S(2)}) %collective-permute-start.8) | collective-permute-done | bytes 327712 | tf_op jit(solution)/shard_map/ppermute | solution.py:306
  89.1 0.0 collective-permute-done.9.near_ref
  89.1 0.0 collective-permute-done.10.far_ref
  89.1 0.9 finish.1
  90.0 0.0 all-to-all-done.2.part_ref
  90.0 0.6 total.1
Async XLA Ops:
  2.8 5.2 %copy-start = (bf16[128,1024]{1,0:T(8,128)(2,1)S(1)}, bf16[128,1024]{1,0:T(8,128)(2,1)}, u32[]{:S(2)}) copy-start(bf16[128,1024]{1,0:T(8,128)(2,1)} %mine_ref.1) | copy-start | bytes 786436
  2.8 8.3 %copy-start.1 = (bf16[64,512]{1,0:T(8,128)(2,1)S(1)}, bf16[64,512]{1,0:T(8,128)(2,1)}, u32[]{:S(2)}) copy-start(bf16[64,512]{1,0:T(8,128)(2,1)} %get-tuple-element.21.own_ref) | copy-start | bytes 196612
  2.8 31.4 %all-to-all-start = ((bf16[4,128,1280]{2,1,0:T(8,128)(2,1)}), bf16[4,128,1280]{2,1,0:T(8,128)(2,1)S(1)}, u32[]{:S(2)}, u32[]{:S(2)}) async-start(bf16[4,128,1280]{2,1,0:T(8,128)(2,1)} %get-tuple-element.20), calls=%async_computation | async-start | bytes 2621440 | tf_op jit(solution)/shard_map/all_to_all | solution.py:316
  8.0 26.2 %collective-permute-start.5 = (bf16[128,1024]{1,0:T(8,128)(2,1)S(1)}, bf16[128,1024]{1,0:T(8,128)(2,1)S(1)}, u32[]{:S(2)}, u32[]{:S(2)}) collective-permute-start(bf16[128,1024]{1,0:T(8,128)(2,1)S(1)} %copy-done), channel_id=1, source_target_pairs={{0,1},{1,0},{2,3},{3,2},{4,5},{5,4},{6,7},{7,6},{8,9},{9,8},{10,11... | collective-permute-start | bytes 786440 | tf_op jit(solution)/shard_map/ppermute | solution.py:306
  11.1 15.5 %collective-permute-start.1 = (bf16[64,512]{1,0:T(8,128)(2,1)S(1)}, bf16[64,512]{1,0:T(8,128)(2,1)S(1)}, u32[]{:S(2)}, u32[]{:S(2)}) collective-permute-start(bf16[64,512]{1,0:T(8,128)(2,1)S(1)} %copy-done.1), channel_id=1, source_target_pairs={{0,32},{8,40},{16,48},{24,56},{32,64},{40,72},{48,80},{56,88},{64,... | collective-permute-start | bytes 196616 | tf_op jit(solution)/shard_map/ppermute | solution.py:298
  16.0 15.0 %collective-permute-start = (bf16[64,512]{1,0:T(8,128)(2,1)S(1)}, bf16[64,512]{1,0:T(8,128)(2,1)S(1)}, u32[]{:S(2)}, u32[]{:S(2)}) collective-permute-start(bf16[64,512]{1,0:T(8,128)(2,1)S(1)} %copy-done.1), channel_id=1, source_target_pairs={{0,16},{8,24},{16,32},{24,40},{32,48},{40,56},{48,64},{56,72},{64,... | collective-permute-start | bytes 196616 | tf_op jit(solution)/shard_map/ppermute | solution.py:298
  19.5 13.4 %collective-permute-start.2 = (bf16[64,512]{1,0:T(8,128)(2,1)S(1)}, bf16[64,512]{1,0:T(8,128)(2,1)S(1)}, u32[]{:S(2)}, u32[]{:S(2)}) collective-permute-start(bf16[64,512]{1,0:T(8,128)(2,1)S(1)} %copy-done.1), channel_id=1, source_target_pairs={{0,8},{8,0},{16,24},{24,16},{32,40},{40,32},{48,56},{56,48},{64,72... | collective-permute-start | bytes 196616 | tf_op jit(solution)/shard_map/ppermute | solution.py:302
  26.6 6.4 %collective-permute-start.4 = (bf16[64,512]{1,0:T(8,128)(2,1)S(1)}, bf16[64,512]{1,0:T(8,128)(2,1)S(1)}, u32[]{:S(2)}, u32[]{:S(2)}) collective-permute-start(bf16[64,512]{1,0:T(8,128)(2,1)S(1)} %collective-permute-done.1.far_ref), channel_id=1, source_target_pairs={{0,8},{8,0},{16,24},{24,16},{32,40},{40,32},{48,56},{56,48},{64,72... | collective-permute-start | bytes 196616 | tf_op jit(solution)/shard_map/ppermute | solution.py:302
  31.0 3.1 %collective-permute-start.3 = (bf16[64,512]{1,0:T(8,128)(2,1)S(1)}, bf16[64,512]{1,0:T(8,128)(2,1)S(1)}, u32[]{:S(2)}, u32[]{:S(2)}) collective-permute-start(bf16[64,512]{1,0:T(8,128)(2,1)S(1)} %collective-permute-done.near_ref), channel_id=1, source_target_pairs={{0,8},{8,0},{16,24},{24,16},{32,40},{40,32},{48,56},{56,48},{64,72... | collective-permute-start | bytes 196616 | tf_op jit(solution)/shard_map/ppermute | solution.py:302
  53.7 36.3 %all-to-all-start.2 = ((bf16[32,16,128]{2,1,0:T(8,128)(2,1)}), bf16[32,16,128]{2,1,0:T(8,128)(2,1)S(1)}, u32[]{:S(2)}, u32[]{:S(2)}) async-start(bf16[32,16,128]{2,1,0:T(8,128)(2,1)} %get-tuple-element.34), calls=%async_computation.2 | async-start | bytes 262144 | tf_op jit(solution)/shard_map/all_to_all | solution.py:334
  63.9 20.4 %collective-permute-start.6 = (bf16[128,1280]{1,0:T(8,128)(2,1)S(1)}, bf16[128,1280]{1,0:T(8,128)(2,1)S(1)}, u32[]{:S(2)}, u32[]{:S(2)}) collective-permute-start(bf16[128,1280]{1,0:T(8,128)(2,1)S(1)} %get-tuple-element.23), channel_id=1, source_target_pairs={{0,2},{1,3},{2,0},{3,1},{4,6},{5,7},{6,4},{7,5},{8,10},{9,11},{10,... | collective-permute-start | bytes 983048 | tf_op jit(solution)/shard_map/ppermute | solution.py:306
  66.8 17.6 %collective-permute-start.7 = (bf16[128,1280]{1,0:T(8,128)(2,1)S(1)}, bf16[128,1280]{1,0:T(8,128)(2,1)S(1)}, u32[]{:S(2)}, u32[]{:S(2)}) collective-permute-start(bf16[128,1280]{1,0:T(8,128)(2,1)S(1)} %get-tuple-element.24), channel_id=1, source_target_pairs={{0,4},{1,5},{2,6},{3,7},{4,0},{5,1},{6,2},{7,3},{8,12},{9,13},{10,... | collective-permute-start | bytes 983048 | tf_op jit(solution)/shard_map/ppermute | solution.py:306
  71.1 18.0 %collective-permute-start.8 = (bf16[128,1280]{1,0:T(8,128)(2,1)S(1)}, bf16[128,1280]{1,0:T(8,128)(2,1)S(1)}, u32[]{:S(2)}, u32[]{:S(2)}) collective-permute-start(bf16[128,1280]{1,0:T(8,128)(2,1)S(1)} %get-tuple-element.25), channel_id=1, source_target_pairs={{0,6},{1,7},{2,4},{3,5},{4,2},{5,3},{6,0},{7,1},{8,14},{9,15},{10,... | collective-permute-start | bytes 983048 | tf_op jit(solution)/shard_map/ppermute | solution.py:306
  73.5 15.6 %collective-permute-start.9 = (bf16[128,128]{1,0:T(8,128)(2,1)S(1)}, bf16[128,128]{1,0:T(8,128)(2,1)S(1)}, u32[]{:S(2)}, u32[]{:S(2)}) collective-permute-start(bf16[128,128]{1,0:T(8,128)(2,1)S(1)} %get-tuple-element.28), channel_id=1, source_target_pairs={{0,496},{8,504},{16,0},{24,8},{32,16},{40,24},{48,32},{56,40},{64,... | collective-permute-start | bytes 98312 | tf_op jit(solution)/shard_map/ppermute | solution.py:298
  80.3 8.8 %collective-permute-start.10 = (bf16[128,128]{1,0:T(8,128)(2,1)S(1)}, bf16[128,128]{1,0:T(8,128)(2,1)S(1)}, u32[]{:S(2)}, u32[]{:S(2)}) collective-permute-start(bf16[128,128]{1,0:T(8,128)(2,1)S(1)} %get-tuple-element.29), channel_id=1, source_target_pairs={{0,480},{8,488},{16,496},{24,504},{32,0},{40,8},{48,16},{56,24},{6... | collective-permute-start | bytes 98312 | tf_op jit(solution)/shard_map/ppermute | solution.py:298

commit v7 on v5

--- a/solution.py
+++ b/solution.py
@@ -86,7 +86,7 @@
 
 def attend_kernel(
     chunk, tgt_ref, blk_ref, x_ref, own_ref, kv1_ref, kv2_ref, kv3_ref, kv4_ref, mine_ref, theirs_ref,
-    back0, back1, back2, back3, four_ref,
+    back0, back1, back2, back3, four_ref, own_keep_ref, own_send_ref,
     key_ref, value_ref, key_t_ref, value_t_ref, weight_ref, key_acc, value_acc, tile_acc,
 ):
     depth = mine_ref.shape[1]
@@ -161,16 +161,19 @@
             four_ref[2 * to + half, :rows_tile, :] = turned[:, to].reshape(rows_tile, PAIR).astype(BF16)
         for other in range(2):
             to = 2 * (core ^ other) + half
-            for slot in range(WIN // 2 + 1):
-                w = 2 * slot + other
+            for slot in range(WIN // 2):
+                w = 2 * slot + 2 - other
                 for part, acc in enumerate((key_acc, value_acc)):
                     at = pl.ds(rows_tile + (2 * slot + part) * SRC_DEV, SRC_DEV)
-                    if w >= WIN:
-                        four_ref[to, at, :] = zero
-                        continue
-                    first = acc[half, w * SRC_DEV : (w + 1) * SRC_DEV, :]
-                    second = acc[half, WIDTH + w * SRC_DEV : WIDTH + (w + 1) * SRC_DEV, :]
-                    four_ref[to, at, :] = jnp.where(lane < HD, first, second).astype(BF16)
+                    first_head = acc[half, w * SRC_DEV : (w + 1) * SRC_DEV, :]
+                    second_head = acc[half, WIDTH + w * SRC_DEV : WIDTH + (w + 1) * SRC_DEV, :]
+                    four_ref[to, at, :] = jnp.where(lane < HD, first_head, second_head).astype(BF16)
+    for pair, ref in ((low, own_keep_ref), (1 - low, own_send_ref)):
+        for part, acc in enumerate((key_acc, value_acc)):
+            first_head = acc[pair, :SRC_DEV, :]
+            second_head = acc[pair, WIDTH : WIDTH + SRC_DEV, :]
+            at = slice(part * SRC_DEV, (part + 1) * SRC_DEV)
+            ref[at, :] = jnp.where(lane < HD, first_head, second_head).astype(ref.dtype)
 
 
 def attend(tgt, blk, n_blk, x, kvs, mine, theirs):
@@ -180,9 +183,13 @@
     return pl.pallas_call(
         functools.partial(attend_kernel, depth // n_blk),
         out_shape=(struct((rows, wide)),) * N_Y
-        + (struct((4, depth // 2 + 2 * (WIN // 2 + 1) * SRC_DEV, PAIR)),),
+        + (
+            struct((4, depth // 2 + 2 * (WIN // 2) * SRC_DEV, PAIR)),
+            struct((2 * SRC_DEV, PAIR), F32),
+            struct((2 * SRC_DEV, PAIR)),
+        ),
         in_specs=[SMEM] * 2 + [VMEM] * 8,
-        out_specs=(VMEM,) * (N_Y + 1),
+        out_specs=(VMEM,) * (N_Y + 3),
         scratch_shapes=[
             pltpu.VMEM((2, 2 * WIDTH, PAIR), BF16),
             pltpu.VMEM((2, 2 * WIDTH, PAIR), BF16),
@@ -218,13 +225,13 @@
     one, three = part(1 - core, 0), part(1 - core, 1)
     zero = jnp.zeros_like(one)
     first = core == 0
-    own_ref[...] = part(core, 0) + jnp.where(first, one, zero)
-    near_ref[...] = (part(core, 1) + jnp.where(first, three, one)).astype(BF16)
-    far_ref[...] = (part(core, 2) + jnp.where(first, zero, three)).astype(BF16)
+    own_ref[...] = jnp.where(first, one, zero)
+    near_ref[...] = (part(core, 0) + jnp.where(first, three, one)).astype(BF16)
+    far_ref[...] = (part(core, 1) + jnp.where(first, zero, three)).astype(BF16)
 
 
 def combine(blk, n_blk, four):
-    rows_tile = four.shape[1] - 2 * (WIN // 2 + 1) * SRC_DEV
+    rows_tile = four.shape[1] - 2 * (WIN // 2) * SRC_DEV
     chips = n_blk // 2
     block = (2 * SRC_DEV, PAIR)
     return pl.pallas_call(
@@ -237,7 +244,7 @@
     )(blk, four)
 
 
-def finish_kernel(tgt_ref, back0, back1, back2, back3, own_ref, near_ref, far_ref, out_ref, query_grad_ref, key_grad_ref, value_grad_ref):
+def finish_kernel(tgt_ref, back0, back1, back2, back3, own_ref, keep_ref, came_ref, near_ref, far_ref, out_ref, query_grad_ref, key_grad_ref, value_grad_ref):
     depth = out_ref.shape[1]
     total = None
     for s, ref in enumerate((back0, back1, back2, back3)):
@@ -245,25 +252,28 @@
         total = part if total is None else total + part
         query_grad_ref[:, pl.ds(pl.multiple_of(((tgt_ref[0] >> 1) ^ s) * QUAD, QUAD), QUAD)] = ref[:, depth:]
     out_ref[...] = total.astype(BF16)
-    grad = (own_ref[...] + near_ref[...].astype(F32) + far_ref[...].astype(F32)).astype(BF16)
+    grad = own_ref[...] + keep_ref[...]
+    for ref in (came_ref, near_ref, far_ref):
+        grad = grad + ref[...].astype(F32)
+    grad = grad.astype(BF16)
     key_grad_ref[...] = grad[:SRC_DEV]
     value_grad_ref[...] = grad[SRC_DEV:]
 
 
-def finish(tgt, backs, own, near, far):
+def finish(tgt, backs, *grads):
     rows, wide = backs[0].shape
     out, grad = struct((rows, wide - QUAD)), struct((SRC_DEV, PAIR))
     return pl.pallas_call(
         finish_kernel,
         out_shape=(out, out, grad, grad),
-        in_specs=[SMEM] + [VMEM] * (N_Y + 3),
+        in_specs=[SMEM] + [VMEM] * (N_Y + 5),
         out_specs=(VMEM,) * 4,
         cost_estimate=pl.CostEstimate(
             flops=N_Y * rows * wide, bytes_accessed=2 * N_Y * rows * wide, transcendentals=0
         ),
         compiler_params=pltpu.CompilerParams(vmem_limit_bytes=8 * 1024 * 1024),
         name="finish",
-    )(tgt, *backs, own, near, far)
+    )(tgt, *backs, *grads)
 
 
 def total_kernel(part_ref, total_ref):
@@ -305,7 +315,7 @@
     )
     theirs = flip(out_weight, 1)
     kvs = [own] + [shift(own, "blk", w) for w in range(1, WIN)]
-    *backs, four = attend(tgt, blk, n_blk, x, kvs, out_weight, theirs)
+    *backs, four, own_keep, own_send = attend(tgt, blk, n_blk, x, kvs, out_weight, theirs)
     fours = [
         [(2 * chip + core) * n_tgt + 2 * y + low for core in range(2) for low in range(2)]
         for chip in range(n_blk // 2)
@@ -319,7 +329,8 @@
         tile, "blk", split_axis=0, concat_axis=0, tiled=True, axis_index_groups=cores
     )
     near, far = shift(near, "blk", -2), shift(far, "blk", -4)
-    outputs, query_grad, key_grad, value_grad = finish(tgt, backs, own_grad, near, far)
+    came = flip(own_send, 1)
+    outputs, query_grad, key_grad, value_grad = finish(tgt, backs, own_grad, own_keep, came, near, far)
     weight_grad = total_of(tiles).T
     return outputs, query_grad, key_grad, value_grad, weight_grad
 

time: 92.5 us -> 91.8 us (level)
  the two profiles are of different devices: /device:TPU:1 before, /device:TPU:24 now
where the time goes in v7:
time: 91.8 us; the launch traced here: 91.2 us
  starting transfers between devices  60.5 us (66%)
  blocking collectives  14 us (15%)
  Pallas kernels  8.67 us (9%)
  waiting for transfers between devices  7.16 us (8%)
    ppermute x6, starting transfers between devices, shift(): lax.ppermute(value, axis, [(i, (i + steps) % count) for i in range(count)])  26.6 us
    ppermute x5, starting transfers between devices, flip(): lax.ppermute(value, 'tgt', [(i, i ^ bits) for i in range(lax.axis_size('t...  14.3 us
    all_to_all x1, blocking collectives, local(): lax.all_to_all(four, ('blk', 'tgt'), split_axis=0, concat_axis=0, tiled=T...  14 us
    all_to_all x1, starting transfers between devices, local(): lax.all_to_all(tile, 'blk', split_axis=0, concat_axis=0, tiled=True, axis...  10.5 us
    all_to_all x1, starting transfers between devices, local(): lax.all_to_all(send, 'tgt', split_axis=0, concat_axis=0, tiled=True, axis...  9.22 us
    ppermute x6, waiting for transfers between devices, shift(): lax.ppermute(value, axis, [(i, (i + steps) % count) for i in range(count)])  7.14 us
    pallas_call x1, Pallas kernels, attend(): pl.pallas_call(functools.partial(attend_kernel, depth // n_blk), out_shap...  4.29 us
    pallas_call x1, Pallas kernels, pack(): pl.pallas_call(pack_kernel, out_shape=(struct((SRC_DEV, 2 * QUAD)), struc...  2.14 us
  transfers between devices with their start and end apart: 13, of which 4 were waited for; matrix products, arithmetic and copies ran while one was open for 0% of the time, Pallas kernels for 1%

profile of v7, /device:TPU:24, one launch (start us, length us, event | category | flops | bytes accessed | tf_op | source)
XLA Modules:
  0.0 91.2 jit_solution(5922594024914523548)
XLA Ops:
  0.6 2.1 %pack.1 = (bf16[64,512]{1,0:T(8,128)(2,1)}, bf16[4,128,1280]{2,1,0:T(8,128)(2,1)}) custom-call(s32[1]{0:T(128)} %bitcast.tgt_ref, bf16[128,1024]{1,0:T(8,128)(2,1)} %query_ref.1, bf16[64,1024]{1,0:T(8,128)(2,1)} %key_ref.1, bf16[64,1024]{1,0:T(8,128)(2,1)} %value_ref.1, bf16[128,1024]{1,0:T(8,128)(2,1)} %out_grad_ref.1), custom_call_target="tpu_custom_call" | custom-call | tf_op jit(solution)/shard_map/pack/pallas_call | solution.py:71
  2.8 0.0 copy-start
  2.8 0.0 copy-start.1
  2.8 9.2 %all-to-all-start = ((bf16[4,128,1280]{2,1,0:T(8,128)(2,1)}), bf16[4,128,1280]{2,1,0:T(8,128)(2,1)S(1)}, u32[]{:S(2)}, u32[]{:S(2)}) async-start(bf16[4,128,1280]{2,1,0:T(8,128)(2,1)} %get-tuple-element.22), calls=%async_computation | async-start | bytes 2621440 | tf_op jit(solution)/shard_map/all_to_all | solution.py:313
  12.0 0.0 copy-done
  12.0 1.9 %collective-permute-start.4 = (bf16[128,1024]{1,0:T(8,128)(2,1)S(1)}, bf16[128,1024]{1,0:T(8,128)(2,1)S(1)}, u32[]{:S(2)}, u32[]{:S(2)}) collective-permute-start(bf16[128,1024]{1,0:T(8,128)(2,1)S(1)} %copy-done), channel_id=1, source_target_pairs={{0,1},{1,0},{2,3},{3,2},{4,5},{5,4},{6,7},{7,6},{8,9},{9,8},{10,11... | collective-permute-start | bytes 786440 | tf_op jit(solution)/shard_map/ppermute | solution.py:303
  13.9 0.0 copy-done.1
  14.0 2.3 %collective-permute-start.3 = (bf16[64,512]{1,0:T(8,128)(2,1)S(1)}, bf16[64,512]{1,0:T(8,128)(2,1)S(1)}, u32[]{:S(2)}, u32[]{:S(2)}) collective-permute-start(bf16[64,512]{1,0:T(8,128)(2,1)S(1)} %copy-done.1), channel_id=1, source_target_pairs={{0,32},{8,40},{16,48},{24,56},{32,64},{40,72},{48,80},{56,88},{64,... | collective-permute-start | bytes 196616 | tf_op jit(solution)/shard_map/ppermute | solution.py:299
  16.2 2.1 %collective-permute-start.2 = (bf16[64,512]{1,0:T(8,128)(2,1)S(1)}, bf16[64,512]{1,0:T(8,128)(2,1)S(1)}, u32[]{:S(2)}, u32[]{:S(2)}) collective-permute-start(bf16[64,512]{1,0:T(8,128)(2,1)S(1)} %copy-done.1), channel_id=1, source_target_pairs={{0,24},{8,32},{16,40},{24,48},{32,56},{40,64},{48,72},{56,80},{64,... | collective-permute-start | bytes 196616 | tf_op jit(solution)/shard_map/ppermute | solution.py:299
  18.4 5.0 %collective-permute-start.1 = (bf16[64,512]{1,0:T(8,128)(2,1)S(1)}, bf16[64,512]{1,0:T(8,128)(2,1)S(1)}, u32[]{:S(2)}, u32[]{:S(2)}) collective-permute-start(bf16[64,512]{1,0:T(8,128)(2,1)S(1)} %copy-done.1), channel_id=1, source_target_pairs={{0,16},{8,24},{16,32},{24,40},{32,48},{40,56},{48,64},{56,72},{64,... | collective-permute-start | bytes 196616 | tf_op jit(solution)/shard_map/ppermute | solution.py:299
  23.4 4.8 %collective-permute-start = (bf16[64,512]{1,0:T(8,128)(2,1)S(1)}, bf16[64,512]{1,0:T(8,128)(2,1)S(1)}, u32[]{:S(2)}, u32[]{:S(2)}) collective-permute-start(bf16[64,512]{1,0:T(8,128)(2,1)S(1)} %copy-done.1), channel_id=1, source_target_pairs={{0,8},{8,16},{16,24},{24,32},{32,40},{40,48},{48,56},{56,64},{64,7... | collective-permute-start | bytes 196616 | tf_op jit(solution)/shard_map/ppermute | solution.py:299
  28.2 1.1 %collective-permute-done.3.kv4_ref = bf16[64,512]{1,0:T(8,128)(2,1)S(1)} collective-permute-done((bf16[64,512]{1,0:T(8,128)(2,1)S(1)}, bf16[64,512]{1,0:T(8,128)(2,1)S(1)}, u32[]{:S(2)}, u32[]{:S(2)}) %collective-permute-start.3) | collective-permute-done | bytes 65568 | tf_op jit(solution)/shard_map/ppermute | solution.py:299
  29.3 0.0 collective-permute-done.2.kv3_ref
  29.4 1.4 %collective-permute-done.1.kv2_ref = bf16[64,512]{1,0:T(8,128)(2,1)S(1)} collective-permute-done((bf16[64,512]{1,0:T(8,128)(2,1)S(1)}, bf16[64,512]{1,0:T(8,128)(2,1)S(1)}, u32[]{:S(2)}, u32[]{:S(2)}) %collective-permute-start.1) | collective-permute-done | bytes 65568 | tf_op jit(solution)/shard_map/ppermute | solution.py:299
  30.7 2.8 %collective-permute-done.kv1_ref = bf16[64,512]{1,0:T(8,128)(2,1)S(1)} collective-permute-done((bf16[64,512]{1,0:T(8,128)(2,1)S(1)}, bf16[64,512]{1,0:T(8,128)(2,1)S(1)}, u32[]{:S(2)}, u32[]{:S(2)}) %collective-permute-start) | collective-permute-done | bytes 65568 | tf_op jit(solution)/shard_map/ppermute | solution.py:299
  33.5 0.0 collective-permute-done.4.theirs_ref
  33.5 0.0 all-to-all-done.x_ref
  33.5 4.3 %attend.1 = (bf16[128,1280]{1,0:T(8,128)(2,1)S(1)}, bf16[128,1280]{1,0:T(8,128)(2,1)S(1)}, bf16[128,1280]{1,0:T(8,128)(2,1)S(1)}, bf16[128,1280]{1,0:T(8,128)(2,...) custom-call(s32[1]{0:T(128)} %bitcast.tgt_ref, s32[1]{0:T(128)} %bitcast.1.blk_ref, ...), custom_call_target="tpu_custom_call" | custom-call | flops 1811939328 | bytes 2621440 | tf_op jit(solution)/shard_map/attend/pallas_call | solution.py:183
  37.8 0.0 copy-start.2
  37.8 14.0 %all_to_all.15.four_ref = bf16[4,768,128]{2,1,0:T(8,128)(2,1)S(1)} all-to-all(bf16[4,768,128]{2,1,0:T(8,128)(2,1)S(1)} %get-tuple-element.28), channel_id=1, replica_groups={{0,1,8,9},{2,3,10,11},{4,5,12,13},{6,7,14,15},{16,17,24,25},{18,19,26,2..., dimensions={0} | all-to-all | bytes 1572864 | tf_op jit(solution)/shard_map/all_to_all | solution.py:324
  51.8 0.7 combine.1
  52.5 0.0 copy-done.2
  52.5 10.5 %all-to-all-start.2 = ((bf16[32,16,128]{2,1,0:T(8,128)(2,1)}), bf16[32,16,128]{2,1,0:T(8,128)(2,1)S(1)}, u32[]{:S(2)}, u32[]{:S(2)}) async-start(bf16[32,16,128]{2,1,0:T(8,128)(2,1)} %get-tuple-element.38), calls=%async_computation.2 | async-start | bytes 262144 | tf_op jit(solution)/shard_map/all_to_all | solution.py:328
  63.0 2.8 %collective-permute-start.5 = (bf16[128,1280]{1,0:T(8,128)(2,1)S(1)}, bf16[128,1280]{1,0:T(8,128)(2,1)S(1)}, u32[]{:S(2)}, u32[]{:S(2)}) collective-permute-start(bf16[128,1280]{1,0:T(8,128)(2,1)S(1)} %get-tuple-element.25), channel_id=1, source_target_pairs={{0,2},{1,3},{2,0},{3,1},{4,6},{5,7},{6,4},{7,5},{8,10},{9,11},{10,... | collective-permute-start | bytes 983048 | tf_op jit(solution)/shard_map/ppermute | solution.py:303
  65.8 2.5 %collective-permute-start.6 = (bf16[128,1280]{1,0:T(8,128)(2,1)S(1)}, bf16[128,1280]{1,0:T(8,128)(2,1)S(1)}, u32[]{:S(2)}, u32[]{:S(2)}) collective-permute-start(bf16[128,1280]{1,0:T(8,128)(2,1)S(1)} %get-tuple-element.26), channel_id=1, source_target_pairs={{0,4},{1,5},{2,6},{3,7},{4,0},{5,1},{6,2},{7,3},{8,12},{9,13},{10,... | collective-permute-start | bytes 983048 | tf_op jit(solution)/shard_map/ppermute | solution.py:303
  68.3 5.1 %collective-permute-start.7 = (bf16[128,1280]{1,0:T(8,128)(2,1)S(1)}, bf16[128,1280]{1,0:T(8,128)(2,1)S(1)}, u32[]{:S(2)}, u32[]{:S(2)}) collective-permute-start(bf16[128,1280]{1,0:T(8,128)(2,1)S(1)} %get-tuple-element.27), channel_id=1, source_target_pairs={{0,6},{1,7},{2,4},{3,5},{4,2},{5,3},{6,0},{7,1},{8,14},{9,15},{10,... | collective-permute-start | bytes 983048 | tf_op jit(solution)/shard_map/ppermute | solution.py:303
  73.4 1.9 %collective-permute-start.8 = (bf16[128,128]{1,0:T(8,128)(2,1)}, bf16[128,128]{1,0:T(8,128)(2,1)S(1)}, u32[]{:S(2)}, u32[]{:S(2)}) collective-permute-start(bf16[128,128]{1,0:T(8,128)(2,1)} %copy-done.2), channel_id=1, source_target_pairs={{0,1},{1,0},{2,3},{3,2},{4,5},{5,4},{6,7},{7,6},{8,9},{9,8},{10,11... | collective-permute-start | bytes 98312 | tf_op jit(solution)/shard_map/ppermute | solution.py:303
  75.4 7.6 %collective-permute-start.9 = (bf16[128,128]{1,0:T(8,128)(2,1)S(1)}, bf16[128,128]{1,0:T(8,128)(2,1)S(1)}, u32[]{:S(2)}, u32[]{:S(2)}) collective-permute-start(bf16[128,128]{1,0:T(8,128)(2,1)S(1)} %get-tuple-element.32), channel_id=1, source_target_pairs={{0,496},{8,504},{16,0},{24,8},{32,16},{40,24},{48,32},{56,40},{64,... | collective-permute-start | bytes 98312 | tf_op jit(solution)/shard_map/ppermute | solution.py:299
  83.0 0.0 collective-permute-done.8.came_ref
  83.0 4.8 %collective-permute-start.10 = (bf16[128,128]{1,0:T(8,128)(2,1)S(1)}, bf16[128,128]{1,0:T(8,128)(2,1)S(1)}, u32[]{:S(2)}, u32[]{:S(2)}) collective-permute-start(bf16[128,128]{1,0:T(8,128)(2,1)S(1)} %get-tuple-element.33), channel_id=1, source_target_pairs={{0,480},{8,488},{16,496},{24,504},{32,0},{40,8},{48,16},{56,24},{6... | collective-permute-start | bytes 98312 | tf_op jit(solution)/shard_map/ppermute | solution.py:299
  87.8 0.0 collective-permute-done.5.back1
  87.8 0.0 collective-permute-done.6.back2
  87.8 0.0 collective-permute-done.7.back3
  87.8 0.0 collective-permute-done.9.near_ref
  87.8 1.9 %collective-permute-done.10.far_ref = bf16[128,128]{1,0:T(8,128)(2,1)S(1)} collective-permute-done((bf16[128,128]{1,0:T(8,128)(2,1)S(1)}, bf16[128,128]{1,0:T(8,128)(2,1)S(1)}, u32[]{:S(2)}, u32[]{:S(2)}) %collective-permute-start.10) | collective-permute-done | bytes 32800 | tf_op jit(solution)/shard_map/ppermute | solution.py:299
  89.7 0.9 finish.1
  90.6 0.0 all-to-all-done.2.part_ref
  90.6 0.6 total.1
Async XLA Ops:
  2.8 9.2 %copy-start = (bf16[128,1024]{1,0:T(8,128)(2,1)S(1)}, bf16[128,1024]{1,0:T(8,128)(2,1)}, u32[]{:S(2)}) copy-start(bf16[128,1024]{1,0:T(8,128)(2,1)} %mine_ref.1) | copy-start | bytes 786436
  2.8 11.2 %copy-start.1 = (bf16[64,512]{1,0:T(8,128)(2,1)S(1)}, bf16[64,512]{1,0:T(8,128)(2,1)}, u32[]{:S(2)}) copy-start(bf16[64,512]{1,0:T(8,128)(2,1)} %get-tuple-element.23.own_ref) | copy-start | bytes 196612
  2.8 30.7 %all-to-all-start = ((bf16[4,128,1280]{2,1,0:T(8,128)(2,1)}), bf16[4,128,1280]{2,1,0:T(8,128)(2,1)S(1)}, u32[]{:S(2)}, u32[]{:S(2)}) async-start(bf16[4,128,1280]{2,1,0:T(8,128)(2,1)} %get-tuple-element.22), calls=%async_computation | async-start | bytes 2621440 | tf_op jit(solution)/shard_map/all_to_all | solution.py:313
  12.0 21.4 %collective-permute-start.4 = (bf16[128,1024]{1,0:T(8,128)(2,1)S(1)}, bf16[128,1024]{1,0:T(8,128)(2,1)S(1)}, u32[]{:S(2)}, u32[]{:S(2)}) collective-permute-start(bf16[128,1024]{1,0:T(8,128)(2,1)S(1)} %copy-done), channel_id=1, source_target_pairs={{0,1},{1,0},{2,3},{3,2},{4,5},{5,4},{6,7},{7,6},{8,9},{9,8},{10,11... | collective-permute-start | bytes 786440 | tf_op jit(solution)/shard_map/ppermute | solution.py:303
  14.0 15.4 %collective-permute-start.3 = (bf16[64,512]{1,0:T(8,128)(2,1)S(1)}, bf16[64,512]{1,0:T(8,128)(2,1)S(1)}, u32[]{:S(2)}, u32[]{:S(2)}) collective-permute-start(bf16[64,512]{1,0:T(8,128)(2,1)S(1)} %copy-done.1), channel_id=1, source_target_pairs={{0,32},{8,40},{16,48},{24,56},{32,64},{40,72},{48,80},{56,88},{64,... | collective-permute-start | bytes 196616 | tf_op jit(solution)/shard_map/ppermute | solution.py:299
  16.2 13.1 %collective-permute-start.2 = (bf16[64,512]{1,0:T(8,128)(2,1)S(1)}, bf16[64,512]{1,0:T(8,128)(2,1)S(1)}, u32[]{:S(2)}, u32[]{:S(2)}) collective-permute-start(bf16[64,512]{1,0:T(8,128)(2,1)S(1)} %copy-done.1), channel_id=1, source_target_pairs={{0,24},{8,32},{16,40},{24,48},{32,56},{40,64},{48,72},{56,80},{64,... | collective-permute-start | bytes 196616 | tf_op jit(solution)/shard_map/ppermute | solution.py:299
  18.4 12.3 %collective-permute-start.1 = (bf16[64,512]{1,0:T(8,128)(2,1)S(1)}, bf16[64,512]{1,0:T(8,128)(2,1)S(1)}, u32[]{:S(2)}, u32[]{:S(2)}) collective-permute-start(bf16[64,512]{1,0:T(8,128)(2,1)S(1)} %copy-done.1), channel_id=1, source_target_pairs={{0,16},{8,24},{16,32},{24,40},{32,48},{40,56},{48,64},{56,72},{64,... | collective-permute-start | bytes 196616 | tf_op jit(solution)/shard_map/ppermute | solution.py:299
  23.4 10.0 %collective-permute-start = (bf16[64,512]{1,0:T(8,128)(2,1)S(1)}, bf16[64,512]{1,0:T(8,128)(2,1)S(1)}, u32[]{:S(2)}, u32[]{:S(2)}) collective-permute-start(bf16[64,512]{1,0:T(8,128)(2,1)S(1)} %copy-done.1), channel_id=1, source_target_pairs={{0,8},{8,16},{16,24},{24,32},{32,40},{40,48},{48,56},{56,64},{64,7... | collective-permute-start | bytes 196616 | tf_op jit(solution)/shard_map/ppermute | solution.py:299
  37.8 14.8 %copy-start.2 = (bf16[128,128]{1,0:T(8,128)(2,1)}, bf16[128,128]{1,0:T(8,128)(2,1)S(1)}, u32[]{:S(2)}) copy-start(bf16[128,128]{1,0:T(8,128)(2,1)S(1)} %get-tuple-element.31) | copy-start | bytes 98308
  52.5 38.0 %all-to-all-start.2 = ((bf16[32,16,128]{2,1,0:T(8,128)(2,1)}), bf16[32,16,128]{2,1,0:T(8,128)(2,1)S(1)}, u32[]{:S(2)}, u32[]{:S(2)}) async-start(bf16[32,16,128]{2,1,0:T(8,128)(2,1)} %get-tuple-element.38), calls=%async_computation.2 | async-start | bytes 262144 | tf_op jit(solution)/shard_map/all_to_all | solution.py:328
  63.0 24.8 %collective-permute-start.5 = (bf16[128,1280]{1,0:T(8,128)(2,1)S(1)}, bf16[128,1280]{1,0:T(8,128)(2,1)S(1)}, u32[]{:S(2)}, u32[]{:S(2)}) collective-permute-start(bf16[128,1280]{1,0:T(8,128)(2,1)S(1)} %get-tuple-element.25), channel_id=1, source_target_pairs={{0,2},{1,3},{2,0},{3,1},{4,6},{5,7},{6,4},{7,5},{8,10},{9,11},{10,... | collective-permute-start | bytes 983048 | tf_op jit(solution)/shard_map/ppermute | solution.py:303
  65.8 22.0 %collective-permute-start.6 = (bf16[128,1280]{1,0:T(8,128)(2,1)S(1)}, bf16[128,1280]{1,0:T(8,128)(2,1)S(1)}, u32[]{:S(2)}, u32[]{:S(2)}) collective-permute-start(bf16[128,1280]{1,0:T(8,128)(2,1)S(1)} %get-tuple-element.26), channel_id=1, source_target_pairs={{0,4},{1,5},{2,6},{3,7},{4,0},{5,1},{6,2},{7,3},{8,12},{9,13},{10,... | collective-permute-start | bytes 983048 | tf_op jit(solution)/shard_map/ppermute | solution.py:303
  68.3 19.5 %collective-permute-start.7 = (bf16[128,1280]{1,0:T(8,128)(2,1)S(1)}, bf16[128,1280]{1,0:T(8,128)(2,1)S(1)}, u32[]{:S(2)}, u32[]{:S(2)}) collective-permute-start(bf16[128,1280]{1,0:T(8,128)(2,1)S(1)} %get-tuple-element.27), channel_id=1, source_target_pairs={{0,6},{1,7},{2,4},{3,5},{4,2},{5,3},{6,0},{7,1},{8,14},{9,15},{10,... | collective-permute-start | bytes 983048 | tf_op jit(solution)/shard_map/ppermute | solution.py:303
  73.4 9.5 %collective-permute-start.8 = (bf16[128,128]{1,0:T(8,128)(2,1)}, bf16[128,128]{1,0:T(8,128)(2,1)S(1)}, u32[]{:S(2)}, u32[]{:S(2)}) collective-permute-start(bf16[128,128]{1,0:T(8,128)(2,1)} %copy-done.2), channel_id=1, source_target_pairs={{0,1},{1,0},{2,3},{3,2},{4,5},{5,4},{6,7},{7,6},{8,9},{9,8},{10,11... | collective-permute-start | bytes 98312 | tf_op jit(solution)/shard_map/ppermute | solution.py:303
  75.4 12.4 %collective-permute-start.9 = (bf16[128,128]{1,0:T(8,128)(2,1)S(1)}, bf16[128,128]{1,0:T(8,128)(2,1)S(1)}, u32[]{:S(2)}, u32[]{:S(2)}) collective-permute-start(bf16[128,128]{1,0:T(8,128)(2,1)S(1)} %get-tuple-element.32), channel_id=1, source_target_pairs={{0,496},{8,504},{16,0},{24,8},{32,16},{40,24},{48,32},{56,40},{64,... | collective-permute-start | bytes 98312 | tf_op jit(solution)/shard_map/ppermute | solution.py:299
  83.0 6.7 %collective-permute-start.10 = (bf16[128,128]{1,0:T(8,128)(2,1)S(1)}, bf16[128,128]{1,0:T(8,128)(2,1)S(1)}, u32[]{:S(2)}, u32[]{:S(2)}) collective-permute-start(bf16[128,128]{1,0:T(8,128)(2,1)S(1)} %get-tuple-element.33), channel_id=1, source_target_pairs={{0,480},{8,488},{16,496},{24,504},{32,0},{40,8},{48,16},{56,24},{6... | collective-permute-start | bytes 98312 | tf_op jit(solution)/shard_map/ppermute | solution.py:299
